TPU v7x, 256 devices: a whole 4x4x8 slice. The times are simulated.
256 devices in a mesh: patch: 128 (over y, z, x), vec: 2 (over core).
Axes of the slice: x: 4, y: 4, z: 8, core: 2. Of those that a mesh axis runs over, the one named last changes fastest.
Arguments:
- vectors: float32 [65536, 512], P('patch', 'vec'), may hold values from -6 to 6
- blocks: bfloat16 [8192, 256, 256], P('patch'), may hold values from -0.075 to 0.075, as said below
- block_row: int32 [8192], P('patch'), may hold values from 0 to 255, as said below
- block_col: int32 [8192], P('patch'), may hold values from 0 to 255, as said below
- block_count: int32 [128], P('patch'), may hold values from 0 to 58, as said below
Outputs:
- subspace: float32 [65536, 512], P('patch', 'vec')
- residual: float32 [65536, 512], P('patch', 'vec')
Inputs may be any that keep to these rules, and one draw needn't show every extreme that they name: `block_row`: device p owns entries p * 64 to (p + 1) * 64 - 1. Its used slots come first and hold tiles of block rows 4 * (p // 2) to 4 * (p // 2) + 3 whose block column is at most the row and at least 4 * (p // 2) - 12; both devices of a pair p // 2 share these rows, tiles grouped by 4 x 4 patches each on one device. Every lower tile of the pattern stands in exactly one used slot, every diagonal tile is present, and unused slots name block row and column 4 * (p // 2). `block_col`: the block column of the tile in the same slot, as described for block_row. `block_count`: at most 58 used slots on a device, reached by some device in every draw; the loads are uneven. `blocks`: entries of unused slots are never read.
All inputs are finite; a program needn't handle non-finite values.
Results may differ from a plain program's by a relative error of at most 0.0038.
Values may be sent and summed in bfloat16 or wider, within the bound.
A program may use at most 128 MiB of HBM per device.

v0:
```python
import jax
import jax.numpy as jnp
from jax import lax
from jax.sharding import PartitionSpec as P

STEPS = 2


step_rate = 0.25
exact_mode = lax.Precision.HIGHEST


def shifted(block, axis, distance):
    devices = range(lax.axis_size(axis))
    route = [(i - distance, i) for i in devices if i - distance in devices]
    return lax.ppermute(block, axis, route)


def accumulate(window_x, totals, block_tiles, row_ids, col_ids, used_slots, window_start):
    group_total = (used_slots + 7) // 8

    def one_turn(group_index, partial_value):
        first_slot = group_index * 8
        chosen = lax.dynamic_slice_in_dim(block_tiles, first_slot, 8, 0)
        rows_here = lax.dynamic_slice_in_dim(row_ids, first_slot, 8, 0) - window_start
        cols_here = lax.dynamic_slice_in_dim(col_ids, first_slot, 8, 0) - window_start
        alive_mask = (first_slot + jnp.arange(8, dtype=jnp.int32) < used_slots).astype(jnp.float32)
        weight = (jnp.where(rows_here == cols_here, 0.5, 1.0).astype(jnp.float32) * alive_mask)[
            :, None, None
        ]
        direct = (
            jnp.einsum(
                "sab,sbk->sak", chosen, window_x[cols_here], preferred_element_type=jnp.float32
            )
            * weight
        )
        mirror = (
            jnp.einsum(
                "sba,sbk->sak", chosen, window_x[rows_here], preferred_element_type=jnp.float32
            )
            * weight
        )
        return partial_value.at[rows_here].add(direct).at[cols_here].add(mirror)

    return lax.fori_loop(0, group_total, one_turn, totals)


def shards(vectors, blocks, block_row, block_col, block_count):
    dev_rows, col_width = vectors.shape
    tile_size = blocks.shape[1]
    total_rows = dev_rows * lax.axis_size("patch")
    position = lax.axis_index("patch")
    parity = position % 2
    window_start = 2 * (position - 6 - parity)
    column_start = lax.axis_index("vec") * col_width
    used_slots = block_count[0]
    current = vectors
    residual = vectors
    for iteration in range(STEPS):
        rounded = current.astype(jnp.bfloat16)
        pieces = {0: rounded}
        for offset in (7, 6, 5, 4, 3, 2, 1, -1):
            pieces[offset] = shifted(rounded, "patch", offset)
        lower_side = jnp.concatenate([pieces[6 - segment] for segment in range(8)], axis=0)
        upper_side = jnp.concatenate([pieces[7 - segment] for segment in range(8)], axis=0)
        window_x = jnp.where(parity == 0, lower_side, upper_side).reshape(16, tile_size, col_width)
        totals = jnp.zeros((16, tile_size, col_width), jnp.float32)
        totals = accumulate(
            window_x, totals, blocks, block_row, block_col, used_slots, window_start
        )
        segments = totals.reshape(8, dev_rows, col_width)
        zero_rows = jnp.zeros((dev_rows, col_width), jnp.float32)
        applied = jnp.where(parity == 0, segments[6], segments[7])
        for offset in (1, -1, -2, -3, -4, -5, -6, -7):
            lower_seg = segments[offset + 6] if 0 <= offset + 6 <= 7 else zero_rows
            upper_seg = segments[offset + 7] if 0 <= offset + 7 <= 7 else zero_rows
            outgoing = jnp.where(parity == 0, lower_seg, upper_seg)
            applied = applied + shifted(outgoing, "patch", offset)
        current_all = lax.all_gather(current, "vec", axis=1, tiled=True)
        rayleigh = lax.psum(
            jnp.dot(
                current_all.T, applied, precision=exact_mode, preferred_element_type=jnp.float32
            )
            / total_rows,
            "patch",
        )
        residual = applied - jnp.dot(
            current_all, rayleigh, precision=exact_mode, preferred_element_type=jnp.float32
        )
        update = current - step_rate * residual
        update_all = lax.all_gather(update, "vec", axis=1, tiled=True)
        gram_matrix = lax.psum(
            jnp.dot(
                update_all.T, update_all, precision=exact_mode, preferred_element_type=jnp.float32
            )
            / total_rows,
            "patch",
        )
        factor = jnp.linalg.cholesky(gram_matrix)
        solved = lax.linalg.triangular_solve(
            factor, update_all, left_side=False, lower=True, transpose_a=True
        )
        current = lax.dynamic_slice_in_dim(solved, column_start, col_width, 1)
    return (current, residual)


def solution(mesh):
    in_specs = (P("patch", "vec"), P("patch", None, None), P("patch"), P("patch"), P("patch"))
    out_specs = (P("patch", "vec"), P("patch", "vec"))
    return jax.shard_map(shards, mesh=mesh, in_specs=in_specs, out_specs=out_specs, check_vma=False)
```

profile of v0, /device:TPU:4, one launch (start us, length us, event | category | flops | bytes accessed | tf_op | source)
XLA Modules:
  0.0 1878.6 jit_solution(11894211632453353742)
XLA Ops:
  69.6 30.9 %collective-permute-start.10 = (f32[512,256]{0,1:T(8,128)}, f32[512,256]{0,1:T(8,128)}, u32[]{:S(2)}, u32[]{:S(2)}) collective-permute-start(f32[512,256]{0,1:T(8,128)} %copy.47), channel_id=1, source_target_pairs={{4,0},{6,2},{8,4},{10,6},{12,8},{14,10},{16,12},{18,14},{20,16},{2... | collective-permute-start | bytes 1572872 | tf_op jit(solution)/shard_map/ppermute | solution.py:16
  114.8 19.8 %collective-permute-done.10 = f32[512,256]{0,1:T(8,128)} collective-permute-done((f32[512,256]{0,1:T(8,128)}, f32[512,256]{0,1:T(8,128)}, u32[]{:S(2)}, u32[]{:S(2)}) %collective-permute-start.10) | collective-permute-done | bytes 524320 | tf_op jit(solution)/shard_map/ppermute | solution.py:16
  135.9 25.8 %collective-permute-done.11 = f32[512,256]{0,1:T(8,128)} collective-permute-done((f32[512,256]{0,1:T(8,128)}, f32[512,256]{0,1:T(8,128)}, u32[]{:S(2)}, u32[]{:S(2)}) %collective-permute-start.11) | collective-permute-done | bytes 524320 | tf_op jit(solution)/shard_map/ppermute | solution.py:16
  164.7 10.6 collective-permute-start.9
  175.6 26.3 %collective-permute-done.13 = f32[512,256]{0,1:T(8,128)S(1)} collective-permute-done((f32[512,256]{0,1:T(8,128)}, f32[512,256]{0,1:T(8,128)S(1)}, u32[]{:S(2)}, u32[]{:S(2)}) %collective-permute-start.13) | collective-permute-done | bytes 524320 | tf_op jit(solution)/shard_map/ppermute | solution.py:16
  201.9 60.9 %collective-permute-done.15 = f32[512,256]{0,1:T(8,128)S(1)} collective-permute-done((f32[512,256]{0,1:T(8,128)}, f32[512,256]{0,1:T(8,128)S(1)}, u32[]{:S(2)}, u32[]{:S(2)}) %collective-permute-start.15) | collective-permute-done | bytes 524320 | tf_op jit(solution)/shard_map/ppermute | solution.py:16
  269.1 283.2 %all-reduce.6.cloned.1.call-done = f32[512,256]{0,1:T(8,128)} async-done(((f32[512,256]{0,1:T(8,128)}), f32[512,256]{0,1:T(8,128)}) %all-reduce.6.cloned.1.call-update) | async-done | bytes 524304 | tf_op jit(solution)/shard_map/psum | solution.py:80
  555.3 11.9 all-gather.7.cloned.1.call-done
  572.1 223.4 %all-reduce.8.cloned.1.call-done = f32[512,512]{0,1:T(8,128)} async-done(((f32[512,512]{0,1:T(8,128)}), f32[512,512]{0,1:T(8,128)}) %all-reduce.8.cloned.1.call-update) | async-done | bytes 1048592 | tf_op jit(solution)/shard_map/psum | solution.py:92
  797.4 11.7 cholesky.286
  809.3 9.8 custom-call.27
  819.8 11.7 cholesky.305
  831.5 9.9 custom-call.28
  842.2 11.7 cholesky.326
  854.6 9.8 custom-call.29
  865.0 11.7 cholesky.343
  889.2 39.3 %custom-call.30 = f32[4,128,128]{1,2,0:T(8,128)S(1)} custom-call(f32[4,128,128]{2,1,0:T(8,128)S(1)} %get-tuple-element.116), custom_call_target="InvertDiagBlocksLowerTriangular" | custom-call | tf_op jit(solution)/shard_map/triangular_solve/custom-call.3 | solution.py:100
  996.5 56.7 %collective-permute-start.24 = (f32[512,256]{0,1:T(8,128)}, f32[512,256]{0,1:T(8,128)}, u32[]{:S(2)}, u32[]{:S(2)}) collective-permute-start(f32[512,256]{0,1:T(8,128)} %copy.55), channel_id=1, source_target_pairs={{0,2},{2,4},{4,6},{6,8},{8,10},{10,12},{12,14},{14,16},{16,18},{18... | collective-permute-start | bytes 1572872 | tf_op jit(solution)/shard_map/ppermute | solution.py:16
  1073.6 12.8 collective-permute-done.26
  1095.0 28.4 %collective-permute-done.28 = f32[512,256]{0,1:T(8,128)S(1)} collective-permute-done((f32[512,256]{0,1:T(8,128)}, f32[512,256]{0,1:T(8,128)S(1)}, u32[]{:S(2)}, u32[]{:S(2)}) %collective-permute-start.28) | collective-permute-done | bytes 524320 | tf_op jit(solution)/shard_map/ppermute | solution.py:16
  1127.8 80.4 %collective-permute-done.30 = f32[512,256]{0,1:T(8,128)S(1)} collective-permute-done((f32[512,256]{0,1:T(8,128)}, f32[512,256]{0,1:T(8,128)S(1)}, u32[]{:S(2)}, u32[]{:S(2)}) %collective-permute-start.30) | collective-permute-done | bytes 524320 | tf_op jit(solution)/shard_map/ppermute | solution.py:16
  1213.5 277.4 %all-reduce.10.cloned.1.call-done = f32[512,256]{1,0:T(8,128)} async-done(((f32[512,256]{1,0:T(8,128)}), f32[512,256]{1,0:T(8,128)}) %all-reduce.10.cloned.1.call-update) | async-done | bytes 524304 | tf_op jit(solution)/shard_map/psum | solution.py:80
  1494.1 11.7 all-gather.11.cloned.1.call-done
  1511.3 222.1 %all-reduce.12.cloned.1.call-done = f32[512,512]{0,1:T(8,128)} async-done(((f32[512,512]{0,1:T(8,128)}), f32[512,512]{0,1:T(8,128)}) %all-reduce.12.cloned.1.call-update) | async-done | bytes 1048592 | tf_op jit(solution)/shard_map/psum | solution.py:92
  1735.3 11.7 cholesky.358
  1747.1 9.8 custom-call.31
  1757.6 11.9 cholesky.377
  1770.9 9.8 custom-call.32
  1781.4 11.7 cholesky.398
  1793.8 9.8 custom-call.33
  1804.2 11.9 cholesky.415
  1827.5 39.3 %custom-call.34 = f32[4,128,128]{1,2,0:T(8,128)S(1)} custom-call(f32[4,128,128]{2,1,0:T(8,128)S(1)} %get-tuple-element.117), custom_call_target="InvertDiagBlocksLowerTriangular" | custom-call | tf_op jit(solution)/shard_map/triangular_solve/custom-call.3 | solution.py:100
  (241 shorter events, 259.2 us)
Async XLA Ops:
  7.2 258.6 %all-gather.5.cloned.1.call-start = ((), (), s32[]{:S(2)}) async-start(), calls=%async_computation | async-start | bytes 1572864 | tf_op jit(solution)/shard_map/all_gather | solution.py:79
  8.5 23.7 %collective-permute-start.7 = (bf16[512,256]{0,1:T(8,128)(2,1)S(1)}, bf16[512,256]{0,1:T(8,128)(2,1)S(1)}, u32[]{:S(2)}, u32[]{:S(2)}) collective-permute-start(bf16[512,256]{0,1:T(8,128)(2,1)S(1)} %convert_element_type.8), channel_id=1, source_target_pairs={{0,14},{2,16},{4,18},{6,20},{8,22},{10,24},{12,26},{14,28},{16,30}... | collective-permute-start | bytes 786440 | tf_op jit(solution)/shard_map/ppermute | solution.py:16
  19.7 23.0 %collective-permute-start.1 = (bf16[512,256]{0,1:T(8,128)(2,1)S(1)}, bf16[512,256]{0,1:T(8,128)(2,1)S(1)}, u32[]{:S(2)}, u32[]{:S(2)}) collective-permute-start(bf16[512,256]{0,1:T(8,128)(2,1)S(1)} %convert_element_type.8), channel_id=1, source_target_pairs={{0,10},{2,12},{4,14},{6,16},{8,18},{10,20},{12,22},{14,24},{16,26}... | collective-permute-start | bytes 786440 | tf_op jit(solution)/shard_map/ppermute | solution.py:16
  24.5 23.8 %collective-permute-start.2 = (bf16[512,256]{0,1:T(8,128)(2,1)S(1)}, bf16[512,256]{0,1:T(8,128)(2,1)S(1)}, u32[]{:S(2)}, u32[]{:S(2)}) collective-permute-start(bf16[512,256]{0,1:T(8,128)(2,1)S(1)} %convert_element_type.8), channel_id=1, source_target_pairs={{0,8},{2,10},{4,12},{6,14},{8,16},{10,18},{12,20},{14,22},{16,24},... | collective-permute-start | bytes 786440 | tf_op jit(solution)/shard_map/ppermute | solution.py:16
  27.4 26.6 %collective-permute-start.3 = (bf16[512,256]{0,1:T(8,128)(2,1)S(1)}, bf16[512,256]{0,1:T(8,128)(2,1)S(1)}, u32[]{:S(2)}, u32[]{:S(2)}) collective-permute-start(bf16[512,256]{0,1:T(8,128)(2,1)S(1)} %convert_element_type.8), channel_id=1, source_target_pairs={{0,6},{2,8},{4,10},{6,12},{8,14},{10,16},{12,18},{14,20},{16,22},{... | collective-permute-start | bytes 786440 | tf_op jit(solution)/shard_map/ppermute | solution.py:16
  32.2 26.5 %collective-permute-start.4 = (bf16[512,256]{0,1:T(8,128)(2,1)S(1)}, bf16[512,256]{0,1:T(8,128)(2,1)S(1)}, u32[]{:S(2)}, u32[]{:S(2)}) collective-permute-start(bf16[512,256]{0,1:T(8,128)(2,1)S(1)} %convert_element_type.8), channel_id=1, source_target_pairs={{0,4},{2,6},{4,8},{6,10},{8,12},{10,14},{12,16},{14,18},{16,20},{1... | collective-permute-start | bytes 786440 | tf_op jit(solution)/shard_map/ppermute | solution.py:16
  69.6 65.0 %collective-permute-start.10 = (f32[512,256]{0,1:T(8,128)}, f32[512,256]{0,1:T(8,128)}, u32[]{:S(2)}, u32[]{:S(2)}) collective-permute-start(f32[512,256]{0,1:T(8,128)} %copy.47), channel_id=1, source_target_pairs={{4,0},{6,2},{8,4},{10,6},{12,8},{14,10},{16,12},{18,14},{20,16},{2... | collective-permute-start | bytes 1572872 | tf_op jit(solution)/shard_map/ppermute | solution.py:16
  102.5 59.1 %collective-permute-start.11 = (f32[512,256]{0,1:T(8,128)}, f32[512,256]{0,1:T(8,128)}, u32[]{:S(2)}, u32[]{:S(2)}) collective-permute-start(f32[512,256]{0,1:T(8,128)} %copy.48), channel_id=1, source_target_pairs={{6,0},{8,2},{10,4},{12,6},{14,8},{16,10},{18,12},{20,14},{22,16},{... | collective-permute-start | bytes 1572872 | tf_op jit(solution)/shard_map/ppermute | solution.py:16
  105.9 58.9 %collective-permute-start.12 = (f32[512,256]{0,1:T(8,128)}, f32[512,256]{0,1:T(8,128)}, u32[]{:S(2)}, u32[]{:S(2)}) collective-permute-start(f32[512,256]{0,1:T(8,128)} %copy.49), channel_id=1, source_target_pairs={{8,0},{10,2},{12,4},{14,6},{16,8},{18,10},{20,12},{22,14},{24,16},... | collective-permute-start | bytes 1572872 | tf_op jit(solution)/shard_map/ppermute | solution.py:16
  107.2 445.1 %all-reduce.6.cloned.1.call-start = ((), (), s32[]{:S(2)}) async-start(), calls=%async_computation.1 | async-start | bytes 1048576 | tf_op jit(solution)/shard_map/psum | solution.py:80
  108.2 93.6 %collective-permute-start.13 = (f32[512,256]{0,1:T(8,128)}, f32[512,256]{0,1:T(8,128)S(1)}, u32[]{:S(2)}, u32[]{:S(2)}) collective-permute-start(f32[512,256]{0,1:T(8,128)} %copy.50), channel_id=1, source_target_pairs={{10,0},{12,2},{14,4},{16,6},{18,8},{20,10},{22,12},{24,14},{26,16}... | collective-permute-start | bytes 1572872 | tf_op jit(solution)/shard_map/ppermute | solution.py:16
  110.5 91.3 %collective-permute-start.14 = (f32[512,256]{0,1:T(8,128)}, f32[512,256]{0,1:T(8,128)S(1)}, u32[]{:S(2)}, u32[]{:S(2)}) collective-permute-start(f32[512,256]{0,1:T(8,128)} %copy.51), channel_id=1, source_target_pairs={{12,0},{14,2},{16,4},{18,6},{20,8},{22,10},{24,12},{26,14},{28,16}... | collective-permute-start | bytes 1572872 | tf_op jit(solution)/shard_map/ppermute | solution.py:16
  134.6 128.1 %collective-permute-start.15 = (f32[512,256]{0,1:T(8,128)}, f32[512,256]{0,1:T(8,128)S(1)}, u32[]{:S(2)}, u32[]{:S(2)}) collective-permute-start(f32[512,256]{0,1:T(8,128)} %copy.52), channel_id=1, source_target_pairs={{14,0},{16,2},{18,4},{20,6},{22,8},{24,10},{26,12},{28,14},{30,16}... | collective-permute-start | bytes 1572872 | tf_op jit(solution)/shard_map/ppermute | solution.py:16
  161.7 101.1 %collective-permute-start.8 = (f32[512,256]{0,1:T(8,128)}, f32[512,256]{0,1:T(8,128)S(1)}, u32[]{:S(2)}, u32[]{:S(2)}) collective-permute-start(f32[512,256]{0,1:T(8,128)} %copy.45), channel_id=1, source_target_pairs={{0,2},{2,4},{4,6},{6,8},{8,10},{10,12},{12,14},{14,16},{16,18},{18... | collective-permute-start | bytes 1572872 | tf_op jit(solution)/shard_map/ppermute | solution.py:16
  164.7 98.8 %collective-permute-start.9 = (f32[512,256]{0,1:T(8,128)}, f32[512,256]{0,1:T(8,128)}, u32[]{:S(2)}, u32[]{:S(2)}) collective-permute-start(f32[512,256]{0,1:T(8,128)} %copy.46), channel_id=1, source_target_pairs={{2,0},{4,2},{6,4},{8,6},{10,8},{12,10},{14,12},{16,14},{18,16},{20... | collective-permute-start | bytes 1572872 | tf_op jit(solution)/shard_map/ppermute | solution.py:16
  269.0 298.2 %all-gather.7.cloned.1.call-start = ((), (), s32[]{:S(2)}) async-start(), calls=%async_computation.2 | async-start | bytes 1572864 | tf_op jit(solution)/shard_map/all_gather | solution.py:91
  555.3 240.3 %all-reduce.8.cloned.1.call-start = ((), (), s32[]{:S(2)}) async-start(), calls=%async_computation.3 | async-start | bytes 2097152 | tf_op jit(solution)/shard_map/psum | solution.py:92
  571.7 638.5 %all-gather.9.cloned.1.call-start = ((), (), s32[]{:S(2)}) async-start(), calls=%async_computation.4 | async-start | bytes 1572864 | tf_op jit(solution)/shard_map/all_gather | solution.py:79
  941.3 23.6 %collective-permute-start.17 = (bf16[512,256]{0,1:T(8,128)(2,1)S(1)}, bf16[512,256]{0,1:T(8,128)(2,1)S(1)}, u32[]{:S(2)}, u32[]{:S(2)}) collective-permute-start(bf16[512,256]{0,1:T(8,128)(2,1)S(1)} %get-tuple-element.190), channel_id=1, source_target_pairs={{0,10},{2,12},{4,14},{6,16},{8,18},{10,20},{12,22},{14,24},{16,26}... | collective-permute-start | bytes 786440 | tf_op jit(solution)/shard_map/ppermute | solution.py:16
  944.4 24.6 %collective-permute-start.18 = (bf16[512,256]{0,1:T(8,128)(2,1)S(1)}, bf16[512,256]{0,1:T(8,128)(2,1)S(1)}, u32[]{:S(2)}, u32[]{:S(2)}) collective-permute-start(bf16[512,256]{0,1:T(8,128)(2,1)S(1)} %get-tuple-element.190), channel_id=1, source_target_pairs={{0,8},{2,10},{4,12},{6,14},{8,16},{10,18},{12,20},{14,22},{16,24},... | collective-permute-start | bytes 786440 | tf_op jit(solution)/shard_map/ppermute | solution.py:16
  947.5 26.3 %collective-permute-start.19 = (bf16[512,256]{0,1:T(8,128)(2,1)S(1)}, bf16[512,256]{0,1:T(8,128)(2,1)S(1)}, u32[]{:S(2)}, u32[]{:S(2)}) collective-permute-start(bf16[512,256]{0,1:T(8,128)(2,1)S(1)} %get-tuple-element.190), channel_id=1, source_target_pairs={{0,6},{2,8},{4,10},{6,12},{8,14},{10,16},{12,18},{14,20},{16,22},{... | collective-permute-start | bytes 786440 | tf_op jit(solution)/shard_map/ppermute | solution.py:16
  951.5 25.1 %collective-permute-start.20 = (bf16[512,256]{0,1:T(8,128)(2,1)S(1)}, bf16[512,256]{0,1:T(8,128)(2,1)S(1)}, u32[]{:S(2)}, u32[]{:S(2)}) collective-permute-start(bf16[512,256]{0,1:T(8,128)(2,1)S(1)} %get-tuple-element.190), channel_id=1, source_target_pairs={{0,4},{2,6},{4,8},{6,10},{8,12},{10,14},{12,16},{14,18},{16,20},{1... | collective-permute-start | bytes 786440 | tf_op jit(solution)/shard_map/ppermute | solution.py:16
  996.5 72.3 %collective-permute-start.24 = (f32[512,256]{0,1:T(8,128)}, f32[512,256]{0,1:T(8,128)}, u32[]{:S(2)}, u32[]{:S(2)}) collective-permute-start(f32[512,256]{0,1:T(8,128)} %copy.55), channel_id=1, source_target_pairs={{0,2},{2,4},{4,6},{6,8},{8,10},{10,12},{12,14},{14,16},{16,18},{18... | collective-permute-start | bytes 1572872 | tf_op jit(solution)/shard_map/ppermute | solution.py:16
  1059.2 27.2 %collective-permute-start.26 = (f32[512,256]{0,1:T(8,128)}, f32[512,256]{0,1:T(8,128)}, u32[]{:S(2)}, u32[]{:S(2)}) collective-permute-start(f32[512,256]{0,1:T(8,128)} %copy.57), channel_id=1, source_target_pairs={{4,0},{6,2},{8,4},{10,6},{12,8},{14,10},{16,12},{18,14},{20,16},{2... | collective-permute-start | bytes 1572872 | tf_op jit(solution)/shard_map/ppermute | solution.py:16
  1061.2 429.7 %all-reduce.10.cloned.1.call-start = ((), (), s32[]{:S(2)}) async-start(), calls=%async_computation.5 | async-start | bytes 1048576 | tf_op jit(solution)/shard_map/psum | solution.py:80
  1062.2 32.8 %collective-permute-start.27 = (f32[512,256]{0,1:T(8,128)}, f32[512,256]{0,1:T(8,128)S(1)}, u32[]{:S(2)}, u32[]{:S(2)}) collective-permute-start(f32[512,256]{0,1:T(8,128)} %copy.58), channel_id=1, source_target_pairs={{6,0},{8,2},{10,4},{12,6},{14,8},{16,10},{18,12},{20,14},{22,16},{... | collective-permute-start | bytes 1572872 | tf_op jit(solution)/shard_map/ppermute | solution.py:16
  1064.5 58.9 %collective-permute-start.28 = (f32[512,256]{0,1:T(8,128)}, f32[512,256]{0,1:T(8,128)S(1)}, u32[]{:S(2)}, u32[]{:S(2)}) collective-permute-start(f32[512,256]{0,1:T(8,128)} %copy.59), channel_id=1, source_target_pairs={{8,0},{10,2},{12,4},{14,6},{16,8},{18,10},{20,12},{22,14},{24,16},... | collective-permute-start | bytes 1572872 | tf_op jit(solution)/shard_map/ppermute | solution.py:16
  1068.8 58.9 %collective-permute-start.29 = (f32[512,256]{0,1:T(8,128)}, f32[512,256]{0,1:T(8,128)S(1)}, u32[]{:S(2)}, u32[]{:S(2)}) collective-permute-start(f32[512,256]{0,1:T(8,128)} %copy.60), channel_id=1, source_target_pairs={{10,0},{12,2},{14,4},{16,6},{18,8},{20,10},{22,12},{24,14},{26,16}... | collective-permute-start | bytes 1572872 | tf_op jit(solution)/shard_map/ppermute | solution.py:16
  1072.3 135.8 %collective-permute-start.30 = (f32[512,256]{0,1:T(8,128)}, f32[512,256]{0,1:T(8,128)S(1)}, u32[]{:S(2)}, u32[]{:S(2)}) collective-permute-start(f32[512,256]{0,1:T(8,128)} %copy.61), channel_id=1, source_target_pairs={{12,0},{14,2},{16,4},{18,6},{20,8},{22,10},{24,12},{26,14},{28,16}... | collective-permute-start | bytes 1572872 | tf_op jit(solution)/shard_map/ppermute | solution.py:16
  1086.4 121.7 %collective-permute-start.31 = (f32[512,256]{0,1:T(8,128)}, f32[512,256]{0,1:T(8,128)}, u32[]{:S(2)}, u32[]{:S(2)}) collective-permute-start(f32[512,256]{0,1:T(8,128)} %copy.62), channel_id=1, source_target_pairs={{14,0},{16,2},{18,4},{20,6},{22,8},{24,10},{26,12},{28,14},{30,16}... | collective-permute-start | bytes 1572872 | tf_op jit(solution)/shard_map/ppermute | solution.py:16
  1213.4 292.4 %all-gather.11.cloned.1.call-start = ((), (), s32[]{:S(2)}) async-start(), calls=%async_computation.6 | async-start | bytes 1572864 | tf_op jit(solution)/shard_map/all_gather | solution.py:91
  1493.9 239.5 %all-reduce.12.cloned.1.call-start = ((), (), s32[]{:S(2)}) async-start(), calls=%async_computation.7 | async-start | bytes 2097152 | tf_op jit(solution)/shard_map/psum | solution.py:92
  (20 other events, 1523.2 us)
Sparse Core Ops, SparseCore 0:
  107.3 137.3 all-gather.4
  269.2 283.1 all-reduce.5
  555.4 11.8 all-gather.6
  573.3 222.1 all-reduce.7
  1061.3 101.0 all-gather.8
  1213.6 277.2 all-reduce.9
  1494.0 11.8 all-gather.10
  1511.2 222.1 all-reduce.11
where the time goes:
time: 1890 us; the launch traced here: 1880 us
  waiting for transfers between devices  1340 us (71%)
  other arithmetic  251 us (13%)
  starting transfers between devices  182 us (10%)
  local copies, waits for them, and re-layouts  56.5 us (3%)
  matrix products  31.1 us (2%)
  between operations  21.3 us (1%)
    psum x2, waiting for transfers between devices, shards(): lax.psum(jnp.dot(current_all.T, applied, precision=exact_mode, preferred_...  561 us
    psum x2, waiting for transfers between devices, shards(): lax.psum(jnp.dot(update_all.T, update_all, precision=exact_mode, preferre...  445 us
    ppermute x32, waiting for transfers between devices, shifted(): return lax.ppermute(block, axis, route)  306 us
    ppermute x32, starting transfers between devices, shifted(): return lax.ppermute(block, axis, route)  181 us
    another operation x29, other arithmetic, shards(): factor = jnp.linalg.cholesky(gram_matrix)  158 us
    another operation x6, other arithmetic, shards(): lax.linalg.triangular_solve(factor, update_all, left_side=False, lower=Tr...  79.6 us
  transfers between devices with their start and end apart: 40, of which 26 were waited for; matrix products, arithmetic and copies ran while one was open for 1% of the time, Pallas kernels for 0%

commit v1 on v0

--- a/solution.py
+++ b/solution.py
@@ -14,6 +14,27 @@
     devices = range(lax.axis_size(axis))
     route = [(i - distance, i) for i in devices if i - distance in devices]
     return lax.ppermute(block, axis, route)
+
+
+def summed_over_patch(block):
+    size = lax.axis_size("patch")
+    me = lax.axis_index("patch")
+    bits = [b for b in (0, 2, 5, 1, 3, 6, 4) if (1 << b) < size]
+    held = block
+    for b in bits:
+        half = held.shape[0] // 2
+        side = (me >> b) & 1
+        keep = lax.dynamic_slice_in_dim(held, side * half, half, 0)
+        send = lax.dynamic_slice_in_dim(held, (1 - side) * half, half, 0)
+        route = [(i, i ^ (1 << b)) for i in range(size)]
+        held = keep + lax.ppermute(send, "patch", route)
+    for b in reversed(bits):
+        side = (me >> b) & 1
+        route = [(i, i ^ (1 << b)) for i in range(size)]
+        other = lax.ppermute(held, "patch", route)
+        both = jnp.stack([held, other, held])
+        held = lax.dynamic_slice_in_dim(both, side, 2, 0).reshape(-1, *held.shape[1:])
+    return held
 
 
 def accumulate(window_x, totals, block_tiles, row_ids, col_ids, used_slots, window_start):
@@ -77,24 +98,22 @@
             outgoing = jnp.where(parity == 0, lower_seg, upper_seg)
             applied = applied + shifted(outgoing, "patch", offset)
         current_all = lax.all_gather(current, "vec", axis=1, tiled=True)
-        rayleigh = lax.psum(
+        rayleigh = summed_over_patch(
             jnp.dot(
                 current_all.T, applied, precision=exact_mode, preferred_element_type=jnp.float32
             )
-            / total_rows,
-            "patch",
+            / total_rows
         )
         residual = applied - jnp.dot(
             current_all, rayleigh, precision=exact_mode, preferred_element_type=jnp.float32
         )
         update = current - step_rate * residual
         update_all = lax.all_gather(update, "vec", axis=1, tiled=True)
-        gram_matrix = lax.psum(
+        gram_matrix = summed_over_patch(
             jnp.dot(
                 update_all.T, update_all, precision=exact_mode, preferred_element_type=jnp.float32
             )
-            / total_rows,
-            "patch",
+            / total_rows
         )
         factor = jnp.linalg.cholesky(gram_matrix)
         solved = lax.linalg.triangular_solve(

time: 1890 us -> 1360 us (0.72)
  waiting for transfers between devices: 1340 us -> 567 us
  starting transfers between devices: 182 us -> 359 us
  other arithmetic: 251 us -> 289 us
    psum x4 -> x0, waiting for transfers between devices: 1010 us -> none  [the longest x2 561 us: shards(): lax.psum(jnp.dot(current_all.T, applied, precision=exact_mode, preferred_...]
    ppermute x0 -> x56, starting transfers between devices: none -> 259 us  [the longest x28 192 us: summed_over_patch(): held = keep + lax.ppermute(send, 'patch', route)]
    ppermute x0 -> x56, waiting for transfers between devices: none -> 223 us  [the longest x28 119 us: summed_over_patch(): held = keep + lax.ppermute(send, 'patch', route)]
    ppermute x32, starting transfers between devices: 181 us -> 100 us  [shifted(): return lax.ppermute(block, axis, route)]
    scatter-add x0 -> x8, other arithmetic: none -> 32.3 us  [one_turn(): return partial_value.at[rows_here].add(direct).at[cols_here].add(mirror)]
  transfers between devices with their start and end apart: 40 -> 92, of which waited for: 26 -> 77; matrix products, arithmetic and copies ran while one was open for 1% -> 2% of each run, Pallas kernels for 0% -> 0%
where the time goes in v1:
time: 1360 us; the launch traced here: 1350 us
  waiting for transfers between devices  567 us (42%)
  starting transfers between devices  359 us (26%)
  other arithmetic  289 us (21%)
  local copies, waits for them, and re-layouts  72.8 us (5%)
  matrix products  39.9 us (3%)
  between operations  21.7 us (2%)
    ppermute x32, waiting for transfers between devices, shifted(): return lax.ppermute(block, axis, route)  312 us
    ppermute x28, starting transfers between devices, summed_over_patch(): held = keep + lax.ppermute(send, 'patch', route)  192 us
    another operation x29, other arithmetic, shards(): factor = jnp.linalg.cholesky(gram_matrix)  159 us
    ppermute x28, waiting for transfers between devices, summed_over_patch(): held = keep + lax.ppermute(send, 'patch', route)  119 us
    ppermute x28, waiting for transfers between devices, summed_over_patch(): other = lax.ppermute(held, 'patch', route)  103 us
    ppermute x32, starting transfers between devices, shifted(): return lax.ppermute(block, axis, route)  100 us
    another operation x6, other arithmetic, shards(): lax.linalg.triangular_solve(factor, update_all, left_side=False, lower=Tr...  79.2 us
    ppermute x28, starting transfers between devices, summed_over_patch(): other = lax.ppermute(held, 'patch', route)  66.9 us
  transfers between devices with their start and end apart: 92, of which 77 were waited for; matrix products, arithmetic and copies ran while one was open for 2% of the time, Pallas kernels for 0%

profile of v1, /device:TPU:4, one launch (start us, length us, event | category | flops | bytes accessed | tf_op | source)
XLA Modules:
  0.0 1350.4 jit_solution(5030832912494969805)
XLA Ops:
  64.0 33.6 %while.24 = (s32[]{:T(128)}, f32[16,256,256]{2,1,0:T(8,128)}, s32[]{:T(128)}, s32[64]{0:T(128)S(1)}, s32[]{:T(128)}, /*index=5*/bf16[64,256,256]{2,1,0:T(8,128)(...) while((s32[]{:T(128)}, f32[16,256,256]{2,1,0:T(8,128)}, ...), condition=%wide.region_3.4_spmd, body=%wide.region_0.3_spmd.sunk | while | flops 538970240 | bytes 25174700 | solution.py:66
  119.5 15.0 %collective-permute-done.10 = f32[512,256]{0,1:T(8,128)} collective-permute-done((f32[512,256]{0,1:T(8,128)}, f32[512,256]{0,1:T(8,128)}, u32[]{:S(2)}, u32[]{:S(2)}) %collective-permute-start.10) | collective-permute-done | bytes 524320 | tf_op jit(solution)/shard_map/ppermute | solution.py:16
  135.8 21.1 %collective-permute-done.11 = f32[512,256]{0,1:T(8,128)} collective-permute-done((f32[512,256]{0,1:T(8,128)}, f32[512,256]{0,1:T(8,128)}, u32[]{:S(2)}, u32[]{:S(2)}) %collective-permute-start.11) | collective-permute-done | bytes 524320 | tf_op jit(solution)/shard_map/ppermute | solution.py:16
  158.8 11.8 collective-permute-start.9
  170.8 30.9 %collective-permute-done.13 = f32[512,256]{0,1:T(8,128)S(1)} collective-permute-done((f32[512,256]{0,1:T(8,128)}, f32[512,256]{0,1:T(8,128)S(1)}, u32[]{:S(2)}, u32[]{:S(2)}) %collective-permute-start.13) | collective-permute-done | bytes 524320 | tf_op jit(solution)/shard_map/ppermute | solution.py:16
  201.7 67.7 %collective-permute-done.14 = f32[512,256]{0,1:T(8,128)S(1)} collective-permute-done((f32[512,256]{0,1:T(8,128)}, f32[512,256]{0,1:T(8,128)S(1)}, u32[]{:S(2)}, u32[]{:S(2)}) %collective-permute-start.14) | collective-permute-done | bytes 524320 | tf_op jit(solution)/shard_map/ppermute | solution.py:16
  281.3 42.9 %collective-permute-start.17 = (f32[128,256]{0,1:T(8,128)S(1)}, f32[128,256]{0,1:T(8,128)S(1)}, u32[]{:S(2)}, u32[]{:S(2)}) collective-permute-start(f32[128,256]{0,1:T(8,128)S(1)} %constant_dynamic-slice_fusion.56), channel_id=1, source_target_pairs={{0,8},{2,10},{4,12},{6,14},{8,0},{10,2},{12,4},{14,6},{16,24},{18,... | collective-permute-start | bytes 393224 | tf_op jit(solution)/shard_map/ppermute | solution.py:30
  327.2 10.6 collective-permute-start.18
  363.1 17.2 %collective-permute-start.22 = (f32[4,256]{0,1:T(8,128)S(1)}, f32[4,256]{0,1:T(8,128)S(1)}, u32[]{:S(2)}, u32[]{:S(2)}) collective-permute-start(f32[4,256]{0,1:T(8,128)S(1)} %constant_dynamic-slice_fusion.51), channel_id=1, source_target_pairs={{0,32},{2,34},{4,36},{6,38},{8,40},{10,42},{12,44},{14,46},{16,48}... | collective-permute-start | bytes 12296 | tf_op jit(solution)/shard_map/ppermute | solution.py:30
  429.0 15.2 %all-gather.7.cloned.1.call-done = f32[512,512]{0,1:T(8,128)} async-done(((f32[512,256]{0,1:T(8,128)}), f32[512,512]{0,1:T(8,128)}) %all-gather.7.cloned.1.call-update) | async-done | bytes 1048592 | tf_op jit(solution)/shard_map/all_gather | solution.py:111
  449.0 13.0 collective-permute-done.30
  470.0 14.3 %collective-permute-start.32 = (f32[64,512]{1,0:T(8,128)S(1)}, f32[64,512]{1,0:T(8,128)S(1)}, u32[]{:S(2)}, u32[]{:S(2)}) collective-permute-start(f32[64,512]{1,0:T(8,128)S(1)} %constant_dynamic-slice_fusion.46), channel_id=1, source_target_pairs={{0,64},{2,66},{4,68},{6,70},{8,72},{10,74},{12,76},{14,78},{16,80}... | collective-permute-start | bytes 393224 | tf_op jit(solution)/shard_map/ppermute | solution.py:30
  557.3 11.7 cholesky.286
  579.7 11.7 cholesky.305
  602.3 11.7 cholesky.326
  625.1 11.7 cholesky.343
  649.3 39.3 %custom-call.30 = f32[4,128,128]{1,2,0:T(8,128)S(1)} custom-call(f32[4,128,128]{2,1,0:T(8,128)S(1)} %get-tuple-element.116), custom_call_target="InvertDiagBlocksLowerTriangular" | custom-call | tf_op jit(solution)/shard_map/triangular_solve/custom-call.3 | solution.py:119
  738.1 33.6 %while.25 = (s32[]{:T(128)}, f32[16,256,256]{2,1,0:T(8,128)}, s32[]{:T(128)}, s32[64]{0:T(128)S(1)}, s32[]{:T(128)}, /*index=5*/bf16[64,256,256]{2,1,0:T(8,128)(...) while((s32[]{:T(128)}, f32[16,256,256]{2,1,0:T(8,128)}, ...), condition=%wide.region_15.18_spmd, body=%wide.region_12.17_spmd.sunk | while | flops 538970240 | bytes 25174700 | solution.py:66
  808.3 26.5 %collective-permute-done.54 = f32[512,256]{0,1:T(8,128)} collective-permute-done((f32[512,256]{0,1:T(8,128)}, f32[512,256]{0,1:T(8,128)}, u32[]{:S(2)}, u32[]{:S(2)}) %collective-permute-start.54) | collective-permute-done | bytes 524320 | tf_op jit(solution)/shard_map/ppermute | solution.py:16
  839.7 35.2 %collective-permute-done.56 = f32[512,256]{0,1:T(8,128)S(1)} collective-permute-done((f32[512,256]{0,1:T(8,128)}, f32[512,256]{0,1:T(8,128)S(1)}, u32[]{:S(2)}, u32[]{:S(2)}) %collective-permute-start.56) | collective-permute-done | bytes 524320 | tf_op jit(solution)/shard_map/ppermute | solution.py:16
  874.9 23.7 %collective-permute-done.57 = f32[512,256]{0,1:T(8,128)S(1)} collective-permute-done((f32[512,256]{0,1:T(8,128)}, f32[512,256]{0,1:T(8,128)S(1)}, u32[]{:S(2)}, u32[]{:S(2)}) %collective-permute-start.57) | collective-permute-done | bytes 524320 | tf_op jit(solution)/shard_map/ppermute | solution.py:16
  898.6 53.8 %collective-permute-done.58 = f32[512,256]{0,1:T(8,128)S(1)} collective-permute-done((f32[512,256]{0,1:T(8,128)}, f32[512,256]{0,1:T(8,128)S(1)}, u32[]{:S(2)}, u32[]{:S(2)}) %collective-permute-start.58) | collective-permute-done | bytes 524320 | tf_op jit(solution)/shard_map/ppermute | solution.py:16
  964.5 17.2 %collective-permute-start.61 = (f32[128,256]{1,0:T(8,128)S(1)}, f32[128,256]{1,0:T(8,128)S(1)}, u32[]{:S(2)}, u32[]{:S(2)}) collective-permute-start(f32[128,256]{1,0:T(8,128)S(1)} %constant_dynamic-slice_fusion.35), channel_id=1, source_target_pairs={{0,8},{2,10},{4,12},{6,14},{8,0},{10,2},{12,4},{14,6},{16,24},{18,... | collective-permute-start | bytes 393224 | tf_op jit(solution)/shard_map/ppermute | solution.py:30
  989.1 19.6 %collective-permute-start.63 = (f32[32,256]{1,0:T(8,128)S(1)}, f32[32,256]{1,0:T(8,128)S(1)}, u32[]{:S(2)}, u32[]{:S(2)}) collective-permute-start(f32[32,256]{1,0:T(8,128)S(1)} %constant_dynamic-slice_fusion.32), channel_id=1, source_target_pairs={{0,4},{2,6},{4,0},{6,2},{8,12},{10,14},{12,8},{14,10},{16,20},{18,... | collective-permute-start | bytes 98312 | tf_op jit(solution)/shard_map/ppermute | solution.py:30
  1024.0 22.0 %collective-permute-start.66 = (f32[4,256]{1,0:T(4,128)S(1)}, f32[4,256]{1,0:T(4,128)S(1)}, u32[]{:S(2)}, u32[]{:S(2)}) collective-permute-start(f32[4,256]{1,0:T(4,128)S(1)} %constant_dynamic-slice_fusion.26), channel_id=1, source_target_pairs={{0,32},{2,34},{4,36},{6,38},{8,40},{10,42},{12,44},{14,46},{16,48}... | collective-permute-start | bytes 12296 | tf_op jit(solution)/shard_map/ppermute | solution.py:30
  1089.7 16.9 %all-gather.11.cloned.1.call-done = f32[512,512]{0,1:T(8,128)} async-done(((f32[512,256]{0,1:T(8,128)}), f32[512,512]{0,1:T(8,128)}) %all-gather.11.cloned.1.call-update) | async-done | bytes 1048592 | tf_op jit(solution)/shard_map/all_gather | solution.py:111
  1111.3 13.0 collective-permute-done.74
  1207.0 11.7 cholesky.358
  1229.4 11.7 cholesky.377
  1253.1 11.7 cholesky.398
  1276.0 11.9 cholesky.415
  1299.5 39.3 %custom-call.34 = f32[4,128,128]{1,2,0:T(8,128)S(1)} custom-call(f32[4,128,128]{2,1,0:T(8,128)S(1)} %get-tuple-element.117), custom_call_target="InvertDiagBlocksLowerTriangular" | custom-call | tf_op jit(solution)/shard_map/triangular_solve/custom-call.3 | solution.py:119
  (475 shorter events, 684.4 us)
Async XLA Ops:
  7.2 265.3 %all-gather.5.cloned.1.call-start = ((), (), s32[]{:S(2)}) async-start(), calls=%async_computation | async-start | bytes 1572864 | tf_op jit(solution)/shard_map/all_gather | solution.py:100
  8.5 23.7 %collective-permute-start.7 = (bf16[512,256]{0,1:T(8,128)(2,1)S(1)}, bf16[512,256]{0,1:T(8,128)(2,1)S(1)}, u32[]{:S(2)}, u32[]{:S(2)}) collective-permute-start(bf16[512,256]{0,1:T(8,128)(2,1)S(1)} %convert_element_type.8), channel_id=1, source_target_pairs={{0,14},{2,16},{4,18},{6,20},{8,22},{10,24},{12,26},{14,28},{16,30}... | collective-permute-start | bytes 786440 | tf_op jit(solution)/shard_map/ppermute | solution.py:16
  13.7 22.9 %collective-permute-start = (bf16[512,256]{0,1:T(8,128)(2,1)S(1)}, bf16[512,256]{0,1:T(8,128)(2,1)S(1)}, u32[]{:S(2)}, u32[]{:S(2)}) collective-permute-start(bf16[512,256]{0,1:T(8,128)(2,1)S(1)} %convert_element_type.8), channel_id=1, source_target_pairs={{0,12},{2,14},{4,16},{6,18},{8,20},{10,22},{12,24},{14,26},{16,28}... | collective-permute-start | bytes 786440 | tf_op jit(solution)/shard_map/ppermute | solution.py:16
  19.7 23.0 %collective-permute-start.1 = (bf16[512,256]{0,1:T(8,128)(2,1)S(1)}, bf16[512,256]{0,1:T(8,128)(2,1)S(1)}, u32[]{:S(2)}, u32[]{:S(2)}) collective-permute-start(bf16[512,256]{0,1:T(8,128)(2,1)S(1)} %convert_element_type.8), channel_id=1, source_target_pairs={{0,10},{2,12},{4,14},{6,16},{8,18},{10,20},{12,22},{14,24},{16,26}... | collective-permute-start | bytes 786440 | tf_op jit(solution)/shard_map/ppermute | solution.py:16
  24.5 23.8 %collective-permute-start.2 = (bf16[512,256]{0,1:T(8,128)(2,1)S(1)}, bf16[512,256]{0,1:T(8,128)(2,1)S(1)}, u32[]{:S(2)}, u32[]{:S(2)}) collective-permute-start(bf16[512,256]{0,1:T(8,128)(2,1)S(1)} %convert_element_type.8), channel_id=1, source_target_pairs={{0,8},{2,10},{4,12},{6,14},{8,16},{10,18},{12,20},{14,22},{16,24},... | collective-permute-start | bytes 786440 | tf_op jit(solution)/shard_map/ppermute | solution.py:16
  27.4 26.6 %collective-permute-start.3 = (bf16[512,256]{0,1:T(8,128)(2,1)S(1)}, bf16[512,256]{0,1:T(8,128)(2,1)S(1)}, u32[]{:S(2)}, u32[]{:S(2)}) collective-permute-start(bf16[512,256]{0,1:T(8,128)(2,1)S(1)} %convert_element_type.8), channel_id=1, source_target_pairs={{0,6},{2,8},{4,10},{6,12},{8,14},{10,16},{12,18},{14,20},{16,22},{... | collective-permute-start | bytes 786440 | tf_op jit(solution)/shard_map/ppermute | solution.py:16
  32.2 26.5 %collective-permute-start.4 = (bf16[512,256]{0,1:T(8,128)(2,1)S(1)}, bf16[512,256]{0,1:T(8,128)(2,1)S(1)}, u32[]{:S(2)}, u32[]{:S(2)}) collective-permute-start(bf16[512,256]{0,1:T(8,128)(2,1)S(1)} %convert_element_type.8), channel_id=1, source_target_pairs={{0,4},{2,6},{4,8},{6,10},{8,12},{10,14},{12,16},{14,18},{16,20},{1... | collective-permute-start | bytes 786440 | tf_op jit(solution)/shard_map/ppermute | solution.py:16
  36.6 22.1 %collective-permute-start.5 = (bf16[512,256]{0,1:T(8,128)(2,1)S(1)}, bf16[512,256]{0,1:T(8,128)(2,1)S(1)}, u32[]{:S(2)}, u32[]{:S(2)}) collective-permute-start(bf16[512,256]{0,1:T(8,128)(2,1)S(1)} %convert_element_type.8), channel_id=1, source_target_pairs={{0,2},{2,4},{4,6},{6,8},{8,10},{10,12},{12,14},{14,16},{16,18},{18... | collective-permute-start | bytes 786440 | tf_op jit(solution)/shard_map/ppermute | solution.py:16
  103.3 31.3 %collective-permute-start.10 = (f32[512,256]{0,1:T(8,128)}, f32[512,256]{0,1:T(8,128)}, u32[]{:S(2)}, u32[]{:S(2)}) collective-permute-start(f32[512,256]{0,1:T(8,128)} %copy.161), channel_id=1, source_target_pairs={{4,0},{6,2},{8,4},{10,6},{12,8},{14,10},{16,12},{18,14},{20,16},{2... | collective-permute-start | bytes 1572872 | tf_op jit(solution)/shard_map/ppermute | solution.py:16
  107.2 49.7 %collective-permute-start.11 = (f32[512,256]{0,1:T(8,128)}, f32[512,256]{0,1:T(8,128)}, u32[]{:S(2)}, u32[]{:S(2)}) collective-permute-start(f32[512,256]{0,1:T(8,128)} %copy.162), channel_id=1, source_target_pairs={{6,0},{8,2},{10,4},{12,6},{14,8},{16,10},{18,12},{20,14},{22,16},{... | collective-permute-start | bytes 1572872 | tf_op jit(solution)/shard_map/ppermute | solution.py:16
  110.6 48.3 %collective-permute-start.12 = (f32[512,256]{0,1:T(8,128)}, f32[512,256]{0,1:T(8,128)}, u32[]{:S(2)}, u32[]{:S(2)}) collective-permute-start(f32[512,256]{0,1:T(8,128)} %copy.163), channel_id=1, source_target_pairs={{8,0},{10,2},{12,4},{14,6},{16,8},{18,10},{20,12},{22,14},{24,16},... | collective-permute-start | bytes 1572872 | tf_op jit(solution)/shard_map/ppermute | solution.py:16
  111.9 332.4 %all-gather.7.cloned.1.call-start = ((), (), s32[]{:S(2)}) async-start(), calls=%async_computation.1 | async-start | bytes 1572864 | tf_op jit(solution)/shard_map/all_gather | solution.py:111
  112.9 88.8 %collective-permute-start.13 = (f32[512,256]{0,1:T(8,128)}, f32[512,256]{0,1:T(8,128)S(1)}, u32[]{:S(2)}, u32[]{:S(2)}) collective-permute-start(f32[512,256]{0,1:T(8,128)} %copy.164), channel_id=1, source_target_pairs={{10,0},{12,2},{14,4},{16,6},{18,8},{20,10},{22,12},{24,14},{26,16}... | collective-permute-start | bytes 1572872 | tf_op jit(solution)/shard_map/ppermute | solution.py:16
  115.2 154.1 %collective-permute-start.14 = (f32[512,256]{0,1:T(8,128)}, f32[512,256]{0,1:T(8,128)S(1)}, u32[]{:S(2)}, u32[]{:S(2)}) collective-permute-start(f32[512,256]{0,1:T(8,128)} %copy.165), channel_id=1, source_target_pairs={{12,0},{14,2},{16,4},{18,6},{20,8},{22,10},{24,12},{26,14},{28,16}... | collective-permute-start | bytes 1572872 | tf_op jit(solution)/shard_map/ppermute | solution.py:16
  134.5 134.8 %collective-permute-start.15 = (f32[512,256]{0,1:T(8,128)}, f32[512,256]{0,1:T(8,128)S(1)}, u32[]{:S(2)}, u32[]{:S(2)}) collective-permute-start(f32[512,256]{0,1:T(8,128)} %copy.166), channel_id=1, source_target_pairs={{14,0},{16,2},{18,4},{20,6},{22,8},{24,10},{26,12},{28,14},{30,16}... | collective-permute-start | bytes 1572872 | tf_op jit(solution)/shard_map/ppermute | solution.py:16
  156.9 112.5 %collective-permute-start.8 = (f32[512,256]{0,1:T(8,128)}, f32[512,256]{0,1:T(8,128)S(1)}, u32[]{:S(2)}, u32[]{:S(2)}) collective-permute-start(f32[512,256]{0,1:T(8,128)} %copy.159), channel_id=1, source_target_pairs={{0,2},{2,4},{4,6},{6,8},{8,10},{10,12},{12,14},{14,16},{16,18},{18... | collective-permute-start | bytes 1572872 | tf_op jit(solution)/shard_map/ppermute | solution.py:16
  158.8 111.4 %collective-permute-start.9 = (f32[512,256]{0,1:T(8,128)}, f32[512,256]{0,1:T(8,128)}, u32[]{:S(2)}, u32[]{:S(2)}) collective-permute-start(f32[512,256]{0,1:T(8,128)} %copy.160), channel_id=1, source_target_pairs={{2,0},{4,2},{6,4},{8,6},{10,8},{12,10},{14,12},{16,14},{18,16},{20... | collective-permute-start | bytes 1572872 | tf_op jit(solution)/shard_map/ppermute | solution.py:16
  281.3 45.8 %collective-permute-start.17 = (f32[128,256]{0,1:T(8,128)S(1)}, f32[128,256]{0,1:T(8,128)S(1)}, u32[]{:S(2)}, u32[]{:S(2)}) collective-permute-start(f32[128,256]{0,1:T(8,128)S(1)} %constant_dynamic-slice_fusion.56), channel_id=1, source_target_pairs={{0,8},{2,10},{4,12},{6,14},{8,0},{10,2},{12,4},{14,6},{16,24},{18,... | collective-permute-start | bytes 393224 | tf_op jit(solution)/shard_map/ppermute | solution.py:30
  429.0 526.7 %all-gather.9.cloned.1.call-start = ((), (), s32[]{:S(2)}) async-start(), calls=%async_computation.2 | async-start | bytes 1572864 | tf_op jit(solution)/shard_map/all_gather | solution.py:100
  693.0 20.6 %collective-permute-start.51 = (bf16[512,256]{0,1:T(8,128)(2,1)S(1)}, bf16[512,256]{0,1:T(8,128)(2,1)S(1)}, u32[]{:S(2)}, u32[]{:S(2)}) collective-permute-start(bf16[512,256]{0,1:T(8,128)(2,1)S(1)} %get-tuple-element.250), channel_id=1, source_target_pairs={{0,14},{2,16},{4,18},{6,20},{8,22},{10,24},{12,26},{14,28},{16,30}... | collective-permute-start | bytes 786440 | tf_op jit(solution)/shard_map/ppermute | solution.py:16
  697.4 20.4 %collective-permute-start.44 = (bf16[512,256]{0,1:T(8,128)(2,1)S(1)}, bf16[512,256]{0,1:T(8,128)(2,1)S(1)}, u32[]{:S(2)}, u32[]{:S(2)}) collective-permute-start(bf16[512,256]{0,1:T(8,128)(2,1)S(1)} %get-tuple-element.250), channel_id=1, source_target_pairs={{0,12},{2,14},{4,16},{6,18},{8,20},{10,22},{12,24},{14,26},{16,28}... | collective-permute-start | bytes 786440 | tf_op jit(solution)/shard_map/ppermute | solution.py:16
  777.4 21.8 %collective-permute-start.52 = (f32[512,256]{0,1:T(8,128)}, f32[512,256]{0,1:T(8,128)}, u32[]{:S(2)}, u32[]{:S(2)}) collective-permute-start(f32[512,256]{0,1:T(8,128)} %copy.170), channel_id=1, source_target_pairs={{0,2},{2,4},{4,6},{6,8},{8,10},{10,12},{12,14},{14,16},{16,18},{18... | collective-permute-start | bytes 1572872 | tf_op jit(solution)/shard_map/ppermute | solution.py:16
  781.4 25.6 %collective-permute-start.53 = (f32[512,256]{0,1:T(8,128)}, f32[512,256]{0,1:T(8,128)}, u32[]{:S(2)}, u32[]{:S(2)}) collective-permute-start(f32[512,256]{0,1:T(8,128)} %copy.171), channel_id=1, source_target_pairs={{2,0},{4,2},{6,4},{8,6},{10,8},{12,10},{14,12},{16,14},{18,16},{20... | collective-permute-start | bytes 1572872 | tf_op jit(solution)/shard_map/ppermute | solution.py:16
  787.9 46.9 %collective-permute-start.54 = (f32[512,256]{0,1:T(8,128)}, f32[512,256]{0,1:T(8,128)}, u32[]{:S(2)}, u32[]{:S(2)}) collective-permute-start(f32[512,256]{0,1:T(8,128)} %copy.172), channel_id=1, source_target_pairs={{4,0},{6,2},{8,4},{10,6},{12,8},{14,10},{16,12},{18,14},{20,16},{2... | collective-permute-start | bytes 1572872 | tf_op jit(solution)/shard_map/ppermute | solution.py:16
  791.4 315.2 %all-gather.11.cloned.1.call-start = ((), (), s32[]{:S(2)}) async-start(), calls=%async_computation.3 | async-start | bytes 1572864 | tf_op jit(solution)/shard_map/all_gather | solution.py:111
  792.7 47.0 %collective-permute-start.55 = (f32[512,256]{0,1:T(8,128)}, f32[512,256]{0,1:T(8,128)S(1)}, u32[]{:S(2)}, u32[]{:S(2)}) collective-permute-start(f32[512,256]{0,1:T(8,128)} %copy.173), channel_id=1, source_target_pairs={{6,0},{8,2},{10,4},{12,6},{14,8},{16,10},{18,12},{20,14},{22,16},{... | collective-permute-start | bytes 1572872 | tf_op jit(solution)/shard_map/ppermute | solution.py:16
  794.9 80.0 %collective-permute-start.56 = (f32[512,256]{0,1:T(8,128)}, f32[512,256]{0,1:T(8,128)S(1)}, u32[]{:S(2)}, u32[]{:S(2)}) collective-permute-start(f32[512,256]{0,1:T(8,128)} %copy.174), channel_id=1, source_target_pairs={{8,0},{10,2},{12,4},{14,6},{16,8},{18,10},{20,12},{22,14},{24,16},... | collective-permute-start | bytes 1572872 | tf_op jit(solution)/shard_map/ppermute | solution.py:16
  799.3 99.4 %collective-permute-start.57 = (f32[512,256]{0,1:T(8,128)}, f32[512,256]{0,1:T(8,128)S(1)}, u32[]{:S(2)}, u32[]{:S(2)}) collective-permute-start(f32[512,256]{0,1:T(8,128)} %copy.175), channel_id=1, source_target_pairs={{10,0},{12,2},{14,4},{16,6},{18,8},{20,10},{22,12},{24,14},{26,16}... | collective-permute-start | bytes 1572872 | tf_op jit(solution)/shard_map/ppermute | solution.py:16
  807.0 145.4 %collective-permute-start.58 = (f32[512,256]{0,1:T(8,128)}, f32[512,256]{0,1:T(8,128)S(1)}, u32[]{:S(2)}, u32[]{:S(2)}) collective-permute-start(f32[512,256]{0,1:T(8,128)} %copy.176), channel_id=1, source_target_pairs={{12,0},{14,2},{16,4},{18,6},{20,8},{22,10},{24,12},{26,14},{28,16}... | collective-permute-start | bytes 1572872 | tf_op jit(solution)/shard_map/ppermute | solution.py:16
  834.8 118.8 %collective-permute-start.59 = (f32[512,256]{0,1:T(8,128)}, f32[512,256]{0,1:T(8,128)}, u32[]{:S(2)}, u32[]{:S(2)}) collective-permute-start(f32[512,256]{0,1:T(8,128)} %copy.177), channel_id=1, source_target_pairs={{14,0},{16,2},{18,4},{20,6},{22,8},{24,10},{26,12},{28,14},{30,16}... | collective-permute-start | bytes 1572872 | tf_op jit(solution)/shard_map/ppermute | solution.py:16
  989.1 21.5 %collective-permute-start.63 = (f32[32,256]{1,0:T(8,128)S(1)}, f32[32,256]{1,0:T(8,128)S(1)}, u32[]{:S(2)}, u32[]{:S(2)}) collective-permute-start(f32[32,256]{1,0:T(8,128)S(1)} %constant_dynamic-slice_fusion.32), channel_id=1, source_target_pairs={{0,4},{2,6},{4,0},{6,2},{8,12},{10,14},{12,8},{14,10},{16,20},{18,... | collective-permute-start | bytes 98312 | tf_op jit(solution)/shard_map/ppermute | solution.py:30
  1024.0 23.6 %collective-permute-start.66 = (f32[4,256]{1,0:T(4,128)S(1)}, f32[4,256]{1,0:T(4,128)S(1)}, u32[]{:S(2)}, u32[]{:S(2)}) collective-permute-start(f32[4,256]{1,0:T(4,128)S(1)} %constant_dynamic-slice_fusion.26), channel_id=1, source_target_pairs={{0,32},{2,34},{4,36},{6,38},{8,40},{10,42},{12,44},{14,46},{16,48}... | collective-permute-start | bytes 12296 | tf_op jit(solution)/shard_map/ppermute | solution.py:30
  (70 other events, 1141.2 us)
Sparse Core Ops, SparseCore 0:
  112.0 132.7 all-gather.4
  429.1 15.1 all-gather.6
  791.5 123.3 all-gather.8
  1089.8 16.7 all-gather.10

commit v2 on v1

--- a/solution.py
+++ b/solution.py
@@ -1,6 +1,8 @@
 import jax
 import jax.numpy as jnp
 from jax import lax
+from jax.experimental import pallas as pl
+from jax.experimental.pallas import tpu as pltpu
 from jax.sharding import PartitionSpec as P
 
 STEPS = 2
@@ -35,6 +37,60 @@
         both = jnp.stack([held, other, held])
         held = lax.dynamic_slice_in_dim(both, side, 2, 0).reshape(-1, *held.shape[1:])
     return held
+
+
+def tile_products(rows_ref, cols_ref, used_ref, tile_ref, x_ref, out_ref):
+    slot = pl.program_id(0)
+
+    @pl.when(slot == 0)
+    def _():
+        out_ref[...] = jnp.zeros_like(out_ref)
+
+    @pl.when(slot < used_ref[0])
+    def _():
+        row = rows_ref[slot]
+        col = cols_ref[slot]
+        tile = tile_ref[0]
+        weight = jnp.where(row == col, jnp.float32(0.5), jnp.float32(1.0))
+        direct = jnp.dot(tile, x_ref[col], preferred_element_type=jnp.float32)
+        out_ref[row] += direct * weight
+        mirror = lax.dot_general(
+            tile, x_ref[row], (((0,), (0,)), ((), ())), preferred_element_type=jnp.float32
+        )
+        out_ref[col] += mirror * weight
+
+
+def hessian_window(window_x, blocks, rows_local, cols_local, used):
+    slots, tile_size, _ = blocks.shape
+    window_tiles, _, col_width = window_x.shape
+
+    def tile_at(slot, rows, cols, used_ref):
+        return (jnp.maximum(jnp.minimum(slot, used_ref[0] - 1), 0), 0, 0)
+
+    def whole(slot, rows, cols, used_ref):
+        return (0, 0, 0)
+
+    grid_spec = pltpu.PrefetchScalarGridSpec(
+        num_scalar_prefetch=3,
+        grid=(slots,),
+        in_specs=[
+            pl.BlockSpec((1, tile_size, tile_size), tile_at),
+            pl.BlockSpec((window_tiles, tile_size, col_width), whole),
+        ],
+        out_specs=pl.BlockSpec((window_tiles, tile_size, col_width), whole),
+    )
+    flops = 4 * slots * tile_size * tile_size * col_width
+    return pl.pallas_call(
+        tile_products,
+        grid_spec=grid_spec,
+        out_shape=jax.ShapeDtypeStruct((window_tiles, tile_size, col_width), jnp.float32),
+        compiler_params=pltpu.CompilerParams(dimension_semantics=("arbitrary",)),
+        cost_estimate=pl.CostEstimate(
+            flops=flops,
+            bytes_accessed=blocks.size * 2 + window_x.size * 2 + window_tiles * tile_size * col_width * 4,
+            transcendentals=0,
+        ),
+    )(rows_local, cols_local, used, blocks, window_x)
 
 
 def accumulate(window_x, totals, block_tiles, row_ids, col_ids, used_slots, window_start):
@@ -85,9 +141,8 @@
         lower_side = jnp.concatenate([pieces[6 - segment] for segment in range(8)], axis=0)
         upper_side = jnp.concatenate([pieces[7 - segment] for segment in range(8)], axis=0)
         window_x = jnp.where(parity == 0, lower_side, upper_side).reshape(16, tile_size, col_width)
-        totals = jnp.zeros((16, tile_size, col_width), jnp.float32)
-        totals = accumulate(
-            window_x, totals, blocks, block_row, block_col, used_slots, window_start
+        totals = hessian_window(
+            window_x, blocks, block_row - window_start, block_col - window_start, block_count
         )
         segments = totals.reshape(8, dev_rows, col_width)
         zero_rows = jnp.zeros((dev_rows, col_width), jnp.float32)

time: 1360 us -> 1130 us (0.83)
  waiting for transfers between devices: 567 us -> 398 us
  Pallas kernels: 0 us -> 34.3 us
  other arithmetic: 289 us -> 255 us
  starting transfers between devices: 359 us -> 335 us
  local copies, waits for them, and re-layouts: 72.8 us -> 50.4 us
  matrix products: 39.9 us -> 25.9 us
    ppermute x32, waiting for transfers between devices: 312 us -> 150 us  [shifted(): return lax.ppermute(block, axis, route)]
    ppermute x28, starting transfers between devices: 192 us -> 141 us  [summed_over_patch(): held = keep + lax.ppermute(send, 'patch', route)]
    pallas_call x0 -> x2, Pallas kernels: none -> 34.3 us  [hessian_window(): pl.pallas_call(tile_products, grid_spec=grid_spec, out_shape=jax.ShapeDty...]
    scatter-add x8 -> x0, other arithmetic: 32.3 us -> none  [one_turn(): return partial_value.at[rows_here].add(direct).at[cols_here].add(mirror)]
    ppermute x32, starting transfers between devices: 100 us -> 118 us  [shifted(): return lax.ppermute(block, axis, route)]
    gather x8 -> x0, local copies, waits for them, and re-layouts: 17.6 us -> none  [the longest x4 8.82 us: one_turn(): window_x[cols_here]]
    dot_general x8 -> x0, matrix products: 13.9 us -> none  [the longest x4 7.2 us: one_turn(): jnp.einsum('sba,sbk->sak', chosen, window_x[rows_here], preferred_element...]
    another operation x29 -> x30, other arithmetic: 159 us -> 159 us  [shards(): factor = jnp.linalg.cholesky(gram_matrix)]
  transfers between devices with their start and end apart: 92 -> 92, of which waited for: 77 -> 73; matrix products, arithmetic and copies ran while one was open for 2% -> 2% of each run, Pallas kernels for 0% -> 0%
where the time goes in v2:
time: 1130 us; the launch traced here: 1120 us
  waiting for transfers between devices  398 us (35%)
  starting transfers between devices  335 us (30%)
  other arithmetic  255 us (23%)
  local copies, waits for them, and re-layouts  50.4 us (4%)
  Pallas kernels  34.3 us (3%)
  matrix products  25.9 us (2%)
  between operations  21.3 us (2%)
    another operation x30, other arithmetic, shards(): factor = jnp.linalg.cholesky(gram_matrix)  159 us
    ppermute x32, waiting for transfers between devices, shifted(): return lax.ppermute(block, axis, route)  150 us
    ppermute x28, starting transfers between devices, summed_over_patch(): held = keep + lax.ppermute(send, 'patch', route)  141 us
    ppermute x28, waiting for transfers between devices, summed_over_patch(): held = keep + lax.ppermute(send, 'patch', route)  120 us
    ppermute x32, starting transfers between devices, shifted(): return lax.ppermute(block, axis, route)  118 us
    ppermute x28, waiting for transfers between devices, summed_over_patch(): other = lax.ppermute(held, 'patch', route)  97.9 us
    another operation x6, other arithmetic, shards(): lax.linalg.triangular_solve(factor, update_all, left_side=False, lower=Tr...  79.2 us
    ppermute x28, starting transfers between devices, summed_over_patch(): other = lax.ppermute(held, 'patch', route)  75.8 us
  transfers between devices with their start and end apart: 92, of which 73 were waited for; matrix products, arithmetic and copies ran while one was open for 2% of the time, Pallas kernels for 0%

profile of v2, /device:TPU:4, one launch (start us, length us, event | category | flops | bytes accessed | tf_op | source)
XLA Modules:
  0.0 1119.9 jit_solution(3269684252801315879)
XLA Ops:
  61.5 17.1 %shard_map.68 = f32[16,256,256]{2,1,0:T(8,128)} custom-call(s32[64]{0:T(128)} %get-tuple-element.123.rows_ref, s32[64]{0:T(128)} %get-tuple-element.122.cols_ref, s32[1]{0:T(128)S(6)} %copy.206.used_ref, bf16[64,256,256]{2,1,0:T(8,128)(2,1)} %tile_ref.3, bf16[16,256,256]{2,1,0:T(8,128)(2,1)} %bitcast.257), custom_call_target="tpu_custom_call" | custom-call | flops 4294967296 | bytes 14680064 | tf_op jit(solution)/shard_map/pallas_call | solution.py:83
  101.0 15.7 %collective-permute-done.15 = f32[512,256]{0,1:T(8,128)} collective-permute-done((f32[512,256]{0,1:T(8,128)}, f32[512,256]{0,1:T(8,128)}, u32[]{:S(2)}, u32[]{:S(2)}) %collective-permute-start.15) | collective-permute-done | bytes 524320 | tf_op jit(solution)/shard_map/ppermute | solution.py:18
  122.6 45.5 %collective-permute-done.14 = f32[512,256]{0,1:T(8,128)} collective-permute-done((f32[512,256]{0,1:T(8,128)}, f32[512,256]{0,1:T(8,128)}, u32[]{:S(2)}, u32[]{:S(2)}) %collective-permute-start.14) | collective-permute-done | bytes 524320 | tf_op jit(solution)/shard_map/ppermute | solution.py:18
  170.0 17.1 %collective-permute-start.8 = (f32[512,256]{0,1:T(8,128)}, f32[512,256]{0,1:T(8,128)}, u32[]{:S(2)}, u32[]{:S(2)}) collective-permute-start(f32[512,256]{0,1:T(8,128)} %copy.104), channel_id=1, source_target_pairs={{0,2},{2,4},{4,6},{6,8},{8,10},{10,12},{12,14},{14,16},{16,18},{18... | collective-permute-start | bytes 1572872 | tf_op jit(solution)/shard_map/ppermute | solution.py:18
  187.4 9.9 collective-permute-done.8
  211.9 26.9 %collective-permute-start.17 = (f32[128,256]{0,1:T(8,128)S(1)}, f32[128,256]{0,1:T(8,128)S(1)}, u32[]{:S(2)}, u32[]{:S(2)}) collective-permute-start(f32[128,256]{0,1:T(8,128)S(1)} %constant_dynamic-slice_fusion.56), channel_id=1, source_target_pairs={{0,8},{2,10},{4,12},{6,14},{8,0},{10,2},{12,4},{14,6},{16,24},{18,... | collective-permute-start | bytes 393224 | tf_op jit(solution)/shard_map/ppermute | solution.py:32
  247.1 10.8 collective-permute-start.19
  333.2 14.2 %all-gather.7.cloned.1.call-done = f32[512,512]{0,1:T(8,128)} async-done(((f32[512,256]{0,1:T(8,128)}), f32[512,512]{0,1:T(8,128)}) %all-gather.7.cloned.1.call-update) | async-done | bytes 1048592 | tf_op jit(solution)/shard_map/all_gather | solution.py:166
  352.1 13.0 %collective-permute-done.30 = f32[256,512]{1,0:T(8,128)S(1)} collective-permute-done((f32[256,512]{1,0:T(8,128)S(1)}, f32[256,512]{1,0:T(8,128)S(1)}, u32[]{:S(2)}, u32[]{:S(2)}) %collective-permute-start.30) | collective-permute-done | bytes 524320 | tf_op jit(solution)/shard_map/ppermute | solution.py:32
  448.0 11.7 %cholesky.286 = f32[128,128]{1,0:T(8,128)S(1)} custom-call(f32[128,128]{1,0:T(8,128)S(1)} %cholesky.426), custom_call_target="Cholesky" | custom-call | tf_op jit(solution)/shard_map/jit(cholesky)/cholesky | solution.py:173
  459.9 9.8 custom-call.27
  470.4 11.7 %cholesky.305 = f32[128,128]{1,0:T(8,128)S(1)} custom-call(f32[128,128]{1,0:T(8,128)S(1)} %cholesky.430), custom_call_target="Cholesky" | custom-call | tf_op jit(solution)/shard_map/jit(cholesky)/cholesky | solution.py:173
  482.1 9.9 custom-call.28
  492.8 11.7 %cholesky.326 = f32[128,128]{1,0:T(8,128)S(1)} custom-call(f32[128,128]{1,0:T(8,128)S(1)} %cholesky.435), custom_call_target="Cholesky" | custom-call | tf_op jit(solution)/shard_map/jit(cholesky)/cholesky | solution.py:173
  504.5 9.8 custom-call.29
  514.9 11.7 %cholesky.343 = f32[128,128]{1,0:T(8,128)S(1)} custom-call(f32[128,128]{1,0:T(8,128)S(1)} %convolution_subtract_fusion.9), custom_call_target="Cholesky" | custom-call | tf_op jit(solution)/shard_map/jit(cholesky)/cholesky | solution.py:173
  540.2 39.3 %custom-call.30 = f32[4,128,128]{1,2,0:T(8,128)S(1)} custom-call(f32[4,128,128]{2,1,0:T(8,128)S(1)} %get-tuple-element.18), custom_call_target="InvertDiagBlocksLowerTriangular" | custom-call | tf_op jit(solution)/shard_map/triangular_solve/custom-call.3 | solution.py:174
  626.6 17.1 %shard_map.69 = f32[16,256,256]{2,1,0:T(8,128)} custom-call(s32[64]{0:T(128)} %get-tuple-element.123.rows_ref, s32[64]{0:T(128)} %get-tuple-element.122.cols_ref, s32[1]{0:T(128)S(6)} %copy.206.used_ref, bf16[64,256,256]{2,1,0:T(8,128)(2,1)} %tile_ref.3, bf16[16,256,256]{2,1,0:T(8,128)(2,1)} %bitcast.256), custom_call_target="tpu_custom_call" | custom-call | flops 4294967296 | bytes 14680064 | tf_op jit(solution)/shard_map/pallas_call | solution.py:83
  664.8 18.0 %collective-permute-done.59 = f32[512,256]{0,1:T(8,128)} collective-permute-done((f32[512,256]{0,1:T(8,128)}, f32[512,256]{0,1:T(8,128)}, u32[]{:S(2)}, u32[]{:S(2)}) %collective-permute-start.59) | collective-permute-done | bytes 524320 | tf_op jit(solution)/shard_map/ppermute | solution.py:18
  684.8 28.3 %collective-permute-done.58 = f32[512,256]{0,1:T(8,128)} collective-permute-done((f32[512,256]{0,1:T(8,128)}, f32[512,256]{0,1:T(8,128)}, u32[]{:S(2)}, u32[]{:S(2)}) %collective-permute-start.58) | collective-permute-done | bytes 524320 | tf_op jit(solution)/shard_map/ppermute | solution.py:18
  715.0 15.1 %collective-permute-start.52 = (f32[512,256]{0,1:T(8,128)}, f32[512,256]{0,1:T(8,128)}, u32[]{:S(2)}, u32[]{:S(2)}) collective-permute-start(f32[512,256]{0,1:T(8,128)} %copy.123), channel_id=1, source_target_pairs={{0,2},{2,4},{4,6},{6,8},{8,10},{10,12},{12,14},{14,16},{16,18},{18... | collective-permute-start | bytes 1572872 | tf_op jit(solution)/shard_map/ppermute | solution.py:18
  749.9 30.0 %collective-permute-start.61 = (f32[128,256]{1,0:T(8,128)S(1)}, f32[128,256]{1,0:T(8,128)S(1)}, u32[]{:S(2)}, u32[]{:S(2)}) collective-permute-start(f32[128,256]{1,0:T(8,128)S(1)} %constant_dynamic-slice_fusion.35), channel_id=1, source_target_pairs={{0,8},{2,10},{4,12},{6,14},{8,0},{10,2},{12,4},{14,6},{16,24},{18,... | collective-permute-start | bytes 393224 | tf_op jit(solution)/shard_map/ppermute | solution.py:32
  860.8 15.8 %all-gather.11.cloned.1.call-done = f32[512,512]{0,1:T(8,128)} async-done(((f32[512,256]{0,1:T(8,128)}), f32[512,512]{0,1:T(8,128)}) %all-gather.11.cloned.1.call-update) | async-done | bytes 1048592 | tf_op jit(solution)/shard_map/all_gather | solution.py:166
  881.2 13.0 %collective-permute-done.74 = f32[256,512]{1,0:T(8,128)S(1)} collective-permute-done((f32[256,512]{1,0:T(8,128)S(1)}, f32[256,512]{1,0:T(8,128)S(1)}, u32[]{:S(2)}, u32[]{:S(2)}) %collective-permute-start.74) | collective-permute-done | bytes 524320 | tf_op jit(solution)/shard_map/ppermute | solution.py:32
  977.0 11.7 %cholesky.358 = f32[128,128]{1,0:T(8,128)S(1)} custom-call(f32[128,128]{1,0:T(8,128)S(1)} %cholesky.439), custom_call_target="Cholesky" | custom-call | tf_op jit(solution)/shard_map/jit(cholesky)/cholesky | solution.py:173
  988.8 9.8 custom-call.31
  999.3 11.7 %cholesky.377 = f32[128,128]{1,0:T(8,128)S(1)} custom-call(f32[128,128]{1,0:T(8,128)S(1)} %cholesky.443), custom_call_target="Cholesky" | custom-call | tf_op jit(solution)/shard_map/jit(cholesky)/cholesky | solution.py:173
  1011.1 10.2 custom-call.32
  1022.0 11.7 %cholesky.398 = f32[128,128]{1,0:T(8,128)S(1)} custom-call(f32[128,128]{1,0:T(8,128)S(1)} %cholesky.448), custom_call_target="Cholesky" | custom-call | tf_op jit(solution)/shard_map/jit(cholesky)/cholesky | solution.py:173
  1033.7 9.8 custom-call.33
  1044.1 11.9 %cholesky.415 = f32[128,128]{1,0:T(8,128)S(1)} custom-call(f32[128,128]{1,0:T(8,128)S(1)} %convolution_subtract_fusion.8), custom_call_target="Cholesky" | custom-call | tf_op jit(solution)/shard_map/jit(cholesky)/cholesky | solution.py:173
  1069.4 39.3 %custom-call.34 = f32[4,128,128]{1,2,0:T(8,128)S(1)} custom-call(f32[4,128,128]{2,1,0:T(8,128)S(1)} %get-tuple-element.19), custom_call_target="InvertDiagBlocksLowerTriangular" | custom-call | tf_op jit(solution)/shard_map/triangular_solve/custom-call.3 | solution.py:174
  (425 shorter events, 575.2 us)
Async XLA Ops:
  7.2 192.3 %all-gather.5.cloned.1.call-start = ((), (), s32[]{:S(2)}) async-start(), calls=%async_computation | async-start | bytes 1572864 | tf_op jit(solution)/shard_map/all_gather | solution.py:155
  8.5 24.9 %collective-permute-start.7 = (bf16[512,256]{0,1:T(8,128)(2,1)S(1)}, bf16[512,256]{0,1:T(8,128)(2,1)S(1)}, u32[]{:S(2)}, u32[]{:S(2)}) collective-permute-start(bf16[512,256]{0,1:T(8,128)(2,1)S(1)} %convert_element_type.6), channel_id=1, source_target_pairs={{0,14},{2,16},{4,18},{6,20},{8,22},{10,24},{12,26},{14,28},{16,30}... | collective-permute-start | bytes 786440 | tf_op jit(solution)/shard_map/ppermute | solution.py:18
  13.7 24.2 %collective-permute-start = (bf16[512,256]{0,1:T(8,128)(2,1)S(1)}, bf16[512,256]{0,1:T(8,128)(2,1)S(1)}, u32[]{:S(2)}, u32[]{:S(2)}) collective-permute-start(bf16[512,256]{0,1:T(8,128)(2,1)S(1)} %convert_element_type.6), channel_id=1, source_target_pairs={{0,12},{2,14},{4,16},{6,18},{8,20},{10,22},{12,24},{14,26},{16,28}... | collective-permute-start | bytes 786440 | tf_op jit(solution)/shard_map/ppermute | solution.py:18
  19.7 23.0 %collective-permute-start.1 = (bf16[512,256]{0,1:T(8,128)(2,1)S(1)}, bf16[512,256]{0,1:T(8,128)(2,1)S(1)}, u32[]{:S(2)}, u32[]{:S(2)}) collective-permute-start(bf16[512,256]{0,1:T(8,128)(2,1)S(1)} %convert_element_type.6), channel_id=1, source_target_pairs={{0,10},{2,12},{4,14},{6,16},{8,18},{10,20},{12,22},{14,24},{16,26}... | collective-permute-start | bytes 786440 | tf_op jit(solution)/shard_map/ppermute | solution.py:18
  24.5 23.8 %collective-permute-start.2 = (bf16[512,256]{0,1:T(8,128)(2,1)S(1)}, bf16[512,256]{0,1:T(8,128)(2,1)S(1)}, u32[]{:S(2)}, u32[]{:S(2)}) collective-permute-start(bf16[512,256]{0,1:T(8,128)(2,1)S(1)} %convert_element_type.6), channel_id=1, source_target_pairs={{0,8},{2,10},{4,12},{6,14},{8,16},{10,18},{12,20},{14,22},{16,24},... | collective-permute-start | bytes 786440 | tf_op jit(solution)/shard_map/ppermute | solution.py:18
  27.4 26.6 %collective-permute-start.3 = (bf16[512,256]{0,1:T(8,128)(2,1)S(1)}, bf16[512,256]{0,1:T(8,128)(2,1)S(1)}, u32[]{:S(2)}, u32[]{:S(2)}) collective-permute-start(bf16[512,256]{0,1:T(8,128)(2,1)S(1)} %convert_element_type.6), channel_id=1, source_target_pairs={{0,6},{2,8},{4,10},{6,12},{8,14},{10,16},{12,18},{14,20},{16,22},{... | collective-permute-start | bytes 786440 | tf_op jit(solution)/shard_map/ppermute | solution.py:18
  33.4 25.2 %collective-permute-start.4 = (bf16[512,256]{0,1:T(8,128)(2,1)S(1)}, bf16[512,256]{0,1:T(8,128)(2,1)S(1)}, u32[]{:S(2)}, u32[]{:S(2)}) collective-permute-start(bf16[512,256]{0,1:T(8,128)(2,1)S(1)} %convert_element_type.6), channel_id=1, source_target_pairs={{0,4},{2,6},{4,8},{6,10},{8,12},{10,14},{12,16},{14,18},{16,20},{1... | collective-permute-start | bytes 786440 | tf_op jit(solution)/shard_map/ppermute | solution.py:18
  37.8 20.9 %collective-permute-start.5 = (bf16[512,256]{0,1:T(8,128)(2,1)S(1)}, bf16[512,256]{0,1:T(8,128)(2,1)S(1)}, u32[]{:S(2)}, u32[]{:S(2)}) collective-permute-start(bf16[512,256]{0,1:T(8,128)(2,1)S(1)} %convert_element_type.6), channel_id=1, source_target_pairs={{0,2},{2,4},{4,6},{6,8},{8,10},{10,12},{12,14},{14,16},{16,18},{18... | collective-permute-start | bytes 786440 | tf_op jit(solution)/shard_map/ppermute | solution.py:18
  84.3 32.3 %collective-permute-start.15 = (f32[512,256]{0,1:T(8,128)}, f32[512,256]{0,1:T(8,128)}, u32[]{:S(2)}, u32[]{:S(2)}) collective-permute-start(f32[512,256]{0,1:T(8,128)} %copy.112), channel_id=1, source_target_pairs={{14,0},{16,2},{18,4},{20,6},{22,8},{24,10},{26,12},{28,14},{30,16}... | collective-permute-start | bytes 1572872 | tf_op jit(solution)/shard_map/ppermute | solution.py:18
  87.7 80.4 %collective-permute-start.14 = (f32[512,256]{0,1:T(8,128)}, f32[512,256]{0,1:T(8,128)}, u32[]{:S(2)}, u32[]{:S(2)}) collective-permute-start(f32[512,256]{0,1:T(8,128)} %copy.111), channel_id=1, source_target_pairs={{12,0},{14,2},{16,4},{18,6},{20,8},{22,10},{24,12},{26,14},{28,16}... | collective-permute-start | bytes 1572872 | tf_op jit(solution)/shard_map/ppermute | solution.py:18
  91.0 79.0 %collective-permute-start.13 = (f32[512,256]{0,1:T(8,128)}, f32[512,256]{0,1:T(8,128)}, u32[]{:S(2)}, u32[]{:S(2)}) collective-permute-start(f32[512,256]{0,1:T(8,128)} %copy.110), channel_id=1, source_target_pairs={{10,0},{12,2},{14,4},{16,6},{18,8},{20,10},{22,12},{24,14},{26,16}... | collective-permute-start | bytes 1572872 | tf_op jit(solution)/shard_map/ppermute | solution.py:18
  92.3 255.1 %all-gather.7.cloned.1.call-start = ((), (), s32[]{:S(2)}) async-start(), calls=%async_computation.1 | async-start | bytes 1572864 | tf_op jit(solution)/shard_map/all_gather | solution.py:166
  94.4 92.9 %collective-permute-start.12 = (f32[512,256]{0,1:T(8,128)}, f32[512,256]{0,1:T(8,128)}, u32[]{:S(2)}, u32[]{:S(2)}) collective-permute-start(f32[512,256]{0,1:T(8,128)} %copy.109), channel_id=1, source_target_pairs={{8,0},{10,2},{12,4},{14,6},{16,8},{18,10},{20,12},{22,14},{24,16},... | collective-permute-start | bytes 1572872 | tf_op jit(solution)/shard_map/ppermute | solution.py:18
  96.7 90.6 %collective-permute-start.11 = (f32[512,256]{0,1:T(8,128)}, f32[512,256]{0,1:T(8,128)S(1)}, u32[]{:S(2)}, u32[]{:S(2)}) collective-permute-start(f32[512,256]{0,1:T(8,128)} %copy.108), channel_id=1, source_target_pairs={{6,0},{8,2},{10,4},{12,6},{14,8},{16,10},{18,12},{20,14},{22,16},{... | collective-permute-start | bytes 1572872 | tf_op jit(solution)/shard_map/ppermute | solution.py:18
  116.7 70.7 %collective-permute-start.10 = (f32[512,256]{0,1:T(8,128)}, f32[512,256]{0,1:T(8,128)S(1)}, u32[]{:S(2)}, u32[]{:S(2)}) collective-permute-start(f32[512,256]{0,1:T(8,128)} %copy.107), channel_id=1, source_target_pairs={{4,0},{6,2},{8,4},{10,6},{12,8},{14,10},{16,12},{18,14},{20,16},{2... | collective-permute-start | bytes 1572872 | tf_op jit(solution)/shard_map/ppermute | solution.py:18
  168.1 19.3 %collective-permute-start.9 = (f32[512,256]{0,1:T(8,128)}, f32[512,256]{0,1:T(8,128)S(1)}, u32[]{:S(2)}, u32[]{:S(2)}) collective-permute-start(f32[512,256]{0,1:T(8,128)} %copy.106), channel_id=1, source_target_pairs={{2,0},{4,2},{6,4},{8,6},{10,8},{12,10},{14,12},{16,14},{18,16},{20... | collective-permute-start | bytes 1572872 | tf_op jit(solution)/shard_map/ppermute | solution.py:18
  170.0 27.3 %collective-permute-start.8 = (f32[512,256]{0,1:T(8,128)}, f32[512,256]{0,1:T(8,128)}, u32[]{:S(2)}, u32[]{:S(2)}) collective-permute-start(f32[512,256]{0,1:T(8,128)} %copy.104), channel_id=1, source_target_pairs={{0,2},{2,4},{4,6},{6,8},{8,10},{10,12},{12,14},{14,16},{16,18},{18... | collective-permute-start | bytes 1572872 | tf_op jit(solution)/shard_map/ppermute | solution.py:18
  211.9 29.8 %collective-permute-start.17 = (f32[128,256]{0,1:T(8,128)S(1)}, f32[128,256]{0,1:T(8,128)S(1)}, u32[]{:S(2)}, u32[]{:S(2)}) collective-permute-start(f32[128,256]{0,1:T(8,128)S(1)} %constant_dynamic-slice_fusion.56), channel_id=1, source_target_pairs={{0,8},{2,10},{4,12},{6,14},{8,0},{10,2},{12,4},{14,6},{16,24},{18,... | collective-permute-start | bytes 393224 | tf_op jit(solution)/shard_map/ppermute | solution.py:32
  333.1 405.7 %all-gather.9.cloned.1.call-start = ((), (), s32[]{:S(2)}) async-start(), calls=%async_computation.2 | async-start | bytes 1572864 | tf_op jit(solution)/shard_map/all_gather | solution.py:155
  583.9 20.6 %collective-permute-start.51 = (bf16[512,256]{0,1:T(8,128)(2,1)S(1)}, bf16[512,256]{0,1:T(8,128)(2,1)S(1)}, u32[]{:S(2)}, u32[]{:S(2)}) collective-permute-start(bf16[512,256]{0,1:T(8,128)(2,1)S(1)} %get-tuple-element.44), channel_id=1, source_target_pairs={{0,14},{2,16},{4,18},{6,20},{8,22},{10,24},{12,26},{14,28},{16,30}... | collective-permute-start | bytes 786440 | tf_op jit(solution)/shard_map/ppermute | solution.py:18
  588.3 20.4 %collective-permute-start.44 = (bf16[512,256]{0,1:T(8,128)(2,1)S(1)}, bf16[512,256]{0,1:T(8,128)(2,1)S(1)}, u32[]{:S(2)}, u32[]{:S(2)}) collective-permute-start(bf16[512,256]{0,1:T(8,128)(2,1)S(1)} %get-tuple-element.44), channel_id=1, source_target_pairs={{0,12},{2,14},{4,16},{6,18},{8,20},{10,22},{12,24},{14,26},{16,28}... | collective-permute-start | bytes 786440 | tf_op jit(solution)/shard_map/ppermute | solution.py:18
  594.2 16.9 %collective-permute-start.45 = (bf16[512,256]{0,1:T(8,128)(2,1)S(1)}, bf16[512,256]{0,1:T(8,128)(2,1)S(1)}, u32[]{:S(2)}, u32[]{:S(2)}) collective-permute-start(bf16[512,256]{0,1:T(8,128)(2,1)S(1)} %get-tuple-element.44), channel_id=1, source_target_pairs={{0,10},{2,12},{4,14},{6,16},{8,18},{10,20},{12,22},{14,24},{16,26}... | collective-permute-start | bytes 786440 | tf_op jit(solution)/shard_map/ppermute | solution.py:18
  649.2 33.6 %collective-permute-start.59 = (f32[512,256]{0,1:T(8,128)}, f32[512,256]{0,1:T(8,128)}, u32[]{:S(2)}, u32[]{:S(2)}) collective-permute-start(f32[512,256]{0,1:T(8,128)} %copy.131), channel_id=1, source_target_pairs={{14,0},{16,2},{18,4},{20,6},{22,8},{24,10},{26,12},{28,14},{30,16}... | collective-permute-start | bytes 1572872 | tf_op jit(solution)/shard_map/ppermute | solution.py:18
  652.5 60.6 %collective-permute-start.58 = (f32[512,256]{0,1:T(8,128)}, f32[512,256]{0,1:T(8,128)}, u32[]{:S(2)}, u32[]{:S(2)}) collective-permute-start(f32[512,256]{0,1:T(8,128)} %copy.130), channel_id=1, source_target_pairs={{12,0},{14,2},{16,4},{18,6},{20,8},{22,10},{24,12},{26,14},{28,16}... | collective-permute-start | bytes 1572872 | tf_op jit(solution)/shard_map/ppermute | solution.py:18
  655.9 59.1 %collective-permute-start.57 = (f32[512,256]{0,1:T(8,128)}, f32[512,256]{0,1:T(8,128)}, u32[]{:S(2)}, u32[]{:S(2)}) collective-permute-start(f32[512,256]{0,1:T(8,128)} %copy.129), channel_id=1, source_target_pairs={{10,0},{12,2},{14,4},{16,6},{18,8},{20,10},{22,12},{24,14},{26,16}... | collective-permute-start | bytes 1572872 | tf_op jit(solution)/shard_map/ppermute | solution.py:18
  657.2 219.3 %all-gather.11.cloned.1.call-start = ((), (), s32[]{:S(2)}) async-start(), calls=%async_computation.3 | async-start | bytes 1572864 | tf_op jit(solution)/shard_map/all_gather | solution.py:166
  658.2 72.1 %collective-permute-start.56 = (f32[512,256]{0,1:T(8,128)}, f32[512,256]{0,1:T(8,128)S(1)}, u32[]{:S(2)}, u32[]{:S(2)}) collective-permute-start(f32[512,256]{0,1:T(8,128)} %copy.128), channel_id=1, source_target_pairs={{8,0},{10,2},{12,4},{14,6},{16,8},{18,10},{20,12},{22,14},{24,16},... | collective-permute-start | bytes 1572872 | tf_op jit(solution)/shard_map/ppermute | solution.py:18
  660.5 69.8 %collective-permute-start.55 = (f32[512,256]{0,1:T(8,128)}, f32[512,256]{0,1:T(8,128)S(1)}, u32[]{:S(2)}, u32[]{:S(2)}) collective-permute-start(f32[512,256]{0,1:T(8,128)} %copy.127), channel_id=1, source_target_pairs={{6,0},{8,2},{10,4},{12,6},{14,8},{16,10},{18,12},{20,14},{22,16},{... | collective-permute-start | bytes 1572872 | tf_op jit(solution)/shard_map/ppermute | solution.py:18
  682.9 51.5 %collective-permute-start.54 = (f32[512,256]{0,1:T(8,128)}, f32[512,256]{0,1:T(8,128)S(1)}, u32[]{:S(2)}, u32[]{:S(2)}) collective-permute-start(f32[512,256]{0,1:T(8,128)} %copy.126), channel_id=1, source_target_pairs={{4,0},{6,2},{8,4},{10,6},{12,8},{14,10},{16,12},{18,14},{20,16},{2... | collective-permute-start | bytes 1572872 | tf_op jit(solution)/shard_map/ppermute | solution.py:18
  713.1 21.2 %collective-permute-start.53 = (f32[512,256]{0,1:T(8,128)}, f32[512,256]{0,1:T(8,128)S(1)}, u32[]{:S(2)}, u32[]{:S(2)}) collective-permute-start(f32[512,256]{0,1:T(8,128)} %copy.125), channel_id=1, source_target_pairs={{2,0},{4,2},{6,4},{8,6},{10,8},{12,10},{14,12},{16,14},{18,16},{20... | collective-permute-start | bytes 1572872 | tf_op jit(solution)/shard_map/ppermute | solution.py:18
  715.0 21.7 %collective-permute-start.52 = (f32[512,256]{0,1:T(8,128)}, f32[512,256]{0,1:T(8,128)}, u32[]{:S(2)}, u32[]{:S(2)}) collective-permute-start(f32[512,256]{0,1:T(8,128)} %copy.123), channel_id=1, source_target_pairs={{0,2},{2,4},{4,6},{6,8},{8,10},{10,12},{12,14},{14,16},{16,18},{18... | collective-permute-start | bytes 1572872 | tf_op jit(solution)/shard_map/ppermute | solution.py:18
  749.9 33.0 %collective-permute-start.61 = (f32[128,256]{1,0:T(8,128)S(1)}, f32[128,256]{1,0:T(8,128)S(1)}, u32[]{:S(2)}, u32[]{:S(2)}) collective-permute-start(f32[128,256]{1,0:T(8,128)S(1)} %constant_dynamic-slice_fusion.35), channel_id=1, source_target_pairs={{0,8},{2,10},{4,12},{6,14},{8,0},{10,2},{12,4},{14,6},{16,24},{18,... | collective-permute-start | bytes 393224 | tf_op jit(solution)/shard_map/ppermute | solution.py:32
  (65 other events, 940.7 us)
Sparse Core Ops, SparseCore 0:
  92.4 49.7 all-gather.4
  333.2 14.1 all-gather.6
  657.3 44.6 all-gather.8
  860.9 15.5 all-gather.10

commit v3 on v2

--- a/solution.py
+++ b/solution.py
@@ -18,24 +18,29 @@
     return lax.ppermute(block, axis, route)
 
 
-def summed_over_patch(block):
+def summed_over_patch(block, groups=((0, 2), (2, 2), (5, 2), (4, 1))):
     size = lax.axis_size("patch")
     me = lax.axis_index("patch")
-    bits = [b for b in (0, 2, 5, 1, 3, 6, 4) if (1 << b) < size]
     held = block
-    for b in bits:
-        half = held.shape[0] // 2
-        side = (me >> b) & 1
-        keep = lax.dynamic_slice_in_dim(held, side * half, half, 0)
-        send = lax.dynamic_slice_in_dim(held, (1 - side) * half, half, 0)
-        route = [(i, i ^ (1 << b)) for i in range(size)]
-        held = keep + lax.ppermute(send, "patch", route)
-    for b in reversed(bits):
-        side = (me >> b) & 1
-        route = [(i, i ^ (1 << b)) for i in range(size)]
-        other = lax.ppermute(held, "patch", route)
-        both = jnp.stack([held, other, held])
-        held = lax.dynamic_slice_in_dim(both, side, 2, 0).reshape(-1, *held.shape[1:])
+    for low, width in groups:
+        ways = 1 << width
+        part = held.shape[0] // ways
+        digit = (me >> low) & (ways - 1)
+        total = lax.dynamic_slice_in_dim(held, digit * part, part, 0)
+        for e in range(1, ways):
+            route = [(i, i ^ (e << low)) for i in range(size)]
+            send = lax.dynamic_slice_in_dim(held, (digit ^ e) * part, part, 0)
+            total = total + lax.ppermute(send, "patch", route)
+        held = total
+    for low, width in reversed(groups):
+        ways = 1 << width
+        digit = (me >> low) & (ways - 1)
+        pieces = [held]
+        for e in range(1, ways):
+            route = [(i, i ^ (e << low)) for i in range(size)]
+            pieces.append(lax.ppermute(held, "patch", route))
+        order = jnp.arange(ways, dtype=jnp.int32) ^ digit
+        held = jnp.take(jnp.stack(pieces), order, axis=0).reshape(-1, *held.shape[1:])
     return held
 
 

time: 1130 us -> 1060 us (0.938)
  waiting for transfers between devices: 398 us -> 323 us
    ppermute x56 -> x80, waiting for transfers between devices: 218 us -> 156 us  [the longest x40 93.7 us: summed_over_patch(): total = total + lax.ppermute(send, 'patch', route)]
    ppermute x32, starting transfers between devices: 118 us -> 147 us  [shifted(): return lax.ppermute(block, axis, route)]
    ppermute x56 -> x80, starting transfers between devices: 217 us -> 190 us  [the longest x40 125 us: summed_over_patch(): total = total + lax.ppermute(send, 'patch', route)]
  transfers between devices with their start and end apart: 92 -> 116, of which waited for: 73 -> 79; matrix products, arithmetic and copies ran while one was open for 2% -> 3% of each run, Pallas kernels for 0% -> 0%
where the time goes in v3:
time: 1060 us; the launch traced here: 1050 us
  starting transfers between devices  337 us (32%)
  waiting for transfers between devices  323 us (30%)
  other arithmetic  256 us (24%)
  local copies, waits for them, and re-layouts  58.8 us (6%)
  matrix products  26.1 us (2%)
  Pallas kernels  25.3 us (2%)
  between operations  21.7 us (2%)
    another operation x30, other arithmetic, shards(): factor = jnp.linalg.cholesky(gram_matrix)  159 us
    ppermute x32, starting transfers between devices, shifted(): return lax.ppermute(block, axis, route)  147 us
    ppermute x32, waiting for transfers between devices, shifted(): return lax.ppermute(block, axis, route)  143 us
    ppermute x40, starting transfers between devices, summed_over_patch(): total = total + lax.ppermute(send, 'patch', route)  125 us
    ppermute x40, waiting for transfers between devices, summed_over_patch(): total = total + lax.ppermute(send, 'patch', route)  93.7 us
    another operation x6, other arithmetic, shards(): lax.linalg.triangular_solve(factor, update_all, left_side=False, lower=Tr...  79.2 us
    ppermute x40, starting transfers between devices, summed_over_patch(): pieces.append(lax.ppermute(held, 'patch', route))  64.6 us
    ppermute x40, waiting for transfers between devices, summed_over_patch(): pieces.append(lax.ppermute(held, 'patch', route))  62.2 us
  transfers between devices with their start and end apart: 116, of which 79 were waited for; matrix products, arithmetic and copies ran while one was open for 3% of the time, Pallas kernels for 0%

profile of v3, /device:TPU:4, one launch (start us, length us, event | category | flops | bytes accessed | tf_op | source)
XLA Modules:
  0.0 1047.7 jit_solution(18311059405628884593)
XLA Ops:
  61.6 12.7 %shard_map.68 = f32[16,256,256]{2,1,0:T(8,128)} custom-call(s32[64]{0:T(128)} %get-tuple-element.175.rows_ref, s32[64]{0:T(128)} %get-tuple-element.174.cols_ref, s32[1]{0:T(128)S(6)} %copy.168.used_ref, bf16[64,256,256]{2,1,0:T(8,128)(2,1)} %tile_ref.3, bf16[16,256,256]{2,1,0:T(8,128)(2,1)} %bitcast.249), custom_call_target="tpu_custom_call" | custom-call | flops 4294967296 | bytes 14680064 | tf_op jit(solution)/shard_map/pallas_call | solution.py:88
  96.6 20.4 %collective-permute-done.15 = f32[512,256]{0,1:T(8,128)} collective-permute-done((f32[512,256]{0,1:T(8,128)}, f32[512,256]{0,1:T(8,128)}, u32[]{:S(2)}, u32[]{:S(2)}) %collective-permute-start.15) | collective-permute-done | bytes 524320 | tf_op jit(solution)/shard_map/ppermute | solution.py:18
  117.0 14.3 %collective-permute-start.10 = (f32[512,256]{0,1:T(8,128)}, f32[512,256]{0,1:T(8,128)S(1)}, u32[]{:S(2)}, u32[]{:S(2)}) collective-permute-start(f32[512,256]{0,1:T(8,128)} %copy.70), channel_id=1, source_target_pairs={{4,0},{6,2},{8,4},{10,6},{12,8},{14,10},{16,12},{18,14},{20,16},{2... | collective-permute-start | bytes 1572872 | tf_op jit(solution)/shard_map/ppermute | solution.py:18
  131.3 29.0 %collective-permute-done.14 = f32[512,256]{0,1:T(8,128)} collective-permute-done((f32[512,256]{0,1:T(8,128)}, f32[512,256]{0,1:T(8,128)}, u32[]{:S(2)}, u32[]{:S(2)}) %collective-permute-start.14) | collective-permute-done | bytes 524320 | tf_op jit(solution)/shard_map/ppermute | solution.py:18
  162.3 23.5 %collective-permute-start.8 = (f32[512,256]{0,1:T(8,128)}, f32[512,256]{0,1:T(8,128)}, u32[]{:S(2)}, u32[]{:S(2)}) collective-permute-start(f32[512,256]{0,1:T(8,128)} %copy.67), channel_id=1, source_target_pairs={{0,2},{2,4},{4,6},{6,8},{8,10},{10,12},{12,14},{14,16},{16,18},{18... | collective-permute-start | bytes 1572872 | tf_op jit(solution)/shard_map/ppermute | solution.py:18
  209.6 31.7 %collective-permute-start.21 = (f32[32,256]{0,1:T(8,128)S(1)}, f32[32,256]{0,1:T(8,128)S(1)}, u32[]{:S(2)}, u32[]{:S(2)}) collective-permute-start(f32[32,256]{0,1:T(8,128)S(1)} %get-tuple-element.127), channel_id=1, source_target_pairs={{0,24},{2,26},{4,28},{6,30},{8,16},{10,18},{12,20},{14,22},{16,8},... | collective-permute-start | bytes 98312 | tf_op jit(solution)/shard_map/ppermute | solution.py:33
  263.4 10.0 collective-permute-done.25
  311.2 11.7 %all-gather.7.cloned.1.call-done = f32[512,512]{0,1:T(8,128)} async-done(((f32[512,256]{0,1:T(8,128)}), f32[512,512]{0,1:T(8,128)}) %all-gather.7.cloned.1.call-update) | async-done | bytes 1048592 | tf_op jit(solution)/shard_map/all_gather | solution.py:171
  331.0 9.7 collective-permute-done.38
  404.3 11.7 %cholesky.286 = f32[128,128]{1,0:T(8,128)S(1)} custom-call(f32[128,128]{1,0:T(8,128)S(1)} %cholesky.426), custom_call_target="Cholesky" | custom-call | tf_op jit(solution)/shard_map/jit(cholesky)/cholesky | solution.py:178
  416.2 9.8 custom-call.27
  426.7 11.7 %cholesky.305 = f32[128,128]{1,0:T(8,128)S(1)} custom-call(f32[128,128]{1,0:T(8,128)S(1)} %cholesky.430), custom_call_target="Cholesky" | custom-call | tf_op jit(solution)/shard_map/jit(cholesky)/cholesky | solution.py:178
  438.4 10.0 custom-call.28
  449.1 11.7 %cholesky.326 = f32[128,128]{1,0:T(8,128)S(1)} custom-call(f32[128,128]{1,0:T(8,128)S(1)} %cholesky.435), custom_call_target="Cholesky" | custom-call | tf_op jit(solution)/shard_map/jit(cholesky)/cholesky | solution.py:178
  460.9 9.8 custom-call.29
  471.3 11.7 %cholesky.343 = f32[128,128]{1,0:T(8,128)S(1)} custom-call(f32[128,128]{1,0:T(8,128)S(1)} %convolution_subtract_fusion.9), custom_call_target="Cholesky" | custom-call | tf_op jit(solution)/shard_map/jit(cholesky)/cholesky | solution.py:178
  496.4 39.3 %custom-call.30 = f32[4,128,128]{1,2,0:T(8,128)S(1)} custom-call(f32[4,128,128]{2,1,0:T(8,128)S(1)} %get-tuple-element.26), custom_call_target="InvertDiagBlocksLowerTriangular" | custom-call | tf_op jit(solution)/shard_map/triangular_solve/custom-call.3 | solution.py:179
  585.4 12.7 %shard_map.69 = f32[16,256,256]{2,1,0:T(8,128)} custom-call(s32[64]{0:T(128)} %get-tuple-element.175.rows_ref, s32[64]{0:T(128)} %get-tuple-element.174.cols_ref, s32[1]{0:T(128)S(6)} %copy.168.used_ref, bf16[64,256,256]{2,1,0:T(8,128)(2,1)} %tile_ref.3, bf16[16,256,256]{2,1,0:T(8,128)(2,1)} %bitcast.248), custom_call_target="tpu_custom_call" | custom-call | flops 4294967296 | bytes 14680064 | tf_op jit(solution)/shard_map/pallas_call | solution.py:88
  619.2 24.9 %collective-permute-done.71 = f32[512,256]{0,1:T(8,128)} collective-permute-done((f32[512,256]{0,1:T(8,128)}, f32[512,256]{0,1:T(8,128)}, u32[]{:S(2)}, u32[]{:S(2)}) %collective-permute-start.71) | collective-permute-done | bytes 524320 | tf_op jit(solution)/shard_map/ppermute | solution.py:18
  651.9 23.5 %collective-permute-done.70 = f32[512,256]{0,1:T(8,128)} collective-permute-done((f32[512,256]{0,1:T(8,128)}, f32[512,256]{0,1:T(8,128)}, u32[]{:S(2)}, u32[]{:S(2)}) %collective-permute-start.70) | collective-permute-done | bytes 524320 | tf_op jit(solution)/shard_map/ppermute | solution.py:18
  677.3 24.9 %collective-permute-start.64 = (f32[512,256]{0,1:T(8,128)}, f32[512,256]{0,1:T(8,128)}, u32[]{:S(2)}, u32[]{:S(2)}) collective-permute-start(f32[512,256]{0,1:T(8,128)} %copy.85), channel_id=1, source_target_pairs={{0,2},{2,4},{4,6},{6,8},{8,10},{10,12},{12,14},{14,16},{16,18},{18... | collective-permute-start | bytes 1572872 | tf_op jit(solution)/shard_map/ppermute | solution.py:18
  723.2 25.9 %collective-permute-start.77 = (f32[32,256]{1,0:T(8,128)S(1)}, f32[32,256]{1,0:T(8,128)S(1)}, u32[]{:S(2)}, u32[]{:S(2)}) collective-permute-start(f32[32,256]{1,0:T(8,128)S(1)} %get-tuple-element.121), channel_id=1, source_target_pairs={{0,24},{2,26},{4,28},{6,30},{8,16},{10,18},{12,20},{14,22},{16,8},... | collective-permute-start | bytes 98312 | tf_op jit(solution)/shard_map/ppermute | solution.py:33
  811.6 12.0 %all-gather.11.cloned.1.call-done = f32[512,512]{0,1:T(8,128)} async-done(((f32[512,256]{0,1:T(8,128)}), f32[512,512]{0,1:T(8,128)}) %all-gather.11.cloned.1.call-update) | async-done | bytes 1048592 | tf_op jit(solution)/shard_map/all_gather | solution.py:171
  831.3 10.0 collective-permute-done.94
  905.0 11.7 %cholesky.358 = f32[128,128]{1,0:T(8,128)S(1)} custom-call(f32[128,128]{1,0:T(8,128)S(1)} %cholesky.439), custom_call_target="Cholesky" | custom-call | tf_op jit(solution)/shard_map/jit(cholesky)/cholesky | solution.py:178
  916.9 9.8 custom-call.31
  927.4 11.7 %cholesky.377 = f32[128,128]{1,0:T(8,128)S(1)} custom-call(f32[128,128]{1,0:T(8,128)S(1)} %cholesky.443), custom_call_target="Cholesky" | custom-call | tf_op jit(solution)/shard_map/jit(cholesky)/cholesky | solution.py:178
  939.1 10.0 custom-call.32
  949.8 11.7 %cholesky.398 = f32[128,128]{1,0:T(8,128)S(1)} custom-call(f32[128,128]{1,0:T(8,128)S(1)} %cholesky.448), custom_call_target="Cholesky" | custom-call | tf_op jit(solution)/shard_map/jit(cholesky)/cholesky | solution.py:178
  961.6 9.8 custom-call.33
  972.0 11.9 %cholesky.415 = f32[128,128]{1,0:T(8,128)S(1)} custom-call(f32[128,128]{1,0:T(8,128)S(1)} %convolution_subtract_fusion.8), custom_call_target="Cholesky" | custom-call | tf_op jit(solution)/shard_map/jit(cholesky)/cholesky | solution.py:178
  996.9 39.3 %custom-call.34 = f32[4,128,128]{1,2,0:T(8,128)S(1)} custom-call(f32[4,128,128]{2,1,0:T(8,128)S(1)} %get-tuple-element.27), custom_call_target="InvertDiagBlocksLowerTriangular" | custom-call | tf_op jit(solution)/shard_map/triangular_solve/custom-call.3 | solution.py:179
  (476 shorter events, 512.6 us)
Async XLA Ops:
  7.2 190.3 %all-gather.5.cloned.1.call-start = ((), (), s32[]{:S(2)}) async-start(), calls=%async_computation | async-start | bytes 1572864 | tf_op jit(solution)/shard_map/all_gather | solution.py:160
  8.5 24.9 %collective-permute-start.7 = (bf16[512,256]{0,1:T(8,128)(2,1)S(1)}, bf16[512,256]{0,1:T(8,128)(2,1)S(1)}, u32[]{:S(2)}, u32[]{:S(2)}) collective-permute-start(bf16[512,256]{0,1:T(8,128)(2,1)S(1)} %convert_element_type.6), channel_id=1, source_target_pairs={{0,14},{2,16},{4,18},{6,20},{8,22},{10,24},{12,26},{14,28},{16,30}... | collective-permute-start | bytes 786440 | tf_op jit(solution)/shard_map/ppermute | solution.py:18
  13.7 24.1 %collective-permute-start = (bf16[512,256]{0,1:T(8,128)(2,1)S(1)}, bf16[512,256]{0,1:T(8,128)(2,1)S(1)}, u32[]{:S(2)}, u32[]{:S(2)}) collective-permute-start(bf16[512,256]{0,1:T(8,128)(2,1)S(1)} %convert_element_type.6), channel_id=1, source_target_pairs={{0,12},{2,14},{4,16},{6,18},{8,20},{10,22},{12,24},{14,26},{16,28}... | collective-permute-start | bytes 786440 | tf_op jit(solution)/shard_map/ppermute | solution.py:18
  19.7 23.0 %collective-permute-start.1 = (bf16[512,256]{0,1:T(8,128)(2,1)S(1)}, bf16[512,256]{0,1:T(8,128)(2,1)S(1)}, u32[]{:S(2)}, u32[]{:S(2)}) collective-permute-start(bf16[512,256]{0,1:T(8,128)(2,1)S(1)} %convert_element_type.6), channel_id=1, source_target_pairs={{0,10},{2,12},{4,14},{6,16},{8,18},{10,20},{12,22},{14,24},{16,26}... | collective-permute-start | bytes 786440 | tf_op jit(solution)/shard_map/ppermute | solution.py:18
  24.5 23.8 %collective-permute-start.2 = (bf16[512,256]{0,1:T(8,128)(2,1)S(1)}, bf16[512,256]{0,1:T(8,128)(2,1)S(1)}, u32[]{:S(2)}, u32[]{:S(2)}) collective-permute-start(bf16[512,256]{0,1:T(8,128)(2,1)S(1)} %convert_element_type.6), channel_id=1, source_target_pairs={{0,8},{2,10},{4,12},{6,14},{8,16},{10,18},{12,20},{14,22},{16,24},... | collective-permute-start | bytes 786440 | tf_op jit(solution)/shard_map/ppermute | solution.py:18
  27.4 26.6 %collective-permute-start.3 = (bf16[512,256]{0,1:T(8,128)(2,1)S(1)}, bf16[512,256]{0,1:T(8,128)(2,1)S(1)}, u32[]{:S(2)}, u32[]{:S(2)}) collective-permute-start(bf16[512,256]{0,1:T(8,128)(2,1)S(1)} %convert_element_type.6), channel_id=1, source_target_pairs={{0,6},{2,8},{4,10},{6,12},{8,14},{10,16},{12,18},{14,20},{16,22},{... | collective-permute-start | bytes 786440 | tf_op jit(solution)/shard_map/ppermute | solution.py:18
  33.4 25.2 %collective-permute-start.4 = (bf16[512,256]{0,1:T(8,128)(2,1)S(1)}, bf16[512,256]{0,1:T(8,128)(2,1)S(1)}, u32[]{:S(2)}, u32[]{:S(2)}) collective-permute-start(bf16[512,256]{0,1:T(8,128)(2,1)S(1)} %convert_element_type.6), channel_id=1, source_target_pairs={{0,4},{2,6},{4,8},{6,10},{8,12},{10,14},{12,16},{14,18},{16,20},{1... | collective-permute-start | bytes 786440 | tf_op jit(solution)/shard_map/ppermute | solution.py:18
  37.8 20.9 %collective-permute-start.5 = (bf16[512,256]{0,1:T(8,128)(2,1)S(1)}, bf16[512,256]{0,1:T(8,128)(2,1)S(1)}, u32[]{:S(2)}, u32[]{:S(2)}) collective-permute-start(bf16[512,256]{0,1:T(8,128)(2,1)S(1)} %convert_element_type.6), channel_id=1, source_target_pairs={{0,2},{2,4},{4,6},{6,8},{8,10},{10,12},{12,14},{14,16},{16,18},{18... | collective-permute-start | bytes 786440 | tf_op jit(solution)/shard_map/ppermute | solution.py:18
  79.9 37.1 %collective-permute-start.15 = (f32[512,256]{0,1:T(8,128)}, f32[512,256]{0,1:T(8,128)}, u32[]{:S(2)}, u32[]{:S(2)}) collective-permute-start(f32[512,256]{0,1:T(8,128)} %copy.75), channel_id=1, source_target_pairs={{14,0},{16,2},{18,4},{20,6},{22,8},{24,10},{26,12},{28,14},{30,16}... | collective-permute-start | bytes 1572872 | tf_op jit(solution)/shard_map/ppermute | solution.py:18
  83.2 77.1 %collective-permute-start.14 = (f32[512,256]{0,1:T(8,128)}, f32[512,256]{0,1:T(8,128)}, u32[]{:S(2)}, u32[]{:S(2)}) collective-permute-start(f32[512,256]{0,1:T(8,128)} %copy.74), channel_id=1, source_target_pairs={{12,0},{14,2},{16,4},{18,6},{20,8},{22,10},{24,12},{26,14},{28,16}... | collective-permute-start | bytes 1572872 | tf_op jit(solution)/shard_map/ppermute | solution.py:18
  86.6 75.7 %collective-permute-start.13 = (f32[512,256]{0,1:T(8,128)}, f32[512,256]{0,1:T(8,128)}, u32[]{:S(2)}, u32[]{:S(2)}) collective-permute-start(f32[512,256]{0,1:T(8,128)} %copy.73), channel_id=1, source_target_pairs={{10,0},{12,2},{14,4},{16,6},{18,8},{20,10},{22,12},{24,14},{26,16}... | collective-permute-start | bytes 1572872 | tf_op jit(solution)/shard_map/ppermute | solution.py:18
  87.9 235.0 %all-gather.7.cloned.1.call-start = ((), (), s32[]{:S(2)}) async-start(), calls=%async_computation.1 | async-start | bytes 1572864 | tf_op jit(solution)/shard_map/all_gather | solution.py:171
  90.0 96.0 %collective-permute-start.12 = (f32[512,256]{0,1:T(8,128)}, f32[512,256]{0,1:T(8,128)}, u32[]{:S(2)}, u32[]{:S(2)}) collective-permute-start(f32[512,256]{0,1:T(8,128)} %copy.72), channel_id=1, source_target_pairs={{8,0},{10,2},{12,4},{14,6},{16,8},{18,10},{20,12},{22,14},{24,16},... | collective-permute-start | bytes 1572872 | tf_op jit(solution)/shard_map/ppermute | solution.py:18
  92.2 93.8 %collective-permute-start.11 = (f32[512,256]{0,1:T(8,128)}, f32[512,256]{0,1:T(8,128)S(1)}, u32[]{:S(2)}, u32[]{:S(2)}) collective-permute-start(f32[512,256]{0,1:T(8,128)} %copy.71), channel_id=1, source_target_pairs={{6,0},{8,2},{10,4},{12,6},{14,8},{16,10},{18,12},{20,14},{22,16},{... | collective-permute-start | bytes 1572872 | tf_op jit(solution)/shard_map/ppermute | solution.py:18
  117.0 69.0 %collective-permute-start.10 = (f32[512,256]{0,1:T(8,128)}, f32[512,256]{0,1:T(8,128)S(1)}, u32[]{:S(2)}, u32[]{:S(2)}) collective-permute-start(f32[512,256]{0,1:T(8,128)} %copy.70), channel_id=1, source_target_pairs={{4,0},{6,2},{8,4},{10,6},{12,8},{14,10},{16,12},{18,14},{20,16},{2... | collective-permute-start | bytes 1572872 | tf_op jit(solution)/shard_map/ppermute | solution.py:18
  160.4 25.7 %collective-permute-start.9 = (f32[512,256]{0,1:T(8,128)}, f32[512,256]{0,1:T(8,128)S(1)}, u32[]{:S(2)}, u32[]{:S(2)}) collective-permute-start(f32[512,256]{0,1:T(8,128)} %copy.69), channel_id=1, source_target_pairs={{2,0},{4,2},{6,4},{8,6},{10,8},{12,10},{14,12},{16,14},{18,16},{20... | collective-permute-start | bytes 1572872 | tf_op jit(solution)/shard_map/ppermute | solution.py:18
  162.3 32.9 %collective-permute-start.8 = (f32[512,256]{0,1:T(8,128)}, f32[512,256]{0,1:T(8,128)}, u32[]{:S(2)}, u32[]{:S(2)}) collective-permute-start(f32[512,256]{0,1:T(8,128)} %copy.67), channel_id=1, source_target_pairs={{0,2},{2,4},{4,6},{6,8},{8,10},{10,12},{12,14},{14,16},{16,18},{18... | collective-permute-start | bytes 1572872 | tf_op jit(solution)/shard_map/ppermute | solution.py:18
  209.6 35.7 %collective-permute-start.21 = (f32[32,256]{0,1:T(8,128)S(1)}, f32[32,256]{0,1:T(8,128)S(1)}, u32[]{:S(2)}, u32[]{:S(2)}) collective-permute-start(f32[32,256]{0,1:T(8,128)S(1)} %get-tuple-element.127), channel_id=1, source_target_pairs={{0,24},{2,26},{4,28},{6,30},{8,16},{10,18},{12,20},{14,22},{16,8},... | collective-permute-start | bytes 98312 | tf_op jit(solution)/shard_map/ppermute | solution.py:33
  311.2 400.0 %all-gather.9.cloned.1.call-start = ((), (), s32[]{:S(2)}) async-start(), calls=%async_computation.2 | async-start | bytes 1572864 | tf_op jit(solution)/shard_map/all_gather | solution.py:160
  543.9 20.9 %collective-permute-start.56 = (bf16[512,256]{0,1:T(8,128)(2,1)S(1)}, bf16[512,256]{0,1:T(8,128)(2,1)S(1)}, u32[]{:S(2)}, u32[]{:S(2)}) collective-permute-start(bf16[512,256]{0,1:T(8,128)(2,1)S(1)} %get-tuple-element.50), channel_id=1, source_target_pairs={{0,12},{2,14},{4,16},{6,18},{8,20},{10,22},{12,24},{14,26},{16,28}... | collective-permute-start | bytes 786440 | tf_op jit(solution)/shard_map/ppermute | solution.py:18
  553.9 20.7 %collective-permute-start.58 = (bf16[512,256]{0,1:T(8,128)(2,1)S(1)}, bf16[512,256]{0,1:T(8,128)(2,1)S(1)}, u32[]{:S(2)}, u32[]{:S(2)}) collective-permute-start(bf16[512,256]{0,1:T(8,128)(2,1)S(1)} %get-tuple-element.50), channel_id=1, source_target_pairs={{0,8},{2,10},{4,12},{6,14},{8,16},{10,18},{12,20},{14,22},{16,24},... | collective-permute-start | bytes 786440 | tf_op jit(solution)/shard_map/ppermute | solution.py:18
  556.2 21.2 %collective-permute-start.59 = (bf16[512,256]{0,1:T(8,128)(2,1)S(1)}, bf16[512,256]{0,1:T(8,128)(2,1)S(1)}, u32[]{:S(2)}, u32[]{:S(2)}) collective-permute-start(bf16[512,256]{0,1:T(8,128)(2,1)S(1)} %get-tuple-element.50), channel_id=1, source_target_pairs={{0,6},{2,8},{4,10},{6,12},{8,14},{10,16},{12,18},{14,20},{16,22},{... | collective-permute-start | bytes 786440 | tf_op jit(solution)/shard_map/ppermute | solution.py:18
  603.5 40.6 %collective-permute-start.71 = (f32[512,256]{0,1:T(8,128)}, f32[512,256]{0,1:T(8,128)}, u32[]{:S(2)}, u32[]{:S(2)}) collective-permute-start(f32[512,256]{0,1:T(8,128)} %copy.93), channel_id=1, source_target_pairs={{14,0},{16,2},{18,4},{20,6},{22,8},{24,10},{26,12},{28,14},{30,16}... | collective-permute-start | bytes 1572872 | tf_op jit(solution)/shard_map/ppermute | solution.py:18
  606.8 68.6 %collective-permute-start.70 = (f32[512,256]{0,1:T(8,128)}, f32[512,256]{0,1:T(8,128)}, u32[]{:S(2)}, u32[]{:S(2)}) collective-permute-start(f32[512,256]{0,1:T(8,128)} %copy.92), channel_id=1, source_target_pairs={{12,0},{14,2},{16,4},{18,6},{20,8},{22,10},{24,12},{26,14},{28,16}... | collective-permute-start | bytes 1572872 | tf_op jit(solution)/shard_map/ppermute | solution.py:18
  610.2 67.1 %collective-permute-start.69 = (f32[512,256]{0,1:T(8,128)}, f32[512,256]{0,1:T(8,128)}, u32[]{:S(2)}, u32[]{:S(2)}) collective-permute-start(f32[512,256]{0,1:T(8,128)} %copy.91), channel_id=1, source_target_pairs={{10,0},{12,2},{14,4},{16,6},{18,8},{20,10},{22,12},{24,14},{26,16}... | collective-permute-start | bytes 1572872 | tf_op jit(solution)/shard_map/ppermute | solution.py:18
  611.5 212.1 %all-gather.11.cloned.1.call-start = ((), (), s32[]{:S(2)}) async-start(), calls=%async_computation.3 | async-start | bytes 1572864 | tf_op jit(solution)/shard_map/all_gather | solution.py:171
  612.5 89.9 %collective-permute-start.68 = (f32[512,256]{0,1:T(8,128)}, f32[512,256]{0,1:T(8,128)S(1)}, u32[]{:S(2)}, u32[]{:S(2)}) collective-permute-start(f32[512,256]{0,1:T(8,128)} %copy.90), channel_id=1, source_target_pairs={{8,0},{10,2},{12,4},{14,6},{16,8},{18,10},{20,12},{22,14},{24,16},... | collective-permute-start | bytes 1572872 | tf_op jit(solution)/shard_map/ppermute | solution.py:18
  614.8 87.7 %collective-permute-start.67 = (f32[512,256]{0,1:T(8,128)}, f32[512,256]{0,1:T(8,128)S(1)}, u32[]{:S(2)}, u32[]{:S(2)}) collective-permute-start(f32[512,256]{0,1:T(8,128)} %copy.89), channel_id=1, source_target_pairs={{6,0},{8,2},{10,4},{12,6},{14,8},{16,10},{18,12},{20,14},{22,16},{... | collective-permute-start | bytes 1572872 | tf_op jit(solution)/shard_map/ppermute | solution.py:18
  644.1 58.4 %collective-permute-start.66 = (f32[512,256]{0,1:T(8,128)}, f32[512,256]{0,1:T(8,128)S(1)}, u32[]{:S(2)}, u32[]{:S(2)}) collective-permute-start(f32[512,256]{0,1:T(8,128)} %copy.88), channel_id=1, source_target_pairs={{4,0},{6,2},{8,4},{10,6},{12,8},{14,10},{16,12},{18,14},{20,16},{2... | collective-permute-start | bytes 1572872 | tf_op jit(solution)/shard_map/ppermute | solution.py:18
  675.4 27.1 %collective-permute-start.65 = (f32[512,256]{0,1:T(8,128)}, f32[512,256]{0,1:T(8,128)S(1)}, u32[]{:S(2)}, u32[]{:S(2)}) collective-permute-start(f32[512,256]{0,1:T(8,128)} %copy.87), channel_id=1, source_target_pairs={{2,0},{4,2},{6,4},{8,6},{10,8},{12,10},{14,12},{16,14},{18,16},{20... | collective-permute-start | bytes 1572872 | tf_op jit(solution)/shard_map/ppermute | solution.py:18
  677.3 31.8 %collective-permute-start.64 = (f32[512,256]{0,1:T(8,128)}, f32[512,256]{0,1:T(8,128)}, u32[]{:S(2)}, u32[]{:S(2)}) collective-permute-start(f32[512,256]{0,1:T(8,128)} %copy.85), channel_id=1, source_target_pairs={{0,2},{2,4},{4,6},{6,8},{8,10},{10,12},{12,14},{14,16},{16,18},{18... | collective-permute-start | bytes 1572872 | tf_op jit(solution)/shard_map/ppermute | solution.py:18
  723.2 31.4 %collective-permute-start.77 = (f32[32,256]{1,0:T(8,128)S(1)}, f32[32,256]{1,0:T(8,128)S(1)}, u32[]{:S(2)}, u32[]{:S(2)}) collective-permute-start(f32[32,256]{1,0:T(8,128)S(1)} %get-tuple-element.121), channel_id=1, source_target_pairs={{0,24},{2,26},{4,28},{6,30},{8,16},{10,18},{12,20},{14,22},{16,8},... | collective-permute-start | bytes 98312 | tf_op jit(solution)/shard_map/ppermute | solution.py:33
  (89 other events, 868.1 us)
Sparse Core Ops, SparseCore 0:
  88.0 55.8 all-gather.4
  311.3 11.5 all-gather.6
  611.6 51.7 all-gather.8
  811.8 11.7 all-gather.10

commit v4 on v2

--- a/solution.py
+++ b/solution.py
@@ -1,3 +1,5 @@
+import functools
+
 import jax
 import jax.numpy as jnp
 from jax import lax
@@ -18,25 +20,83 @@
     return lax.ppermute(block, axis, route)
 
 
-def summed_over_patch(block):
+ORDER = (0, 2, 5, 1, 3, 6, 4)
+
+def exchange_sum(size, x_ref, out_ref, work_ref, recv_ref, final_ref, send_sems, recv_sems):
+    me = lax.axis_index("patch")
+    bits = [b for b in ORDER if (1 << b) < size]
+    mesh_ids = pl.DeviceIdType.MESH
+
+    def partner_of(b):
+        side = (me // (1 << b)) % 2
+        return side, me + (1 - 2 * side) * (1 << b)
+
+    barrier = pltpu.get_barrier_semaphore()
+    for b in bits:
+        _, partner = partner_of(b)
+        pl.semaphore_signal(barrier, 1, device_id={"patch": partner}, device_id_type=mesh_ids)
+    pl.semaphore_wait(barrier, len(bits))
+    work_ref[...] = x_ref[...]
+    lo = 0
+    span = work_ref.shape[0]
+    recv_at = 0
+    for k, b in enumerate(bits):
+        span = span // 2
+        side, partner = partner_of(b)
+        keep = lo + side * span
+        send = lo + (1 - side) * span
+        copy = pltpu.make_async_remote_copy(
+            src_ref=work_ref.at[pl.ds(send, span)],
+            dst_ref=recv_ref.at[pl.ds(recv_at, span)],
+            send_sem=send_sems.at[k],
+            recv_sem=recv_sems.at[k],
+            device_id={"patch": partner},
+            device_id_type=mesh_ids,
+        )
+        copy.start()
+        copy.wait()
+        work_ref[pl.ds(keep, span)] = work_ref[pl.ds(keep, span)] + recv_ref[pl.ds(recv_at, span)]
+        lo = keep
+        recv_at += span
+    final_ref[pl.ds(lo, span)] = work_ref[pl.ds(lo, span)]
+    for j, b in enumerate(reversed(bits)):
+        side, partner = partner_of(b)
+        copy = pltpu.make_async_remote_copy(
+            src_ref=final_ref.at[pl.ds(lo, span)],
+            dst_ref=final_ref.at[pl.ds(lo, span)],
+            send_sem=send_sems.at[len(bits) + j],
+            recv_sem=recv_sems.at[len(bits) + j],
+            device_id={"patch": partner},
+            device_id_type=mesh_ids,
+        )
+        copy.start()
+        copy.wait()
+        lo = lo - side * span
+        span = span * 2
+    out_ref[...] = final_ref[...]
+
+
+def summed_over_patch(block, collective):
     size = lax.axis_size("patch")
-    me = lax.axis_index("patch")
-    bits = [b for b in (0, 2, 5, 1, 3, 6, 4) if (1 << b) < size]
-    held = block
-    for b in bits:
-        half = held.shape[0] // 2
-        side = (me >> b) & 1
-        keep = lax.dynamic_slice_in_dim(held, side * half, half, 0)
-        send = lax.dynamic_slice_in_dim(held, (1 - side) * half, half, 0)
-        route = [(i, i ^ (1 << b)) for i in range(size)]
-        held = keep + lax.ppermute(send, "patch", route)
-    for b in reversed(bits):
-        side = (me >> b) & 1
-        route = [(i, i ^ (1 << b)) for i in range(size)]
-        other = lax.ppermute(held, "patch", route)
-        both = jnp.stack([held, other, held])
-        held = lax.dynamic_slice_in_dim(both, side, 2, 0).reshape(-1, *held.shape[1:])
-    return held
+    rows, cols = block.shape
+    lead = size
+    flat = block.reshape(lead, (rows * cols) // (lead * 128), 128)
+    steps = 2 * len([b for b in ORDER if (1 << b) < size])
+    out = pl.pallas_call(
+        functools.partial(exchange_sum, size),
+        out_shape=jax.ShapeDtypeStruct(flat.shape, flat.dtype),
+        in_specs=[pl.BlockSpec(memory_space=pltpu.VMEM)],
+        out_specs=pl.BlockSpec(memory_space=pltpu.VMEM),
+        scratch_shapes=[
+            pltpu.VMEM(flat.shape, flat.dtype),
+            pltpu.VMEM(flat.shape, flat.dtype),
+            pltpu.VMEM(flat.shape, flat.dtype),
+            pltpu.SemaphoreType.DMA((steps,)),
+            pltpu.SemaphoreType.DMA((steps,)),
+        ],
+        compiler_params=pltpu.CompilerParams(collective_id=collective, has_side_effects=True),
+    )(flat)
+    return out.reshape(rows, cols)
 
 
 def tile_products(rows_ref, cols_ref, used_ref, tile_ref, x_ref, out_ref):
@@ -157,7 +217,8 @@
             jnp.dot(
                 current_all.T, applied, precision=exact_mode, preferred_element_type=jnp.float32
             )
-            / total_rows
+            / total_rows,
+            0,
         )
         residual = applied - jnp.dot(
             current_all, rayleigh, precision=exact_mode, preferred_element_type=jnp.float32
@@ -168,7 +229,8 @@
             jnp.dot(
                 update_all.T, update_all, precision=exact_mode, preferred_element_type=jnp.float32
             )
-            / total_rows
+            / total_rows,
+            1,
         )
         factor = jnp.linalg.cholesky(gram_matrix)
         solved = lax.linalg.triangular_solve(

time: 1130 us -> 1080 us (0.956)
  Pallas kernels: 34.3 us -> 402 us
  starting transfers between devices: 335 us -> 104 us
  waiting for transfers between devices: 398 us -> 182 us
  local copies, waits for them, and re-layouts: 50.4 us -> 68.5 us
  matrix products: 25.9 us -> 38.6 us
    pallas_call x0 -> x4, Pallas kernels: none -> 379 us  [summed_over_patch(): pl.pallas_call(functools.partial(exchange_sum, size), out_shape=jax.Shape...]
    ppermute x56 -> x0, waiting for transfers between devices: 218 us -> none  [the longest x28 120 us: summed_over_patch(): held = keep + lax.ppermute(send, 'patch', route)]
    ppermute x56 -> x0, starting transfers between devices: 217 us -> none  [the longest x28 141 us: summed_over_patch(): held = keep + lax.ppermute(send, 'patch', route)]
    ppermute x32, starting transfers between devices: 118 us -> 104 us  [shifted(): return lax.ppermute(block, axis, route)]
  transfers between devices with their start and end apart: 92 -> 36, of which waited for: 73 -> 21; matrix products, arithmetic and copies ran while one was open for 2% -> 3% of each run, Pallas kernels for 0% -> 0%
where the time goes in v4:
time: 1080 us; the launch traced here: 1070 us
  Pallas kernels  402 us (37%)
  other arithmetic  255 us (24%)
  waiting for transfers between devices  182 us (17%)
  starting transfers between devices  104 us (10%)
  local copies, waits for them, and re-layouts  68.5 us (6%)
  matrix products  38.6 us (4%)
  between operations  21 us (2%)
    pallas_call x4, Pallas kernels, summed_over_patch(): pl.pallas_call(functools.partial(exchange_sum, size), out_shape=jax.Shape...  379 us
    another operation x30, other arithmetic, shards(): factor = jnp.linalg.cholesky(gram_matrix)  159 us
    ppermute x32, waiting for transfers between devices, shifted(): return lax.ppermute(block, axis, route)  153 us
    ppermute x32, starting transfers between devices, shifted(): return lax.ppermute(block, axis, route)  104 us
    another operation x6, other arithmetic, shards(): lax.linalg.triangular_solve(factor, update_all, left_side=False, lower=Tr...  81.1 us
    all_gather x2, waiting for transfers between devices, shards(): update_all = lax.all_gather(update, 'vec', axis=1, tiled=True)  28.8 us
    another operation x27, local copies, waits for them, and re-layouts, shards(): lax.linalg.triangular_solve(factor, update_all, left_side=False, lower=Tr...  24 us
    select_n x16, local copies, waits for them, and re-layouts, shards(): outgoing = jnp.where(parity == 0, lower_seg, upper_seg)  23.4 us
  transfers between devices with their start and end apart: 36, of which 21 were waited for; matrix products, arithmetic and copies ran while one was open for 3% of the time, Pallas kernels for 0%

profile of v4, /device:TPU:4, one launch (start us, length us, event | category | flops | bytes accessed | tf_op | source)
XLA Modules:
  0.0 1071.6 jit_solution(14143198729985478827)
XLA Ops:
  61.5 11.5 %shard_map.68 = f32[16,256,256]{2,1,0:T(8,128)} custom-call(s32[64]{0:T(128)} %get-tuple-element.119.rows_ref, s32[64]{0:T(128)} %get-tuple-element.118.cols_ref, s32[1]{0:T(128)S(6)} %copy.121.used_ref, bf16[64,256,256]{2,1,0:T(8,128)(2,1)} %tile_ref.3, bf16[16,256,256]{2,1,0:T(8,128)(2,1)} %bitcast.162), custom_call_target="tpu_custom_call" | custom-call | flops 4294967296 | bytes 14680064 | tf_op jit(solution)/shard_map/pallas_call | solution.py:143
  95.4 21.8 %collective-permute-done.15 = f32[512,256]{0,1:T(8,128)} collective-permute-done((f32[512,256]{0,1:T(8,128)}, f32[512,256]{0,1:T(8,128)}, u32[]{:S(2)}, u32[]{:S(2)}) %collective-permute-start.15) | collective-permute-done | bytes 524320 | tf_op jit(solution)/shard_map/ppermute | solution.py:20
  119.1 28.9 %collective-permute-done.14 = f32[512,256]{0,1:T(8,128)} collective-permute-done((f32[512,256]{0,1:T(8,128)}, f32[512,256]{0,1:T(8,128)}, u32[]{:S(2)}, u32[]{:S(2)}) %collective-permute-start.14) | collective-permute-done | bytes 524320 | tf_op jit(solution)/shard_map/ppermute | solution.py:20
  150.0 12.4 %collective-permute-start.8 = (f32[512,256]{0,1:T(8,128)}, f32[512,256]{0,1:T(8,128)}, u32[]{:S(2)}, u32[]{:S(2)}) collective-permute-start(f32[512,256]{0,1:T(8,128)} %copy.37), channel_id=1, source_target_pairs={{0,2},{2,4},{4,6},{6,8},{8,10},{10,12},{12,14},{14,16},{16,18},{18... | collective-permute-start | bytes 1572872 | tf_op jit(solution)/shard_map/ppermute | solution.py:20
  167.7 12.5 %collective-permute-done.8 = f32[512,256]{0,1:T(8,128)} collective-permute-done((f32[512,256]{0,1:T(8,128)}, f32[512,256]{0,1:T(8,128)}, u32[]{:S(2)}, u32[]{:S(2)}) %collective-permute-start.8) | collective-permute-done | bytes 524320 | tf_op jit(solution)/shard_map/ppermute | solution.py:20
  185.7 106.2 %shard_map.69 = f32[128,8,128]{2,1,0:T(8,128)} custom-call(f32[128,8,128]{2,1,0:T(8,128)} %reshape.147.x_ref), custom_call_target="tpu_custom_call" | custom-call | tf_op jit(solution)/shard_map/pallas_call | solution.py:85
  296.1 14.7 %all-gather.7.cloned.1.call-done = f32[512,512]{0,1:T(8,128)} async-done(((f32[512,256]{0,1:T(8,128)}), f32[512,512]{0,1:T(8,128)}) %all-gather.7.cloned.1.call-update) | async-done | bytes 1048592 | tf_op jit(solution)/shard_map/all_gather | solution.py:227
  315.3 81.2 %shard_map.70 = f32[128,16,128]{2,1,0:T(8,128)} custom-call(f32[128,16,128]{2,1,0:T(8,128)} %reshape.149.x_ref), custom_call_target="tpu_custom_call" | custom-call | tf_op jit(solution)/shard_map/pallas_call | solution.py:85
  399.4 11.7 %cholesky.286 = f32[128,128]{1,0:T(8,128)S(1)} custom-call(f32[128,128]{1,0:T(8,128)S(1)} %cholesky.426), custom_call_target="Cholesky" | custom-call | tf_op jit(solution)/shard_map/jit(cholesky)/cholesky | solution.py:235
  423.6 12.1 %cholesky.305 = f32[128,128]{1,0:T(8,128)S(1)} custom-call(f32[128,128]{1,0:T(8,128)S(1)} %cholesky.430), custom_call_target="Cholesky" | custom-call | tf_op jit(solution)/shard_map/jit(cholesky)/cholesky | solution.py:235
  435.8 9.8 custom-call.28
  447.2 11.7 %cholesky.326 = f32[128,128]{1,0:T(8,128)S(1)} custom-call(f32[128,128]{1,0:T(8,128)S(1)} %cholesky.435), custom_call_target="Cholesky" | custom-call | tf_op jit(solution)/shard_map/jit(cholesky)/cholesky | solution.py:235
  458.9 9.8 custom-call.29
  470.2 11.9 %cholesky.343 = f32[128,128]{1,0:T(8,128)S(1)} custom-call(f32[128,128]{1,0:T(8,128)S(1)} %convolution_subtract_fusion.9), custom_call_target="Cholesky" | custom-call | tf_op jit(solution)/shard_map/jit(cholesky)/cholesky | solution.py:235
  488.5 12.0 %while.4 = (s32[]{:T(128)}, f32[512,512]{1,0:T(8,128)}, s32[4,2]{0,1:T(2,128)S(1)}, f32[4,128,128]{2,1,0:T(8,128)S(1)}, s32[]{:T(128)}) while((s32[]{:T(128)}, f32[512,512]{1,0:T(8,128)}, s32[4,2]{0,1:T(2,128)S(1)}, f32[4,128,128]{2,1,0:T(8,128)S(1)}, s32[]{:T(128)}) %tuple.89), condition=%wide.while_cond, body=%wide.while_body.sunk | while | flops 2 | bytes 131189 | solution.py:236
  500.5 39.3 %custom-call.30 = f32[4,128,128]{1,2,0:T(8,128)S(1)} custom-call(f32[4,128,128]{2,1,0:T(8,128)S(1)} %get-tuple-element.18), custom_call_target="InvertDiagBlocksLowerTriangular" | custom-call | tf_op jit(solution)/shard_map/triangular_solve/custom-call.3 | solution.py:236
  590.3 11.5 %shard_map.71 = f32[16,256,256]{2,1,0:T(8,128)} custom-call(s32[64]{0:T(128)} %get-tuple-element.119.rows_ref, s32[64]{0:T(128)} %get-tuple-element.118.cols_ref, s32[1]{0:T(128)S(6)} %copy.121.used_ref, bf16[64,256,256]{2,1,0:T(8,128)(2,1)} %tile_ref.3, bf16[16,256,256]{2,1,0:T(8,128)(2,1)} %bitcast.161), custom_call_target="tpu_custom_call" | custom-call | flops 4294967296 | bytes 14680064 | tf_op jit(solution)/shard_map/pallas_call | solution.py:143
  623.0 31.7 %collective-permute-done.31 = f32[512,256]{0,1:T(8,128)} collective-permute-done((f32[512,256]{0,1:T(8,128)}, f32[512,256]{0,1:T(8,128)}, u32[]{:S(2)}, u32[]{:S(2)}) %collective-permute-start.31) | collective-permute-done | bytes 524320 | tf_op jit(solution)/shard_map/ppermute | solution.py:20
  656.6 17.0 %collective-permute-done.30 = f32[512,256]{0,1:T(8,128)} collective-permute-done((f32[512,256]{0,1:T(8,128)}, f32[512,256]{0,1:T(8,128)}, u32[]{:S(2)}, u32[]{:S(2)}) %collective-permute-start.30) | collective-permute-done | bytes 524320 | tf_op jit(solution)/shard_map/ppermute | solution.py:20
  675.5 12.6 %collective-permute-start.24 = (f32[512,256]{0,1:T(8,128)}, f32[512,256]{0,1:T(8,128)}, u32[]{:S(2)}, u32[]{:S(2)}) collective-permute-start(f32[512,256]{0,1:T(8,128)} %copy.50), channel_id=1, source_target_pairs={{0,2},{2,4},{4,6},{6,8},{8,10},{10,12},{12,14},{14,16},{16,18},{18... | collective-permute-start | bytes 1572872 | tf_op jit(solution)/shard_map/ppermute | solution.py:20
  699.9 110.3 %shard_map.72 = f32[128,8,128]{2,1,0:T(8,128)} custom-call(f32[128,8,128]{2,1,0:T(8,128)} %reshape.151.x_ref), custom_call_target="tpu_custom_call" | custom-call | tf_op jit(solution)/shard_map/pallas_call | solution.py:85
  814.4 14.1 %all-gather.11.cloned.1.call-done = f32[512,512]{0,1:T(8,128)} async-done(((f32[512,256]{0,1:T(8,128)}), f32[512,512]{0,1:T(8,128)}) %all-gather.11.cloned.1.call-update) | async-done | bytes 1048592 | tf_op jit(solution)/shard_map/all_gather | solution.py:227
  833.0 81.2 %shard_map.73 = f32[128,16,128]{2,1,0:T(8,128)} custom-call(f32[128,16,128]{2,1,0:T(8,128)} %reshape.153.x_ref), custom_call_target="tpu_custom_call" | custom-call | tf_op jit(solution)/shard_map/pallas_call | solution.py:85
  917.2 11.7 %cholesky.358 = f32[128,128]{1,0:T(8,128)S(1)} custom-call(f32[128,128]{1,0:T(8,128)S(1)} %cholesky.439), custom_call_target="Cholesky" | custom-call | tf_op jit(solution)/shard_map/jit(cholesky)/cholesky | solution.py:235
  929.0 10.0 custom-call.31
  941.5 11.7 %cholesky.377 = f32[128,128]{1,0:T(8,128)S(1)} custom-call(f32[128,128]{1,0:T(8,128)S(1)} %cholesky.443), custom_call_target="Cholesky" | custom-call | tf_op jit(solution)/shard_map/jit(cholesky)/cholesky | solution.py:235
  953.3 9.8 custom-call.32
  964.7 11.9 %cholesky.398 = f32[128,128]{1,0:T(8,128)S(1)} custom-call(f32[128,128]{1,0:T(8,128)S(1)} %cholesky.448), custom_call_target="Cholesky" | custom-call | tf_op jit(solution)/shard_map/jit(cholesky)/cholesky | solution.py:235
  976.6 9.8 custom-call.33
  987.9 11.7 %cholesky.415 = f32[128,128]{1,0:T(8,128)S(1)} custom-call(f32[128,128]{1,0:T(8,128)S(1)} %convolution_subtract_fusion.8), custom_call_target="Cholesky" | custom-call | tf_op jit(solution)/shard_map/jit(cholesky)/cholesky | solution.py:235
  1006.0 12.3 %while.5 = (s32[]{:T(128)}, f32[512,512]{1,0:T(8,128)}, s32[4,2]{0,1:T(2,128)S(1)}, f32[4,128,128]{2,1,0:T(8,128)S(1)}, s32[]{:T(128)}) while((s32[]{:T(128)}, f32[512,512]{1,0:T(8,128)}, s32[4,2]{0,1:T(2,128)S(1)}, f32[4,128,128]{2,1,0:T(8,128)S(1)}, s32[]{:T(128)}) %tuple.103), condition=%wide.while_cond.clone, body=%wide.while_body.clone.sunk | while | flops 2 | bytes 131189 | solution.py:236
  1018.3 39.3 %custom-call.34 = f32[4,128,128]{1,2,0:T(8,128)S(1)} custom-call(f32[4,128,128]{2,1,0:T(8,128)S(1)} %get-tuple-element.19), custom_call_target="InvertDiagBlocksLowerTriangular" | custom-call | tf_op jit(solution)/shard_map/triangular_solve/custom-call.3 | solution.py:236
  (232 shorter events, 260.5 us)
Async XLA Ops:
  7.2 175.2 %all-gather.5.cloned.1.call-start = ((), (), s32[]{:S(2)}) async-start(), calls=%async_computation | async-start | bytes 1572864 | tf_op jit(solution)/shard_map/all_gather | solution.py:215
  8.5 24.9 %collective-permute-start.7 = (bf16[512,256]{0,1:T(8,128)(2,1)S(1)}, bf16[512,256]{0,1:T(8,128)(2,1)S(1)}, u32[]{:S(2)}, u32[]{:S(2)}) collective-permute-start(bf16[512,256]{0,1:T(8,128)(2,1)S(1)} %convert_element_type.6), channel_id=1, source_target_pairs={{0,14},{2,16},{4,18},{6,20},{8,22},{10,24},{12,26},{14,28},{16,30}... | collective-permute-start | bytes 786440 | tf_op jit(solution)/shard_map/ppermute | solution.py:20
  13.7 24.1 %collective-permute-start = (bf16[512,256]{0,1:T(8,128)(2,1)S(1)}, bf16[512,256]{0,1:T(8,128)(2,1)S(1)}, u32[]{:S(2)}, u32[]{:S(2)}) collective-permute-start(bf16[512,256]{0,1:T(8,128)(2,1)S(1)} %convert_element_type.6), channel_id=1, source_target_pairs={{0,12},{2,14},{4,16},{6,18},{8,20},{10,22},{12,24},{14,26},{16,28}... | collective-permute-start | bytes 786440 | tf_op jit(solution)/shard_map/ppermute | solution.py:20
  19.7 23.0 %collective-permute-start.1 = (bf16[512,256]{0,1:T(8,128)(2,1)S(1)}, bf16[512,256]{0,1:T(8,128)(2,1)S(1)}, u32[]{:S(2)}, u32[]{:S(2)}) collective-permute-start(bf16[512,256]{0,1:T(8,128)(2,1)S(1)} %convert_element_type.6), channel_id=1, source_target_pairs={{0,10},{2,12},{4,14},{6,16},{8,18},{10,20},{12,22},{14,24},{16,26}... | collective-permute-start | bytes 786440 | tf_op jit(solution)/shard_map/ppermute | solution.py:20
  24.5 23.8 %collective-permute-start.2 = (bf16[512,256]{0,1:T(8,128)(2,1)S(1)}, bf16[512,256]{0,1:T(8,128)(2,1)S(1)}, u32[]{:S(2)}, u32[]{:S(2)}) collective-permute-start(bf16[512,256]{0,1:T(8,128)(2,1)S(1)} %convert_element_type.6), channel_id=1, source_target_pairs={{0,8},{2,10},{4,12},{6,14},{8,16},{10,18},{12,20},{14,22},{16,24},... | collective-permute-start | bytes 786440 | tf_op jit(solution)/shard_map/ppermute | solution.py:20
  27.4 26.6 %collective-permute-start.3 = (bf16[512,256]{0,1:T(8,128)(2,1)S(1)}, bf16[512,256]{0,1:T(8,128)(2,1)S(1)}, u32[]{:S(2)}, u32[]{:S(2)}) collective-permute-start(bf16[512,256]{0,1:T(8,128)(2,1)S(1)} %convert_element_type.6), channel_id=1, source_target_pairs={{0,6},{2,8},{4,10},{6,12},{8,14},{10,16},{12,18},{14,20},{16,22},{... | collective-permute-start | bytes 786440 | tf_op jit(solution)/shard_map/ppermute | solution.py:20
  33.4 25.2 %collective-permute-start.4 = (bf16[512,256]{0,1:T(8,128)(2,1)S(1)}, bf16[512,256]{0,1:T(8,128)(2,1)S(1)}, u32[]{:S(2)}, u32[]{:S(2)}) collective-permute-start(bf16[512,256]{0,1:T(8,128)(2,1)S(1)} %convert_element_type.6), channel_id=1, source_target_pairs={{0,4},{2,6},{4,8},{6,10},{8,12},{10,14},{12,16},{14,18},{16,20},{1... | collective-permute-start | bytes 786440 | tf_op jit(solution)/shard_map/ppermute | solution.py:20
  37.8 20.9 %collective-permute-start.5 = (bf16[512,256]{0,1:T(8,128)(2,1)S(1)}, bf16[512,256]{0,1:T(8,128)(2,1)S(1)}, u32[]{:S(2)}, u32[]{:S(2)}) collective-permute-start(bf16[512,256]{0,1:T(8,128)(2,1)S(1)} %convert_element_type.6), channel_id=1, source_target_pairs={{0,2},{2,4},{4,6},{6,8},{8,10},{10,12},{12,14},{14,16},{16,18},{18... | collective-permute-start | bytes 786440 | tf_op jit(solution)/shard_map/ppermute | solution.py:20
  78.7 38.5 %collective-permute-start.15 = (f32[512,256]{0,1:T(8,128)}, f32[512,256]{0,1:T(8,128)}, u32[]{:S(2)}, u32[]{:S(2)}) collective-permute-start(f32[512,256]{0,1:T(8,128)} %copy.45), channel_id=1, source_target_pairs={{14,0},{16,2},{18,4},{20,6},{22,8},{24,10},{26,12},{28,14},{30,16}... | collective-permute-start | bytes 1572872 | tf_op jit(solution)/shard_map/ppermute | solution.py:20
  82.0 66.0 %collective-permute-start.14 = (f32[512,256]{0,1:T(8,128)}, f32[512,256]{0,1:T(8,128)}, u32[]{:S(2)}, u32[]{:S(2)}) collective-permute-start(f32[512,256]{0,1:T(8,128)} %copy.44), channel_id=1, source_target_pairs={{12,0},{14,2},{16,4},{18,6},{20,8},{22,10},{24,12},{26,14},{28,16}... | collective-permute-start | bytes 1572872 | tf_op jit(solution)/shard_map/ppermute | solution.py:20
  85.4 64.6 %collective-permute-start.13 = (f32[512,256]{0,1:T(8,128)}, f32[512,256]{0,1:T(8,128)}, u32[]{:S(2)}, u32[]{:S(2)}) collective-permute-start(f32[512,256]{0,1:T(8,128)} %copy.43), channel_id=1, source_target_pairs={{10,0},{12,2},{14,4},{16,6},{18,8},{20,10},{22,12},{24,14},{26,16}... | collective-permute-start | bytes 1572872 | tf_op jit(solution)/shard_map/ppermute | solution.py:20
  86.7 224.1 %all-gather.7.cloned.1.call-start = ((), (), s32[]{:S(2)}) async-start(), calls=%async_computation.1 | async-start | bytes 1572864 | tf_op jit(solution)/shard_map/all_gather | solution.py:227
  88.8 73.8 %collective-permute-start.12 = (f32[512,256]{0,1:T(8,128)}, f32[512,256]{0,1:T(8,128)}, u32[]{:S(2)}, u32[]{:S(2)}) collective-permute-start(f32[512,256]{0,1:T(8,128)} %copy.42), channel_id=1, source_target_pairs={{8,0},{10,2},{12,4},{14,6},{16,8},{18,10},{20,12},{22,14},{24,16},... | collective-permute-start | bytes 1572872 | tf_op jit(solution)/shard_map/ppermute | solution.py:20
  91.1 73.6 %collective-permute-start.11 = (f32[512,256]{0,1:T(8,128)}, f32[512,256]{0,1:T(8,128)S(1)}, u32[]{:S(2)}, u32[]{:S(2)}) collective-permute-start(f32[512,256]{0,1:T(8,128)} %copy.41), channel_id=1, source_target_pairs={{6,0},{8,2},{10,4},{12,6},{14,8},{16,10},{18,12},{20,14},{22,16},{... | collective-permute-start | bytes 1572872 | tf_op jit(solution)/shard_map/ppermute | solution.py:20
  117.2 50.4 %collective-permute-start.10 = (f32[512,256]{0,1:T(8,128)}, f32[512,256]{0,1:T(8,128)S(1)}, u32[]{:S(2)}, u32[]{:S(2)}) collective-permute-start(f32[512,256]{0,1:T(8,128)} %copy.40), channel_id=1, source_target_pairs={{4,0},{6,2},{8,4},{10,6},{12,8},{14,10},{16,12},{18,14},{20,16},{2... | collective-permute-start | bytes 1572872 | tf_op jit(solution)/shard_map/ppermute | solution.py:20
  148.0 19.6 %collective-permute-start.9 = (f32[512,256]{0,1:T(8,128)}, f32[512,256]{0,1:T(8,128)S(1)}, u32[]{:S(2)}, u32[]{:S(2)}) collective-permute-start(f32[512,256]{0,1:T(8,128)} %copy.39), channel_id=1, source_target_pairs={{2,0},{4,2},{6,4},{8,6},{10,8},{12,10},{14,12},{16,14},{18,16},{20... | collective-permute-start | bytes 1572872 | tf_op jit(solution)/shard_map/ppermute | solution.py:20
  150.0 30.2 %collective-permute-start.8 = (f32[512,256]{0,1:T(8,128)}, f32[512,256]{0,1:T(8,128)}, u32[]{:S(2)}, u32[]{:S(2)}) collective-permute-start(f32[512,256]{0,1:T(8,128)} %copy.37), channel_id=1, source_target_pairs={{0,2},{2,4},{4,6},{6,8},{8,10},{10,12},{12,14},{14,16},{16,18},{18... | collective-permute-start | bytes 1572872 | tf_op jit(solution)/shard_map/ppermute | solution.py:20
  295.8 401.0 %all-gather.9.cloned.1.call-start = ((), (), s32[]{:S(2)}) async-start(), calls=%async_computation.2 | async-start | bytes 1572864 | tf_op jit(solution)/shard_map/all_gather | solution.py:215
  546.8 18.1 %collective-permute-start.23 = (bf16[512,256]{0,1:T(8,128)(2,1)S(1)}, bf16[512,256]{0,1:T(8,128)(2,1)S(1)}, u32[]{:S(2)}, u32[]{:S(2)}) collective-permute-start(bf16[512,256]{0,1:T(8,128)(2,1)S(1)} %get-tuple-element.40), channel_id=1, source_target_pairs={{0,14},{2,16},{4,18},{6,20},{8,22},{10,24},{12,26},{14,28},{16,30}... | collective-permute-start | bytes 786440 | tf_op jit(solution)/shard_map/ppermute | solution.py:20
  549.5 19.3 %collective-permute-start.16 = (bf16[512,256]{0,1:T(8,128)(2,1)S(1)}, bf16[512,256]{0,1:T(8,128)(2,1)S(1)}, u32[]{:S(2)}, u32[]{:S(2)}) collective-permute-start(bf16[512,256]{0,1:T(8,128)(2,1)S(1)} %get-tuple-element.40), channel_id=1, source_target_pairs={{0,12},{2,14},{4,16},{6,18},{8,20},{10,22},{12,24},{14,26},{16,28}... | collective-permute-start | bytes 786440 | tf_op jit(solution)/shard_map/ppermute | solution.py:20
  554.0 21.1 %collective-permute-start.17 = (bf16[512,256]{0,1:T(8,128)(2,1)S(1)}, bf16[512,256]{0,1:T(8,128)(2,1)S(1)}, u32[]{:S(2)}, u32[]{:S(2)}) collective-permute-start(bf16[512,256]{0,1:T(8,128)(2,1)S(1)} %get-tuple-element.40), channel_id=1, source_target_pairs={{0,10},{2,12},{4,14},{6,16},{8,18},{10,20},{12,22},{14,24},{16,26}... | collective-permute-start | bytes 786440 | tf_op jit(solution)/shard_map/ppermute | solution.py:20
  558.1 20.7 %collective-permute-start.18 = (bf16[512,256]{0,1:T(8,128)(2,1)S(1)}, bf16[512,256]{0,1:T(8,128)(2,1)S(1)}, u32[]{:S(2)}, u32[]{:S(2)}) collective-permute-start(bf16[512,256]{0,1:T(8,128)(2,1)S(1)} %get-tuple-element.40), channel_id=1, source_target_pairs={{0,8},{2,10},{4,12},{6,14},{8,16},{10,18},{12,20},{14,22},{16,24},... | collective-permute-start | bytes 786440 | tf_op jit(solution)/shard_map/ppermute | solution.py:20
  561.6 20.8 %collective-permute-start.19 = (bf16[512,256]{0,1:T(8,128)(2,1)S(1)}, bf16[512,256]{0,1:T(8,128)(2,1)S(1)}, u32[]{:S(2)}, u32[]{:S(2)}) collective-permute-start(bf16[512,256]{0,1:T(8,128)(2,1)S(1)} %get-tuple-element.40), channel_id=1, source_target_pairs={{0,6},{2,8},{4,10},{6,12},{8,14},{10,16},{12,18},{14,20},{16,22},{... | collective-permute-start | bytes 786440 | tf_op jit(solution)/shard_map/ppermute | solution.py:20
  564.9 20.3 %collective-permute-start.20 = (bf16[512,256]{0,1:T(8,128)(2,1)S(1)}, bf16[512,256]{0,1:T(8,128)(2,1)S(1)}, u32[]{:S(2)}, u32[]{:S(2)}) collective-permute-start(bf16[512,256]{0,1:T(8,128)(2,1)S(1)} %get-tuple-element.40), channel_id=1, source_target_pairs={{0,4},{2,6},{4,8},{6,10},{8,12},{10,14},{12,16},{14,18},{16,20},{1... | collective-permute-start | bytes 786440 | tf_op jit(solution)/shard_map/ppermute | solution.py:20
  607.3 47.4 %collective-permute-start.31 = (f32[512,256]{0,1:T(8,128)}, f32[512,256]{0,1:T(8,128)}, u32[]{:S(2)}, u32[]{:S(2)}) collective-permute-start(f32[512,256]{0,1:T(8,128)} %copy.58), channel_id=1, source_target_pairs={{14,0},{16,2},{18,4},{20,6},{22,8},{24,10},{26,12},{28,14},{30,16}... | collective-permute-start | bytes 1572872 | tf_op jit(solution)/shard_map/ppermute | solution.py:20
  610.6 62.9 %collective-permute-start.30 = (f32[512,256]{0,1:T(8,128)}, f32[512,256]{0,1:T(8,128)}, u32[]{:S(2)}, u32[]{:S(2)}) collective-permute-start(f32[512,256]{0,1:T(8,128)} %copy.57), channel_id=1, source_target_pairs={{12,0},{14,2},{16,4},{18,6},{20,8},{22,10},{24,12},{26,14},{28,16}... | collective-permute-start | bytes 1572872 | tf_op jit(solution)/shard_map/ppermute | solution.py:20
  614.0 61.5 %collective-permute-start.29 = (f32[512,256]{0,1:T(8,128)}, f32[512,256]{0,1:T(8,128)}, u32[]{:S(2)}, u32[]{:S(2)}) collective-permute-start(f32[512,256]{0,1:T(8,128)} %copy.56), channel_id=1, source_target_pairs={{10,0},{12,2},{14,4},{16,6},{18,8},{20,10},{22,12},{24,14},{26,16}... | collective-permute-start | bytes 1572872 | tf_op jit(solution)/shard_map/ppermute | solution.py:20
  615.3 213.2 %all-gather.11.cloned.1.call-start = ((), (), s32[]{:S(2)}) async-start(), calls=%async_computation.3 | async-start | bytes 1572864 | tf_op jit(solution)/shard_map/all_gather | solution.py:227
  616.3 72.0 %collective-permute-start.28 = (f32[512,256]{0,1:T(8,128)}, f32[512,256]{0,1:T(8,128)S(1)}, u32[]{:S(2)}, u32[]{:S(2)}) collective-permute-start(f32[512,256]{0,1:T(8,128)} %copy.55), channel_id=1, source_target_pairs={{8,0},{10,2},{12,4},{14,6},{16,8},{18,10},{20,12},{22,14},{24,16},... | collective-permute-start | bytes 1572872 | tf_op jit(solution)/shard_map/ppermute | solution.py:20
  618.6 69.7 %collective-permute-start.27 = (f32[512,256]{0,1:T(8,128)}, f32[512,256]{0,1:T(8,128)S(1)}, u32[]{:S(2)}, u32[]{:S(2)}) collective-permute-start(f32[512,256]{0,1:T(8,128)} %copy.54), channel_id=1, source_target_pairs={{6,0},{8,2},{10,4},{12,6},{14,8},{16,10},{18,12},{20,14},{22,16},{... | collective-permute-start | bytes 1572872 | tf_op jit(solution)/shard_map/ppermute | solution.py:20
  654.7 35.5 %collective-permute-start.26 = (f32[512,256]{0,1:T(8,128)}, f32[512,256]{0,1:T(8,128)S(1)}, u32[]{:S(2)}, u32[]{:S(2)}) collective-permute-start(f32[512,256]{0,1:T(8,128)} %copy.53), channel_id=1, source_target_pairs={{4,0},{6,2},{8,4},{10,6},{12,8},{14,10},{16,12},{18,14},{20,16},{2... | collective-permute-start | bytes 1572872 | tf_op jit(solution)/shard_map/ppermute | solution.py:20
  675.5 19.2 %collective-permute-start.24 = (f32[512,256]{0,1:T(8,128)}, f32[512,256]{0,1:T(8,128)}, u32[]{:S(2)}, u32[]{:S(2)}) collective-permute-start(f32[512,256]{0,1:T(8,128)} %copy.50), channel_id=1, source_target_pairs={{0,2},{2,4},{4,6},{6,8},{8,10},{10,12},{12,14},{14,16},{16,18},{18... | collective-permute-start | bytes 1572872 | tf_op jit(solution)/shard_map/ppermute | solution.py:20
  (11 other events, 582.5 us)
Sparse Core Ops, SparseCore 0:
  86.8 60.1 all-gather.4
  295.9 14.7 all-gather.6
  615.4 53.7 all-gather.8
  813.6 14.9 all-gather.10

commit v5 on v4

--- a/solution.py
+++ b/solution.py
@@ -20,68 +20,102 @@
     return lax.ppermute(block, axis, route)
 
 
-ORDER = (0, 2, 5, 1, 3, 6, 4)
+GROUPS = ((0, 2), (2, 2), (5, 2), (4, 1))
+
+
+def digit_groups(size):
+    nbits = size.bit_length() - 1
+    return [(low, min(width, nbits - low)) for low, width in GROUPS if low < nbits]
+
+
+def flipped(digit, e, width):
+    total = 0
+    for bit in range(width):
+        total = total + ((digit // (1 << bit) + e // (1 << bit)) % 2) * (1 << bit)
+    return total
+
 
 def exchange_sum(size, x_ref, out_ref, work_ref, recv_ref, final_ref, send_sems, recv_sems):
     me = lax.axis_index("patch")
-    bits = [b for b in ORDER if (1 << b) < size]
+    groups = digit_groups(size)
     mesh_ids = pl.DeviceIdType.MESH
 
-    def partner_of(b):
-        side = (me // (1 << b)) % 2
-        return side, me + (1 - 2 * side) * (1 << b)
+    def digit_of(low, width):
+        return (me // (1 << low)) % (1 << width)
+
+    def partner_of(low, width, e):
+        digit = digit_of(low, width)
+        return me + (flipped(digit, e, width) - digit) * (1 << low)
 
     barrier = pltpu.get_barrier_semaphore()
-    for b in bits:
-        _, partner = partner_of(b)
-        pl.semaphore_signal(barrier, 1, device_id={"patch": partner}, device_id_type=mesh_ids)
-    pl.semaphore_wait(barrier, len(bits))
+    greeted = 0
+    for low, width in groups:
+        for e in range(1, 1 << width):
+            pl.semaphore_signal(
+                barrier, 1, device_id={"patch": partner_of(low, width, e)}, device_id_type=mesh_ids
+            )
+            greeted += 1
+    pl.semaphore_wait(barrier, greeted)
     work_ref[...] = x_ref[...]
     lo = 0
     span = work_ref.shape[0]
     recv_at = 0
-    for k, b in enumerate(bits):
-        span = span // 2
-        side, partner = partner_of(b)
-        keep = lo + side * span
-        send = lo + (1 - side) * span
-        copy = pltpu.make_async_remote_copy(
-            src_ref=work_ref.at[pl.ds(send, span)],
-            dst_ref=recv_ref.at[pl.ds(recv_at, span)],
-            send_sem=send_sems.at[k],
-            recv_sem=recv_sems.at[k],
-            device_id={"patch": partner},
-            device_id_type=mesh_ids,
-        )
-        copy.start()
-        copy.wait()
-        work_ref[pl.ds(keep, span)] = work_ref[pl.ds(keep, span)] + recv_ref[pl.ds(recv_at, span)]
+    sem = 0
+    for low, width in groups:
+        ways = 1 << width
+        span = span // ways
+        digit = digit_of(low, width)
+        copies = []
+        for e in range(1, ways):
+            copy = pltpu.make_async_remote_copy(
+                src_ref=work_ref.at[pl.ds(lo + flipped(digit, e, width) * span, span)],
+                dst_ref=recv_ref.at[pl.ds(recv_at + (e - 1) * span, span)],
+                send_sem=send_sems.at[sem],
+                recv_sem=recv_sems.at[sem],
+                device_id={"patch": partner_of(low, width, e)},
+                device_id_type=mesh_ids,
+            )
+            copy.start()
+            copies.append(copy)
+            sem += 1
+        for copy in copies:
+            copy.wait()
+        keep = lo + digit * span
+        total = work_ref[pl.ds(keep, span)]
+        for e in range(1, ways):
+            total = total + recv_ref[pl.ds(recv_at + (e - 1) * span, span)]
+        work_ref[pl.ds(keep, span)] = total
         lo = keep
-        recv_at += span
+        recv_at += (ways - 1) * span
     final_ref[pl.ds(lo, span)] = work_ref[pl.ds(lo, span)]
-    for j, b in enumerate(reversed(bits)):
-        side, partner = partner_of(b)
-        copy = pltpu.make_async_remote_copy(
-            src_ref=final_ref.at[pl.ds(lo, span)],
-            dst_ref=final_ref.at[pl.ds(lo, span)],
-            send_sem=send_sems.at[len(bits) + j],
-            recv_sem=recv_sems.at[len(bits) + j],
-            device_id={"patch": partner},
-            device_id_type=mesh_ids,
-        )
-        copy.start()
-        copy.wait()
-        lo = lo - side * span
-        span = span * 2
+    for low, width in reversed(groups):
+        ways = 1 << width
+        digit = digit_of(low, width)
+        copies = []
+        for e in range(1, ways):
+            copy = pltpu.make_async_remote_copy(
+                src_ref=final_ref.at[pl.ds(lo, span)],
+                dst_ref=final_ref.at[pl.ds(lo, span)],
+                send_sem=send_sems.at[sem],
+                recv_sem=recv_sems.at[sem],
+                device_id={"patch": partner_of(low, width, e)},
+                device_id_type=mesh_ids,
+            )
+            copy.start()
+            copies.append(copy)
+            sem += 1
+        for copy in copies:
+            copy.wait()
+        lo = lo - digit * span
+        span = span * ways
     out_ref[...] = final_ref[...]
 
 
 def summed_over_patch(block, collective):
     size = lax.axis_size("patch")
     rows, cols = block.shape
-    lead = size
-    flat = block.reshape(lead, (rows * cols) // (lead * 128), 128)
-    steps = 2 * len([b for b in ORDER if (1 << b) < size])
+    flat = block.reshape(size, (rows * cols) // (size * 128), 128)
+    steps = 2 * sum((1 << width) - 1 for _, width in digit_groups(size))
     out = pl.pallas_call(
         functools.partial(exchange_sum, size),
         out_shape=jax.ShapeDtypeStruct(flat.shape, flat.dtype),

time: 1080 us -> 1010 us (0.935)
  Pallas kernels: 402 us -> 312 us
  waiting for transfers between devices: 182 us -> 193 us
    pallas_call x4, Pallas kernels: 379 us -> 285 us  [summed_over_patch(): pl.pallas_call(functools.partial(exchange_sum, size), out_shape=jax.Shape...]
    ppermute x32, waiting for transfers between devices: 153 us -> 171 us  [shifted(): return lax.ppermute(block, axis, route)]
  transfers between devices with their start and end apart: 36 -> 36, of which waited for: 21 -> 20; matrix products, arithmetic and copies ran while one was open for 3% -> 3% of each run, Pallas kernels for 0% -> 0%
where the time goes in v5:
time: 1010 us; the launch traced here: 1000 us
  Pallas kernels  312 us (31%)
  other arithmetic  255 us (25%)
  waiting for transfers between devices  193 us (19%)
  starting transfers between devices  112 us (11%)
  local copies, waits for them, and re-layouts  68.5 us (7%)
  matrix products  38.6 us (4%)
  between operations  21 us (2%)
    pallas_call x4, Pallas kernels, summed_over_patch(): pl.pallas_call(functools.partial(exchange_sum, size), out_shape=jax.Shape...  285 us
    ppermute x32, waiting for transfers between devices, shifted(): return lax.ppermute(block, axis, route)  171 us
    another operation x30, other arithmetic, shards(): factor = jnp.linalg.cholesky(gram_matrix)  159 us
    ppermute x32, starting transfers between devices, shifted(): return lax.ppermute(block, axis, route)  112 us
    another operation x6, other arithmetic, shards(): lax.linalg.triangular_solve(factor, update_all, left_side=False, lower=Tr...  81.1 us
    pallas_call x2, Pallas kernels, hessian_window(): pl.pallas_call(tile_products, grid_spec=grid_spec, out_shape=jax.ShapeDty...  27.4 us
    another operation x27, local copies, waits for them, and re-layouts, shards(): lax.linalg.triangular_solve(factor, update_all, left_side=False, lower=Tr...  24 us
    select_n x16, local copies, waits for them, and re-layouts, shards(): outgoing = jnp.where(parity == 0, lower_seg, upper_seg)  23.4 us
  transfers between devices with their start and end apart: 36, of which 20 were waited for; matrix products, arithmetic and copies ran while one was open for 3% of the time, Pallas kernels for 0%

profile of v5, /device:TPU:4, one launch (start us, length us, event | category | flops | bytes accessed | tf_op | source)
XLA Modules:
  0.0 1001.1 jit_solution(3853444790676564160)
XLA Ops:
  61.5 13.7 %shard_map.68 = f32[16,256,256]{2,1,0:T(8,128)} custom-call(s32[64]{0:T(128)} %get-tuple-element.119.rows_ref, s32[64]{0:T(128)} %get-tuple-element.118.cols_ref, s32[1]{0:T(128)S(6)} %copy.121.used_ref, bf16[64,256,256]{2,1,0:T(8,128)(2,1)} %tile_ref.3, bf16[16,256,256]{2,1,0:T(8,128)(2,1)} %bitcast.162), custom_call_target="tpu_custom_call" | custom-call | flops 4294967296 | bytes 14680064 | tf_op jit(solution)/shard_map/pallas_call | solution.py:177
  97.6 25.9 %collective-permute-done.15 = f32[512,256]{0,1:T(8,128)} collective-permute-done((f32[512,256]{0,1:T(8,128)}, f32[512,256]{0,1:T(8,128)}, u32[]{:S(2)}, u32[]{:S(2)}) %collective-permute-start.15) | collective-permute-done | bytes 524320 | tf_op jit(solution)/shard_map/ppermute | solution.py:20
  126.4 33.9 %collective-permute-done.14 = f32[512,256]{0,1:T(8,128)} collective-permute-done((f32[512,256]{0,1:T(8,128)}, f32[512,256]{0,1:T(8,128)}, u32[]{:S(2)}, u32[]{:S(2)}) %collective-permute-start.14) | collective-permute-done | bytes 524320 | tf_op jit(solution)/shard_map/ppermute | solution.py:20
  162.2 13.8 %collective-permute-start.8 = (f32[512,256]{0,1:T(8,128)}, f32[512,256]{0,1:T(8,128)}, u32[]{:S(2)}, u32[]{:S(2)}) collective-permute-start(f32[512,256]{0,1:T(8,128)} %copy.37), channel_id=1, source_target_pairs={{0,2},{2,4},{4,6},{6,8},{8,10},{10,12},{12,14},{14,16},{16,18},{18... | collective-permute-start | bytes 1572872 | tf_op jit(solution)/shard_map/ppermute | solution.py:20
  192.7 86.7 %shard_map.69 = f32[128,8,128]{2,1,0:T(8,128)} custom-call(f32[128,8,128]{2,1,0:T(8,128)} %reshape.147.x_ref), custom_call_target="tpu_custom_call" | custom-call | tf_op jit(solution)/shard_map/pallas_call | solution.py:119
  283.6 11.7 %all-gather.7.cloned.1.call-done = f32[512,512]{0,1:T(8,128)} async-done(((f32[512,256]{0,1:T(8,128)}), f32[512,512]{0,1:T(8,128)}) %all-gather.7.cloned.1.call-update) | async-done | bytes 1048592 | tf_op jit(solution)/shard_map/all_gather | solution.py:261
  299.8 60.7 %shard_map.70 = f32[128,16,128]{2,1,0:T(8,128)} custom-call(f32[128,16,128]{2,1,0:T(8,128)} %reshape.149.x_ref), custom_call_target="tpu_custom_call" | custom-call | tf_op jit(solution)/shard_map/pallas_call | solution.py:119
  363.5 11.7 %cholesky.286 = f32[128,128]{1,0:T(8,128)S(1)} custom-call(f32[128,128]{1,0:T(8,128)S(1)} %cholesky.426), custom_call_target="Cholesky" | custom-call | tf_op jit(solution)/shard_map/jit(cholesky)/cholesky | solution.py:269
  375.4 9.8 custom-call.27
  387.7 12.1 %cholesky.305 = f32[128,128]{1,0:T(8,128)S(1)} custom-call(f32[128,128]{1,0:T(8,128)S(1)} %cholesky.430), custom_call_target="Cholesky" | custom-call | tf_op jit(solution)/shard_map/jit(cholesky)/cholesky | solution.py:269
  399.8 9.8 custom-call.28
  411.2 11.7 %cholesky.326 = f32[128,128]{1,0:T(8,128)S(1)} custom-call(f32[128,128]{1,0:T(8,128)S(1)} %cholesky.435), custom_call_target="Cholesky" | custom-call | tf_op jit(solution)/shard_map/jit(cholesky)/cholesky | solution.py:269
  423.0 9.8 custom-call.29
  434.2 11.9 %cholesky.343 = f32[128,128]{1,0:T(8,128)S(1)} custom-call(f32[128,128]{1,0:T(8,128)S(1)} %convolution_subtract_fusion.9), custom_call_target="Cholesky" | custom-call | tf_op jit(solution)/shard_map/jit(cholesky)/cholesky | solution.py:269
  452.5 12.0 %while.4 = (s32[]{:T(128)}, f32[512,512]{1,0:T(8,128)}, s32[4,2]{0,1:T(2,128)S(1)}, f32[4,128,128]{2,1,0:T(8,128)S(1)}, s32[]{:T(128)}) while((s32[]{:T(128)}, f32[512,512]{1,0:T(8,128)}, s32[4,2]{0,1:T(2,128)S(1)}, f32[4,128,128]{2,1,0:T(8,128)S(1)}, s32[]{:T(128)}) %tuple.89), condition=%wide.while_cond, body=%wide.while_body.sunk | while | flops 2 | bytes 131189 | solution.py:270
  464.6 39.3 %custom-call.30 = f32[4,128,128]{1,2,0:T(8,128)S(1)} custom-call(f32[4,128,128]{2,1,0:T(8,128)S(1)} %get-tuple-element.18), custom_call_target="InvertDiagBlocksLowerTriangular" | custom-call | tf_op jit(solution)/shard_map/triangular_solve/custom-call.3 | solution.py:270
  556.7 13.7 %shard_map.71 = f32[16,256,256]{2,1,0:T(8,128)} custom-call(s32[64]{0:T(128)} %get-tuple-element.119.rows_ref, s32[64]{0:T(128)} %get-tuple-element.118.cols_ref, s32[1]{0:T(128)S(6)} %copy.121.used_ref, bf16[64,256,256]{2,1,0:T(8,128)(2,1)} %tile_ref.3, bf16[16,256,256]{2,1,0:T(8,128)(2,1)} %bitcast.161), custom_call_target="tpu_custom_call" | custom-call | flops 4294967296 | bytes 14680064 | tf_op jit(solution)/shard_map/pallas_call | solution.py:177
  591.6 28.8 %collective-permute-done.31 = f32[512,256]{0,1:T(8,128)} collective-permute-done((f32[512,256]{0,1:T(8,128)}, f32[512,256]{0,1:T(8,128)}, u32[]{:S(2)}, u32[]{:S(2)}) %collective-permute-start.31) | collective-permute-done | bytes 524320 | tf_op jit(solution)/shard_map/ppermute | solution.py:20
  622.3 27.1 %collective-permute-done.30 = f32[512,256]{0,1:T(8,128)} collective-permute-done((f32[512,256]{0,1:T(8,128)}, f32[512,256]{0,1:T(8,128)}, u32[]{:S(2)}, u32[]{:S(2)}) %collective-permute-start.30) | collective-permute-done | bytes 524320 | tf_op jit(solution)/shard_map/ppermute | solution.py:20
  651.3 19.8 %collective-permute-start.24 = (f32[512,256]{0,1:T(8,128)}, f32[512,256]{0,1:T(8,128)}, u32[]{:S(2)}, u32[]{:S(2)}) collective-permute-start(f32[512,256]{0,1:T(8,128)} %copy.50), channel_id=1, source_target_pairs={{0,2},{2,4},{4,6},{6,8},{8,10},{10,12},{12,14},{14,16},{16,18},{18... | collective-permute-start | bytes 1572872 | tf_op jit(solution)/shard_map/ppermute | solution.py:20
  687.2 76.8 %shard_map.72 = f32[128,8,128]{2,1,0:T(8,128)} custom-call(f32[128,8,128]{2,1,0:T(8,128)} %reshape.151.x_ref), custom_call_target="tpu_custom_call" | custom-call | tf_op jit(solution)/shard_map/pallas_call | solution.py:119
  768.1 10.2 %all-gather.11.cloned.1.call-done = f32[512,512]{0,1:T(8,128)} async-done(((f32[512,256]{0,1:T(8,128)}), f32[512,512]{0,1:T(8,128)}) %all-gather.11.cloned.1.call-update) | async-done | bytes 1048592 | tf_op jit(solution)/shard_map/all_gather | solution.py:261
  782.9 60.7 %shard_map.73 = f32[128,16,128]{2,1,0:T(8,128)} custom-call(f32[128,16,128]{2,1,0:T(8,128)} %reshape.153.x_ref), custom_call_target="tpu_custom_call" | custom-call | tf_op jit(solution)/shard_map/pallas_call | solution.py:119
  846.6 11.7 %cholesky.358 = f32[128,128]{1,0:T(8,128)S(1)} custom-call(f32[128,128]{1,0:T(8,128)S(1)} %cholesky.439), custom_call_target="Cholesky" | custom-call | tf_op jit(solution)/shard_map/jit(cholesky)/cholesky | solution.py:269
  858.4 10.0 custom-call.31
  870.9 11.7 %cholesky.377 = f32[128,128]{1,0:T(8,128)S(1)} custom-call(f32[128,128]{1,0:T(8,128)S(1)} %cholesky.443), custom_call_target="Cholesky" | custom-call | tf_op jit(solution)/shard_map/jit(cholesky)/cholesky | solution.py:269
  882.7 9.8 custom-call.32
  894.1 11.9 %cholesky.398 = f32[128,128]{1,0:T(8,128)S(1)} custom-call(f32[128,128]{1,0:T(8,128)S(1)} %cholesky.448), custom_call_target="Cholesky" | custom-call | tf_op jit(solution)/shard_map/jit(cholesky)/cholesky | solution.py:269
  906.0 9.8 custom-call.33
  917.3 11.7 %cholesky.415 = f32[128,128]{1,0:T(8,128)S(1)} custom-call(f32[128,128]{1,0:T(8,128)S(1)} %convolution_subtract_fusion.8), custom_call_target="Cholesky" | custom-call | tf_op jit(solution)/shard_map/jit(cholesky)/cholesky | solution.py:269
  935.4 12.3 %while.5 = (s32[]{:T(128)}, f32[512,512]{1,0:T(8,128)}, s32[4,2]{0,1:T(2,128)S(1)}, f32[4,128,128]{2,1,0:T(8,128)S(1)}, s32[]{:T(128)}) while((s32[]{:T(128)}, f32[512,512]{1,0:T(8,128)}, s32[4,2]{0,1:T(2,128)S(1)}, f32[4,128,128]{2,1,0:T(8,128)S(1)}, s32[]{:T(128)}) %tuple.103), condition=%wide.while_cond.clone, body=%wide.while_body.clone.sunk | while | flops 2 | bytes 131189 | solution.py:270
  947.7 39.3 %custom-call.34 = f32[4,128,128]{1,2,0:T(8,128)S(1)} custom-call(f32[4,128,128]{2,1,0:T(8,128)S(1)} %get-tuple-element.19), custom_call_target="InvertDiagBlocksLowerTriangular" | custom-call | tf_op jit(solution)/shard_map/triangular_solve/custom-call.3 | solution.py:270
  (232 shorter events, 264.0 us)
Async XLA Ops:
  7.2 182.2 %all-gather.5.cloned.1.call-start = ((), (), s32[]{:S(2)}) async-start(), calls=%async_computation | async-start | bytes 1572864 | tf_op jit(solution)/shard_map/all_gather | solution.py:249
  8.5 24.9 %collective-permute-start.7 = (bf16[512,256]{0,1:T(8,128)(2,1)S(1)}, bf16[512,256]{0,1:T(8,128)(2,1)S(1)}, u32[]{:S(2)}, u32[]{:S(2)}) collective-permute-start(bf16[512,256]{0,1:T(8,128)(2,1)S(1)} %convert_element_type.6), channel_id=1, source_target_pairs={{0,14},{2,16},{4,18},{6,20},{8,22},{10,24},{12,26},{14,28},{16,30}... | collective-permute-start | bytes 786440 | tf_op jit(solution)/shard_map/ppermute | solution.py:20
  13.7 24.1 %collective-permute-start = (bf16[512,256]{0,1:T(8,128)(2,1)S(1)}, bf16[512,256]{0,1:T(8,128)(2,1)S(1)}, u32[]{:S(2)}, u32[]{:S(2)}) collective-permute-start(bf16[512,256]{0,1:T(8,128)(2,1)S(1)} %convert_element_type.6), channel_id=1, source_target_pairs={{0,12},{2,14},{4,16},{6,18},{8,20},{10,22},{12,24},{14,26},{16,28}... | collective-permute-start | bytes 786440 | tf_op jit(solution)/shard_map/ppermute | solution.py:20
  19.7 23.0 %collective-permute-start.1 = (bf16[512,256]{0,1:T(8,128)(2,1)S(1)}, bf16[512,256]{0,1:T(8,128)(2,1)S(1)}, u32[]{:S(2)}, u32[]{:S(2)}) collective-permute-start(bf16[512,256]{0,1:T(8,128)(2,1)S(1)} %convert_element_type.6), channel_id=1, source_target_pairs={{0,10},{2,12},{4,14},{6,16},{8,18},{10,20},{12,22},{14,24},{16,26}... | collective-permute-start | bytes 786440 | tf_op jit(solution)/shard_map/ppermute | solution.py:20
  24.5 23.8 %collective-permute-start.2 = (bf16[512,256]{0,1:T(8,128)(2,1)S(1)}, bf16[512,256]{0,1:T(8,128)(2,1)S(1)}, u32[]{:S(2)}, u32[]{:S(2)}) collective-permute-start(bf16[512,256]{0,1:T(8,128)(2,1)S(1)} %convert_element_type.6), channel_id=1, source_target_pairs={{0,8},{2,10},{4,12},{6,14},{8,16},{10,18},{12,20},{14,22},{16,24},... | collective-permute-start | bytes 786440 | tf_op jit(solution)/shard_map/ppermute | solution.py:20
  27.4 26.6 %collective-permute-start.3 = (bf16[512,256]{0,1:T(8,128)(2,1)S(1)}, bf16[512,256]{0,1:T(8,128)(2,1)S(1)}, u32[]{:S(2)}, u32[]{:S(2)}) collective-permute-start(bf16[512,256]{0,1:T(8,128)(2,1)S(1)} %convert_element_type.6), channel_id=1, source_target_pairs={{0,6},{2,8},{4,10},{6,12},{8,14},{10,16},{12,18},{14,20},{16,22},{... | collective-permute-start | bytes 786440 | tf_op jit(solution)/shard_map/ppermute | solution.py:20
  33.4 25.2 %collective-permute-start.4 = (bf16[512,256]{0,1:T(8,128)(2,1)S(1)}, bf16[512,256]{0,1:T(8,128)(2,1)S(1)}, u32[]{:S(2)}, u32[]{:S(2)}) collective-permute-start(bf16[512,256]{0,1:T(8,128)(2,1)S(1)} %convert_element_type.6), channel_id=1, source_target_pairs={{0,4},{2,6},{4,8},{6,10},{8,12},{10,14},{12,16},{14,18},{16,20},{1... | collective-permute-start | bytes 786440 | tf_op jit(solution)/shard_map/ppermute | solution.py:20
  37.8 20.9 %collective-permute-start.5 = (bf16[512,256]{0,1:T(8,128)(2,1)S(1)}, bf16[512,256]{0,1:T(8,128)(2,1)S(1)}, u32[]{:S(2)}, u32[]{:S(2)}) collective-permute-start(bf16[512,256]{0,1:T(8,128)(2,1)S(1)} %convert_element_type.6), channel_id=1, source_target_pairs={{0,2},{2,4},{4,6},{6,8},{8,10},{10,12},{12,14},{14,16},{16,18},{18... | collective-permute-start | bytes 786440 | tf_op jit(solution)/shard_map/ppermute | solution.py:20
  80.9 42.6 %collective-permute-start.15 = (f32[512,256]{0,1:T(8,128)}, f32[512,256]{0,1:T(8,128)}, u32[]{:S(2)}, u32[]{:S(2)}) collective-permute-start(f32[512,256]{0,1:T(8,128)} %copy.45), channel_id=1, source_target_pairs={{14,0},{16,2},{18,4},{20,6},{22,8},{24,10},{26,12},{28,14},{30,16}... | collective-permute-start | bytes 1572872 | tf_op jit(solution)/shard_map/ppermute | solution.py:20
  84.3 76.0 %collective-permute-start.14 = (f32[512,256]{0,1:T(8,128)}, f32[512,256]{0,1:T(8,128)}, u32[]{:S(2)}, u32[]{:S(2)}) collective-permute-start(f32[512,256]{0,1:T(8,128)} %copy.44), channel_id=1, source_target_pairs={{12,0},{14,2},{16,4},{18,6},{20,8},{22,10},{24,12},{26,14},{28,16}... | collective-permute-start | bytes 1572872 | tf_op jit(solution)/shard_map/ppermute | solution.py:20
  87.6 74.6 %collective-permute-start.13 = (f32[512,256]{0,1:T(8,128)}, f32[512,256]{0,1:T(8,128)}, u32[]{:S(2)}, u32[]{:S(2)}) collective-permute-start(f32[512,256]{0,1:T(8,128)} %copy.43), channel_id=1, source_target_pairs={{10,0},{12,2},{14,4},{16,6},{18,8},{20,10},{22,12},{24,14},{26,16}... | collective-permute-start | bytes 1572872 | tf_op jit(solution)/shard_map/ppermute | solution.py:20
  88.9 206.4 %all-gather.7.cloned.1.call-start = ((), (), s32[]{:S(2)}) async-start(), calls=%async_computation.1 | async-start | bytes 1572864 | tf_op jit(solution)/shard_map/all_gather | solution.py:261
  91.0 85.3 %collective-permute-start.12 = (f32[512,256]{0,1:T(8,128)}, f32[512,256]{0,1:T(8,128)}, u32[]{:S(2)}, u32[]{:S(2)}) collective-permute-start(f32[512,256]{0,1:T(8,128)} %copy.42), channel_id=1, source_target_pairs={{8,0},{10,2},{12,4},{14,6},{16,8},{18,10},{20,12},{22,14},{24,16},... | collective-permute-start | bytes 1572872 | tf_op jit(solution)/shard_map/ppermute | solution.py:20
  93.3 83.0 %collective-permute-start.11 = (f32[512,256]{0,1:T(8,128)}, f32[512,256]{0,1:T(8,128)S(1)}, u32[]{:S(2)}, u32[]{:S(2)}) collective-permute-start(f32[512,256]{0,1:T(8,128)} %copy.41), channel_id=1, source_target_pairs={{6,0},{8,2},{10,4},{12,6},{14,8},{16,10},{18,12},{20,14},{22,16},{... | collective-permute-start | bytes 1572872 | tf_op jit(solution)/shard_map/ppermute | solution.py:20
  123.5 56.3 %collective-permute-start.10 = (f32[512,256]{0,1:T(8,128)}, f32[512,256]{0,1:T(8,128)S(1)}, u32[]{:S(2)}, u32[]{:S(2)}) collective-permute-start(f32[512,256]{0,1:T(8,128)} %copy.40), channel_id=1, source_target_pairs={{4,0},{6,2},{8,4},{10,6},{12,8},{14,10},{16,12},{18,14},{20,16},{2... | collective-permute-start | bytes 1572872 | tf_op jit(solution)/shard_map/ppermute | solution.py:20
  160.3 19.6 %collective-permute-start.9 = (f32[512,256]{0,1:T(8,128)}, f32[512,256]{0,1:T(8,128)S(1)}, u32[]{:S(2)}, u32[]{:S(2)}) collective-permute-start(f32[512,256]{0,1:T(8,128)} %copy.39), channel_id=1, source_target_pairs={{2,0},{4,2},{6,4},{8,6},{10,8},{12,10},{14,12},{16,14},{18,16},{20... | collective-permute-start | bytes 1572872 | tf_op jit(solution)/shard_map/ppermute | solution.py:20
  162.2 24.9 %collective-permute-start.8 = (f32[512,256]{0,1:T(8,128)}, f32[512,256]{0,1:T(8,128)}, u32[]{:S(2)}, u32[]{:S(2)}) collective-permute-start(f32[512,256]{0,1:T(8,128)} %copy.37), channel_id=1, source_target_pairs={{0,2},{2,4},{4,6},{6,8},{8,10},{10,12},{12,14},{14,16},{16,18},{18... | collective-permute-start | bytes 1572872 | tf_op jit(solution)/shard_map/ppermute | solution.py:20
  283.3 400.8 %all-gather.9.cloned.1.call-start = ((), (), s32[]{:S(2)}) async-start(), calls=%async_computation.2 | async-start | bytes 1572864 | tf_op jit(solution)/shard_map/all_gather | solution.py:249
  513.7 20.8 %collective-permute-start.16 = (bf16[512,256]{0,1:T(8,128)(2,1)S(1)}, bf16[512,256]{0,1:T(8,128)(2,1)S(1)}, u32[]{:S(2)}, u32[]{:S(2)}) collective-permute-start(bf16[512,256]{0,1:T(8,128)(2,1)S(1)} %get-tuple-element.40), channel_id=1, source_target_pairs={{0,12},{2,14},{4,16},{6,18},{8,20},{10,22},{12,24},{14,26},{16,28}... | collective-permute-start | bytes 786440 | tf_op jit(solution)/shard_map/ppermute | solution.py:20
  518.8 21.2 %collective-permute-start.17 = (bf16[512,256]{0,1:T(8,128)(2,1)S(1)}, bf16[512,256]{0,1:T(8,128)(2,1)S(1)}, u32[]{:S(2)}, u32[]{:S(2)}) collective-permute-start(bf16[512,256]{0,1:T(8,128)(2,1)S(1)} %get-tuple-element.40), channel_id=1, source_target_pairs={{0,10},{2,12},{4,14},{6,16},{8,18},{10,20},{12,22},{14,24},{16,26}... | collective-permute-start | bytes 786440 | tf_op jit(solution)/shard_map/ppermute | solution.py:20
  522.4 23.2 %collective-permute-start.18 = (bf16[512,256]{0,1:T(8,128)(2,1)S(1)}, bf16[512,256]{0,1:T(8,128)(2,1)S(1)}, u32[]{:S(2)}, u32[]{:S(2)}) collective-permute-start(bf16[512,256]{0,1:T(8,128)(2,1)S(1)} %get-tuple-element.40), channel_id=1, source_target_pairs={{0,8},{2,10},{4,12},{6,14},{8,16},{10,18},{12,20},{14,22},{16,24},... | collective-permute-start | bytes 786440 | tf_op jit(solution)/shard_map/ppermute | solution.py:20
  525.1 24.9 %collective-permute-start.19 = (bf16[512,256]{0,1:T(8,128)(2,1)S(1)}, bf16[512,256]{0,1:T(8,128)(2,1)S(1)}, u32[]{:S(2)}, u32[]{:S(2)}) collective-permute-start(bf16[512,256]{0,1:T(8,128)(2,1)S(1)} %get-tuple-element.40), channel_id=1, source_target_pairs={{0,6},{2,8},{4,10},{6,12},{8,14},{10,16},{12,18},{14,20},{16,22},{... | collective-permute-start | bytes 786440 | tf_op jit(solution)/shard_map/ppermute | solution.py:20
  528.5 24.3 %collective-permute-start.20 = (bf16[512,256]{0,1:T(8,128)(2,1)S(1)}, bf16[512,256]{0,1:T(8,128)(2,1)S(1)}, u32[]{:S(2)}, u32[]{:S(2)}) collective-permute-start(bf16[512,256]{0,1:T(8,128)(2,1)S(1)} %get-tuple-element.40), channel_id=1, source_target_pairs={{0,4},{2,6},{4,8},{6,10},{8,12},{10,14},{12,16},{14,18},{16,20},{1... | collective-permute-start | bytes 786440 | tf_op jit(solution)/shard_map/ppermute | solution.py:20
  575.9 44.4 %collective-permute-start.31 = (f32[512,256]{0,1:T(8,128)}, f32[512,256]{0,1:T(8,128)}, u32[]{:S(2)}, u32[]{:S(2)}) collective-permute-start(f32[512,256]{0,1:T(8,128)} %copy.58), channel_id=1, source_target_pairs={{14,0},{16,2},{18,4},{20,6},{22,8},{24,10},{26,12},{28,14},{30,16}... | collective-permute-start | bytes 1572872 | tf_op jit(solution)/shard_map/ppermute | solution.py:20
  579.3 70.2 %collective-permute-start.30 = (f32[512,256]{0,1:T(8,128)}, f32[512,256]{0,1:T(8,128)}, u32[]{:S(2)}, u32[]{:S(2)}) collective-permute-start(f32[512,256]{0,1:T(8,128)} %copy.57), channel_id=1, source_target_pairs={{12,0},{14,2},{16,4},{18,6},{20,8},{22,10},{24,12},{26,14},{28,16}... | collective-permute-start | bytes 1572872 | tf_op jit(solution)/shard_map/ppermute | solution.py:20
  582.6 68.8 %collective-permute-start.29 = (f32[512,256]{0,1:T(8,128)}, f32[512,256]{0,1:T(8,128)}, u32[]{:S(2)}, u32[]{:S(2)}) collective-permute-start(f32[512,256]{0,1:T(8,128)} %copy.56), channel_id=1, source_target_pairs={{10,0},{12,2},{14,4},{16,6},{18,8},{20,10},{22,12},{24,14},{26,16}... | collective-permute-start | bytes 1572872 | tf_op jit(solution)/shard_map/ppermute | solution.py:20
  583.9 194.5 %all-gather.11.cloned.1.call-start = ((), (), s32[]{:S(2)}) async-start(), calls=%async_computation.3 | async-start | bytes 1572864 | tf_op jit(solution)/shard_map/all_gather | solution.py:261
  585.0 86.4 %collective-permute-start.28 = (f32[512,256]{0,1:T(8,128)}, f32[512,256]{0,1:T(8,128)S(1)}, u32[]{:S(2)}, u32[]{:S(2)}) collective-permute-start(f32[512,256]{0,1:T(8,128)} %copy.55), channel_id=1, source_target_pairs={{8,0},{10,2},{12,4},{14,6},{16,8},{18,10},{20,12},{22,14},{24,16},... | collective-permute-start | bytes 1572872 | tf_op jit(solution)/shard_map/ppermute | solution.py:20
  587.3 84.1 %collective-permute-start.27 = (f32[512,256]{0,1:T(8,128)}, f32[512,256]{0,1:T(8,128)S(1)}, u32[]{:S(2)}, u32[]{:S(2)}) collective-permute-start(f32[512,256]{0,1:T(8,128)} %copy.54), channel_id=1, source_target_pairs={{6,0},{8,2},{10,4},{12,6},{14,8},{16,10},{18,12},{20,14},{22,16},{... | collective-permute-start | bytes 1572872 | tf_op jit(solution)/shard_map/ppermute | solution.py:20
  620.4 52.3 %collective-permute-start.26 = (f32[512,256]{0,1:T(8,128)}, f32[512,256]{0,1:T(8,128)S(1)}, u32[]{:S(2)}, u32[]{:S(2)}) collective-permute-start(f32[512,256]{0,1:T(8,128)} %copy.53), channel_id=1, source_target_pairs={{4,0},{6,2},{8,4},{10,6},{12,8},{14,10},{16,12},{18,14},{20,16},{2... | collective-permute-start | bytes 1572872 | tf_op jit(solution)/shard_map/ppermute | solution.py:20
  649.4 23.3 %collective-permute-start.25 = (f32[512,256]{0,1:T(8,128)}, f32[512,256]{0,1:T(8,128)S(1)}, u32[]{:S(2)}, u32[]{:S(2)}) collective-permute-start(f32[512,256]{0,1:T(8,128)} %copy.52), channel_id=1, source_target_pairs={{2,0},{4,2},{6,4},{8,6},{10,8},{12,10},{14,12},{16,14},{18,16},{20... | collective-permute-start | bytes 1572872 | tf_op jit(solution)/shard_map/ppermute | solution.py:20
  651.3 30.6 %collective-permute-start.24 = (f32[512,256]{0,1:T(8,128)}, f32[512,256]{0,1:T(8,128)}, u32[]{:S(2)}, u32[]{:S(2)}) collective-permute-start(f32[512,256]{0,1:T(8,128)} %copy.50), channel_id=1, source_target_pairs={{0,2},{2,4},{4,6},{6,8},{8,10},{10,12},{12,14},{14,16},{16,18},{18... | collective-permute-start | bytes 1572872 | tf_op jit(solution)/shard_map/ppermute | solution.py:20
  (11 other events, 500.2 us)
Sparse Core Ops, SparseCore 0:
  89.0 59.1 all-gather.4
  283.4 11.7 all-gather.6
  584.0 51.9 all-gather.8
  767.3 11.0 all-gather.10

commit v6 on v5

--- a/solution.py
+++ b/solution.py
@@ -133,6 +133,83 @@
     return out.reshape(rows, cols)
 
 
+SHIFTS = (1, -1, -2, -3, -4, -5, -6, -7)
+
+
+def gather_partials(size, own_ref, parts_ref, out_ref, recv_ref, send_sems, recv_sems):
+    me = lax.axis_index("patch")
+    mesh_ids = pl.DeviceIdType.MESH
+    barrier = pltpu.get_barrier_semaphore()
+    targets = 0
+    for shift in SHIFTS:
+        source = me - shift
+        target = me + shift
+
+        @pl.when((source >= 0) & (source < size))
+        def _():
+            pl.semaphore_signal(barrier, 1, device_id={"patch": source}, device_id_type=mesh_ids)
+
+        targets = targets + ((target >= 0) & (target < size)).astype(jnp.int32)
+    for slot, shift in enumerate(SHIFTS):
+        source = me - shift
+
+        @pl.when((source < 0) | (source >= size))
+        def _():
+            recv_ref[slot] = jnp.zeros(recv_ref.shape[1:], recv_ref.dtype)
+
+    pl.semaphore_wait(barrier, targets)
+    copies = []
+    for slot, shift in enumerate(SHIFTS):
+        target = me + shift
+        source = me - shift
+        copy = pltpu.make_async_remote_copy(
+            src_ref=parts_ref.at[slot],
+            dst_ref=recv_ref.at[slot],
+            send_sem=send_sems.at[slot],
+            recv_sem=recv_sems.at[slot],
+            device_id={"patch": target},
+            device_id_type=mesh_ids,
+        )
+        sends = (target >= 0) & (target < size)
+        gets = (source >= 0) & (source < size)
+
+        @pl.when(sends)
+        def _():
+            copy.start()
+
+        copies.append((copy, sends, gets))
+    total = own_ref[...]
+    for slot, (copy, sends, gets) in enumerate(copies):
+
+        @pl.when(gets)
+        def _():
+            copy.wait_recv()
+
+        total = total + jnp.where(gets, recv_ref[slot], jnp.float32(0.0))
+    out_ref[...] = total
+    for copy, sends, gets in copies:
+
+        @pl.when(sends)
+        def _():
+            copy.wait_send()
+
+
+def summed_partials(own, parts):
+    size = lax.axis_size("patch")
+    return pl.pallas_call(
+        functools.partial(gather_partials, size),
+        out_shape=jax.ShapeDtypeStruct(own.shape, own.dtype),
+        in_specs=[pl.BlockSpec(memory_space=pltpu.VMEM)] * 2,
+        out_specs=pl.BlockSpec(memory_space=pltpu.VMEM),
+        scratch_shapes=[
+            pltpu.VMEM(parts.shape, parts.dtype),
+            pltpu.SemaphoreType.DMA((len(SHIFTS),)),
+            pltpu.SemaphoreType.DMA((len(SHIFTS),)),
+        ],
+        compiler_params=pltpu.CompilerParams(collective_id=2, has_side_effects=True),
+    )(own, parts)
+
+
 def tile_products(rows_ref, cols_ref, used_ref, tile_ref, x_ref, out_ref):
     slot = pl.program_id(0)
 
@@ -241,11 +318,12 @@
         segments = totals.reshape(8, dev_rows, col_width)
         zero_rows = jnp.zeros((dev_rows, col_width), jnp.float32)
         applied = jnp.where(parity == 0, segments[6], segments[7])
-        for offset in (1, -1, -2, -3, -4, -5, -6, -7):
+        outgoing = []
+        for offset in SHIFTS:
             lower_seg = segments[offset + 6] if 0 <= offset + 6 <= 7 else zero_rows
             upper_seg = segments[offset + 7] if 0 <= offset + 7 <= 7 else zero_rows
-            outgoing = jnp.where(parity == 0, lower_seg, upper_seg)
-            applied = applied + shifted(outgoing, "patch", offset)
+            outgoing.append(jnp.where(parity == 0, lower_seg, upper_seg))
+        applied = summed_partials(applied, jnp.stack(outgoing))
         current_all = lax.all_gather(current, "vec", axis=1, tiled=True)
         rayleigh = summed_over_patch(
             jnp.dot(

time: 1010 us -> 1100 us (1.089)
  Pallas kernels: 312 us -> 627 us
  waiting for transfers between devices: 193 us -> 61.1 us
  starting transfers between devices: 112 us -> 57.8 us
  local copies, waits for them, and re-layouts: 68.5 us -> 40.1 us
    pallas_call x0 -> x2, Pallas kernels: none -> 287 us  [summed_partials(): pl.pallas_call(functools.partial(gather_partials, size), out_shape=jax.Sh...]
    ppermute x32 -> x16, waiting for transfers between devices: 171 us -> 33.4 us  [shifted(): return lax.ppermute(block, axis, route)]
    ppermute x32 -> x16, starting transfers between devices: 112 us -> 57.2 us  [shifted(): return lax.ppermute(block, axis, route)]
    pallas_call x4, Pallas kernels: 285 us -> 326 us  [summed_over_patch(): pl.pallas_call(functools.partial(exchange_sum, size), out_shape=jax.Shape...]
    select_n x20 -> x0, local copies, waits for them, and re-layouts: 28.7 us -> none  [the longest x16 23.4 us: shards(): outgoing = jnp.where(parity == 0, lower_seg, upper_seg)]
    pallas_call x2, Pallas kernels: 27.4 us -> 13.6 us  [hessian_window(): pl.pallas_call(tile_products, grid_spec=grid_spec, out_shape=jax.ShapeDty...]
    another operation x27 -> x28, local copies, waits for them, and re-layouts: 24 us -> 15.2 us  [shards(): lax.linalg.triangular_solve(factor, update_all, left_side=False, lower=Tr...]
  transfers between devices with their start and end apart: 36 -> 20, of which waited for: 20 -> 12; matrix products, arithmetic and copies ran while one was open for 3% -> 2% of each run, Pallas kernels for 0% -> 28%
where the time goes in v6:
time: 1100 us; the launch traced here: 1090 us
  Pallas kernels  627 us (57%)
  other arithmetic  252 us (23%)
  waiting for transfers between devices  61.1 us (6%)
  starting transfers between devices  57.8 us (5%)
  local copies, waits for them, and re-layouts  40.1 us (4%)
  matrix products  28.1 us (3%)
  between operations  20.7 us (2%)
    pallas_call x4, Pallas kernels, summed_over_patch(): pl.pallas_call(functools.partial(exchange_sum, size), out_shape=jax.Shape...  326 us
    pallas_call x2, Pallas kernels, summed_partials(): pl.pallas_call(functools.partial(gather_partials, size), out_shape=jax.Sh...  287 us
    another operation x30, other arithmetic, shards(): factor = jnp.linalg.cholesky(gram_matrix)  159 us
    another operation x6, other arithmetic, shards(): lax.linalg.triangular_solve(factor, update_all, left_side=False, lower=Tr...  79.2 us
    ppermute x16, starting transfers between devices, shifted(): return lax.ppermute(block, axis, route)  57.2 us
    ppermute x16, waiting for transfers between devices, shifted(): return lax.ppermute(block, axis, route)  33.4 us
    all_gather x2, waiting for transfers between devices, shards(): update_all = lax.all_gather(update, 'vec', axis=1, tiled=True)  27.6 us
  transfers between devices with their start and end apart: 20, of which 12 were waited for; matrix products, arithmetic and copies ran while one was open for 2% of the time, Pallas kernels for 28%

profile of v6, /device:TPU:4, one launch (start us, length us, event | category | flops | bytes accessed | tf_op | source)
XLA Modules:
  0.0 1087.0 jit_solution(2414747814114057901)
XLA Ops:
  8.3 5.2 collective-permute-start.7
  13.5 6.0 collective-permute-start
  48.1 5.6 collective-permute-done.3
  60.2 6.8 shard_map.68
  77.1 151.7 %shard_map.69 = f32[512,256]{1,0:T(8,128)} custom-call(f32[512,256]{1,0:T(8,128)} %bitcast.181, f32[8,512,256]{2,1,0:T(8,128)} %bitcast_dynamic-update-slice_fusion.10.parts_ref), custom_call_target="tpu_custom_call" | custom-call | tf_op jit(solution)/shard_map/pallas_call | solution.py:199
  232.3 114.1 %shard_map.70 = f32[128,8,128]{2,1,0:T(8,128)} custom-call(f32[128,8,128]{2,1,0:T(8,128)} %reshape.391.x_ref), custom_call_target="tpu_custom_call" | custom-call | tf_op jit(solution)/shard_map/pallas_call | solution.py:119
  350.0 13.5 %all-gather.7.cloned.1.call-done = f32[512,512]{1,0:T(8,128)} async-done(((f32[512,256]{1,0:T(8,128)}), f32[512,512]{1,0:T(8,128)}) %all-gather.7.cloned.1.call-update) | async-done | bytes 1048592 | tf_op jit(solution)/shard_map/all_gather | solution.py:339
  367.9 60.7 %shard_map.71 = f32[128,16,128]{2,1,0:T(8,128)} custom-call(f32[128,16,128]{2,1,0:T(8,128)} %reshape.393.x_ref), custom_call_target="tpu_custom_call" | custom-call | tf_op jit(solution)/shard_map/pallas_call | solution.py:119
  430.6 11.7 %cholesky.286 = f32[128,128]{1,0:T(8,128)S(1)} custom-call(f32[128,128]{1,0:T(8,128)S(1)} %cholesky.426), custom_call_target="Cholesky" | custom-call | tf_op jit(solution)/shard_map/jit(cholesky)/cholesky | solution.py:347
  442.5 9.8 custom-call.27
  453.0 11.9 %cholesky.305 = f32[128,128]{1,0:T(8,128)S(1)} custom-call(f32[128,128]{1,0:T(8,128)S(1)} %cholesky.430), custom_call_target="Cholesky" | custom-call | tf_op jit(solution)/shard_map/jit(cholesky)/cholesky | solution.py:347
  464.9 9.8 custom-call.28
  475.4 11.7 %cholesky.326 = f32[128,128]{1,0:T(8,128)S(1)} custom-call(f32[128,128]{1,0:T(8,128)S(1)} %cholesky.435), custom_call_target="Cholesky" | custom-call | tf_op jit(solution)/shard_map/jit(cholesky)/cholesky | solution.py:347
  487.1 9.8 custom-call.29
  497.6 11.9 %cholesky.343 = f32[128,128]{1,0:T(8,128)S(1)} custom-call(f32[128,128]{1,0:T(8,128)S(1)} %convolution_subtract_fusion.12), custom_call_target="Cholesky" | custom-call | tf_op jit(solution)/shard_map/jit(cholesky)/cholesky | solution.py:347
  514.8 7.6 while.4
  522.4 39.3 %custom-call.30 = f32[4,128,128]{1,2,0:T(8,128)S(1)} custom-call(f32[4,128,128]{2,1,0:T(8,128)S(1)} %get-tuple-element.18), custom_call_target="InvertDiagBlocksLowerTriangular" | custom-call | tf_op jit(solution)/shard_map/triangular_solve/custom-call.3 | solution.py:348
  569.1 5.2 collective-permute-start.8
  611.1 6.8 shard_map.72
  628.0 135.5 %shard_map.73 = f32[512,256]{1,0:T(8,128)} custom-call(f32[512,256]{1,0:T(8,128)} %bitcast.180, f32[8,512,256]{2,1,0:T(8,128)} %bitcast_dynamic-update-slice_fusion.2.parts_ref), custom_call_target="tpu_custom_call" | custom-call | tf_op jit(solution)/shard_map/pallas_call | solution.py:199
  767.5 90.9 %shard_map.74 = f32[128,8,128]{2,1,0:T(8,128)} custom-call(f32[128,8,128]{2,1,0:T(8,128)} %reshape.395.x_ref), custom_call_target="tpu_custom_call" | custom-call | tf_op jit(solution)/shard_map/pallas_call | solution.py:119
  861.6 14.1 %all-gather.11.cloned.1.call-done = f32[512,512]{1,0:T(8,128)} async-done(((f32[512,256]{1,0:T(8,128)}), f32[512,512]{1,0:T(8,128)}) %all-gather.11.cloned.1.call-update) | async-done | bytes 1048592 | tf_op jit(solution)/shard_map/all_gather | solution.py:339
  880.1 60.7 %shard_map.75 = f32[128,16,128]{2,1,0:T(8,128)} custom-call(f32[128,16,128]{2,1,0:T(8,128)} %reshape.397.x_ref), custom_call_target="tpu_custom_call" | custom-call | tf_op jit(solution)/shard_map/pallas_call | solution.py:119
  942.8 11.7 %cholesky.358 = f32[128,128]{1,0:T(8,128)S(1)} custom-call(f32[128,128]{1,0:T(8,128)S(1)} %cholesky.439), custom_call_target="Cholesky" | custom-call | tf_op jit(solution)/shard_map/jit(cholesky)/cholesky | solution.py:347
  954.7 10.0 custom-call.31
  965.3 11.7 %cholesky.377 = f32[128,128]{1,0:T(8,128)S(1)} custom-call(f32[128,128]{1,0:T(8,128)S(1)} %cholesky.443), custom_call_target="Cholesky" | custom-call | tf_op jit(solution)/shard_map/jit(cholesky)/cholesky | solution.py:347
  977.1 9.8 custom-call.32
  987.6 11.9 %cholesky.398 = f32[128,128]{1,0:T(8,128)S(1)} custom-call(f32[128,128]{1,0:T(8,128)S(1)} %cholesky.448), custom_call_target="Cholesky" | custom-call | tf_op jit(solution)/shard_map/jit(cholesky)/cholesky | solution.py:347
  999.5 9.8 custom-call.33
  1009.9 11.7 %cholesky.415 = f32[128,128]{1,0:T(8,128)S(1)} custom-call(f32[128,128]{1,0:T(8,128)S(1)} %convolution_subtract_fusion.11), custom_call_target="Cholesky" | custom-call | tf_op jit(solution)/shard_map/jit(cholesky)/cholesky | solution.py:347
  1026.9 7.9 while.5
  1034.8 39.3 %custom-call.34 = f32[4,128,128]{1,2,0:T(8,128)S(1)} custom-call(f32[4,128,128]{2,1,0:T(8,128)S(1)} %get-tuple-element.19), custom_call_target="InvertDiagBlocksLowerTriangular" | custom-call | tf_op jit(solution)/shard_map/triangular_solve/custom-call.3 | solution.py:348
  (197 shorter events, 157.5 us)
Async XLA Ops:
  7.2 221.6 %all-gather.5.cloned.1.call-start = ((), (), s32[]{:S(2)}) async-start(), calls=%async_computation | async-start | bytes 1572864 | tf_op jit(solution)/shard_map/all_gather | solution.py:327
  8.3 25.0 %collective-permute-start.7 = (bf16[512,256]{1,0:T(8,128)(2,1)S(1)}, bf16[512,256]{1,0:T(8,128)(2,1)S(1)}, u32[]{:S(2)}, u32[]{:S(2)}) collective-permute-start(bf16[512,256]{1,0:T(8,128)(2,1)S(1)} %convert_element_type.6), channel_id=1, source_target_pairs={{0,14},{2,16},{4,18},{6,20},{8,22},{10,24},{12,26},{14,28},{16,30}... | collective-permute-start | bytes 786440 | tf_op jit(solution)/shard_map/ppermute | solution.py:20
  13.5 24.2 %collective-permute-start = (bf16[512,256]{1,0:T(8,128)(2,1)S(1)}, bf16[512,256]{1,0:T(8,128)(2,1)S(1)}, u32[]{:S(2)}, u32[]{:S(2)}) collective-permute-start(bf16[512,256]{1,0:T(8,128)(2,1)S(1)} %convert_element_type.6), channel_id=1, source_target_pairs={{0,12},{2,14},{4,16},{6,18},{8,20},{10,22},{12,24},{14,26},{16,28}... | collective-permute-start | bytes 786440 | tf_op jit(solution)/shard_map/ppermute | solution.py:20
  19.5 23.0 %collective-permute-start.1 = (bf16[512,256]{1,0:T(8,128)(2,1)S(1)}, bf16[512,256]{1,0:T(8,128)(2,1)S(1)}, u32[]{:S(2)}, u32[]{:S(2)}) collective-permute-start(bf16[512,256]{1,0:T(8,128)(2,1)S(1)} %convert_element_type.6), channel_id=1, source_target_pairs={{0,10},{2,12},{4,14},{6,16},{8,18},{10,20},{12,22},{14,24},{16,26}... | collective-permute-start | bytes 786440 | tf_op jit(solution)/shard_map/ppermute | solution.py:20
  24.3 23.8 %collective-permute-start.2 = (bf16[512,256]{1,0:T(8,128)(2,1)S(1)}, bf16[512,256]{1,0:T(8,128)(2,1)S(1)}, u32[]{:S(2)}, u32[]{:S(2)}) collective-permute-start(bf16[512,256]{1,0:T(8,128)(2,1)S(1)} %convert_element_type.6), channel_id=1, source_target_pairs={{0,8},{2,10},{4,12},{6,14},{8,16},{10,18},{12,20},{14,22},{16,24},... | collective-permute-start | bytes 786440 | tf_op jit(solution)/shard_map/ppermute | solution.py:20
  27.2 26.6 %collective-permute-start.3 = (bf16[512,256]{1,0:T(8,128)(2,1)S(1)}, bf16[512,256]{1,0:T(8,128)(2,1)S(1)}, u32[]{:S(2)}, u32[]{:S(2)}) collective-permute-start(bf16[512,256]{1,0:T(8,128)(2,1)S(1)} %convert_element_type.6), channel_id=1, source_target_pairs={{0,6},{2,8},{4,10},{6,12},{8,14},{10,16},{12,18},{14,20},{16,22},{... | collective-permute-start | bytes 786440 | tf_op jit(solution)/shard_map/ppermute | solution.py:20
  31.3 332.2 %all-gather.7.cloned.1.call-start = ((), (), s32[]{:S(2)}) async-start(), calls=%async_computation.1 | async-start | bytes 1572864 | tf_op jit(solution)/shard_map/all_gather | solution.py:339
  33.3 25.2 %collective-permute-start.4 = (bf16[512,256]{1,0:T(8,128)(2,1)S(1)}, bf16[512,256]{1,0:T(8,128)(2,1)S(1)}, u32[]{:S(2)}, u32[]{:S(2)}) collective-permute-start(bf16[512,256]{1,0:T(8,128)(2,1)S(1)} %convert_element_type.6), channel_id=1, source_target_pairs={{0,4},{2,6},{4,8},{6,10},{8,12},{10,14},{12,16},{14,18},{16,20},{1... | collective-permute-start | bytes 786440 | tf_op jit(solution)/shard_map/ppermute | solution.py:20
  37.7 20.8 %collective-permute-start.5 = (bf16[512,256]{1,0:T(8,128)(2,1)S(1)}, bf16[512,256]{1,0:T(8,128)(2,1)S(1)}, u32[]{:S(2)}, u32[]{:S(2)}) collective-permute-start(bf16[512,256]{1,0:T(8,128)(2,1)S(1)} %convert_element_type.6), channel_id=1, source_target_pairs={{0,2},{2,4},{4,6},{6,8},{8,10},{10,12},{12,14},{14,16},{16,18},{18... | collective-permute-start | bytes 786440 | tf_op jit(solution)/shard_map/ppermute | solution.py:20
  39.9 18.6 %copy-start.2 = (f32[512,256]{1,0:T(8,128)S(1)}, f32[512,256]{1,0:T(8,128)}, u32[]{:S(2)}) copy-start(f32[512,256]{1,0:T(8,128)} %param.8) | copy-start | bytes 1572868
  42.5 16.1 %collective-permute-start.6 = (bf16[512,256]{1,0:T(8,128)(2,1)S(1)}, bf16[512,256]{1,0:T(8,128)(2,1)S(1)}, u32[]{:S(2)}, u32[]{:S(2)}) collective-permute-start(bf16[512,256]{1,0:T(8,128)(2,1)S(1)} %convert_element_type.6), channel_id=1, source_target_pairs={{2,0},{4,2},{6,4},{8,6},{10,8},{12,10},{14,12},{16,14},{18,16},{20... | collective-permute-start | bytes 786440 | tf_op jit(solution)/shard_map/ppermute | solution.py:20
  231.2 116.4 %copy-start.5 = (f32[512,256]{1,0:T(8,128)S(1)}, f32[512,256]{1,0:T(8,128)}, u32[]{:S(2)}) copy-start(f32[512,256]{1,0:T(8,128)} %shard_map.69) | copy-start | bytes 1572868
  231.2 116.4 %copy-start.6 = (f32[512,512]{1,0:T(8,128)S(1)}, f32[512,512]{1,0:T(8,128)}, u32[]{:S(2)}) copy-start(f32[512,512]{1,0:T(8,128)} %all-gather.5.cloned.1.call-done) | copy-start | bytes 3145732
  349.4 414.0 %all-gather.9.cloned.1.call-start = ((), (), s32[]{:S(2)}) async-start(), calls=%async_computation.2 | async-start | bytes 1572864 | tf_op jit(solution)/shard_map/all_gather | solution.py:327
  475.4 86.3 %copy-start = (f32[512,512]{1,0:T(8,128)S(1)}, f32[512,512]{1,0:T(8,128)}, u32[]{:S(2)}) copy-start(f32[512,512]{1,0:T(8,128)} %all-gather.7.cloned.1.call-done) | copy-start | bytes 3145732
  566.4 17.7 %collective-permute-start.15 = (bf16[512,256]{1,0:T(8,128)(2,1)S(1)}, bf16[512,256]{1,0:T(8,128)(2,1)S(1)}, u32[]{:S(2)}, u32[]{:S(2)}) collective-permute-start(bf16[512,256]{1,0:T(8,128)(2,1)S(1)} %get-tuple-element.40), channel_id=1, source_target_pairs={{0,14},{2,16},{4,18},{6,20},{8,22},{10,24},{12,26},{14,28},{16,30}... | collective-permute-start | bytes 786440 | tf_op jit(solution)/shard_map/ppermute | solution.py:20
  569.1 20.8 %collective-permute-start.8 = (bf16[512,256]{1,0:T(8,128)(2,1)S(1)}, bf16[512,256]{1,0:T(8,128)(2,1)S(1)}, u32[]{:S(2)}, u32[]{:S(2)}) collective-permute-start(bf16[512,256]{1,0:T(8,128)(2,1)S(1)} %get-tuple-element.40), channel_id=1, source_target_pairs={{0,12},{2,14},{4,16},{6,18},{8,20},{10,22},{12,24},{14,26},{16,28}... | collective-permute-start | bytes 786440 | tf_op jit(solution)/shard_map/ppermute | solution.py:20
  574.3 21.2 %collective-permute-start.9 = (bf16[512,256]{1,0:T(8,128)(2,1)S(1)}, bf16[512,256]{1,0:T(8,128)(2,1)S(1)}, u32[]{:S(2)}, u32[]{:S(2)}) collective-permute-start(bf16[512,256]{1,0:T(8,128)(2,1)S(1)} %get-tuple-element.40), channel_id=1, source_target_pairs={{0,10},{2,12},{4,14},{6,16},{8,18},{10,20},{12,22},{14,24},{16,26}... | collective-permute-start | bytes 786440 | tf_op jit(solution)/shard_map/ppermute | solution.py:20
  577.9 23.2 %collective-permute-start.10 = (bf16[512,256]{1,0:T(8,128)(2,1)S(1)}, bf16[512,256]{1,0:T(8,128)(2,1)S(1)}, u32[]{:S(2)}, u32[]{:S(2)}) collective-permute-start(bf16[512,256]{1,0:T(8,128)(2,1)S(1)} %get-tuple-element.40), channel_id=1, source_target_pairs={{0,8},{2,10},{4,12},{6,14},{8,16},{10,18},{12,20},{14,22},{16,24},... | collective-permute-start | bytes 786440 | tf_op jit(solution)/shard_map/ppermute | solution.py:20
  580.5 24.9 %collective-permute-start.11 = (bf16[512,256]{1,0:T(8,128)(2,1)S(1)}, bf16[512,256]{1,0:T(8,128)(2,1)S(1)}, u32[]{:S(2)}, u32[]{:S(2)}) collective-permute-start(bf16[512,256]{1,0:T(8,128)(2,1)S(1)} %get-tuple-element.40), channel_id=1, source_target_pairs={{0,6},{2,8},{4,10},{6,12},{8,14},{10,16},{12,18},{14,20},{16,22},{... | collective-permute-start | bytes 786440 | tf_op jit(solution)/shard_map/ppermute | solution.py:20
  584.0 291.7 %all-gather.11.cloned.1.call-start = ((), (), s32[]{:S(2)}) async-start(), calls=%async_computation.3 | async-start | bytes 1572864 | tf_op jit(solution)/shard_map/all_gather | solution.py:339
  584.0 24.3 %collective-permute-start.12 = (bf16[512,256]{1,0:T(8,128)(2,1)S(1)}, bf16[512,256]{1,0:T(8,128)(2,1)S(1)}, u32[]{:S(2)}, u32[]{:S(2)}) collective-permute-start(bf16[512,256]{1,0:T(8,128)(2,1)S(1)} %get-tuple-element.40), channel_id=1, source_target_pairs={{0,4},{2,6},{4,8},{6,10},{8,12},{10,14},{12,16},{14,18},{16,20},{1... | collective-permute-start | bytes 786440 | tf_op jit(solution)/shard_map/ppermute | solution.py:20
  589.9 18.5 %collective-permute-start.13 = (bf16[512,256]{1,0:T(8,128)(2,1)S(1)}, bf16[512,256]{1,0:T(8,128)(2,1)S(1)}, u32[]{:S(2)}, u32[]{:S(2)}) collective-permute-start(bf16[512,256]{1,0:T(8,128)(2,1)S(1)} %get-tuple-element.40), channel_id=1, source_target_pairs={{0,2},{2,4},{4,6},{6,8},{8,10},{10,12},{12,14},{14,16},{16,18},{18... | collective-permute-start | bytes 786440 | tf_op jit(solution)/shard_map/ppermute | solution.py:20
  595.5 14.0 %collective-permute-start.14 = (bf16[512,256]{1,0:T(8,128)(2,1)S(1)}, bf16[512,256]{1,0:T(8,128)(2,1)S(1)}, u32[]{:S(2)}, u32[]{:S(2)}) collective-permute-start(bf16[512,256]{1,0:T(8,128)(2,1)S(1)} %get-tuple-element.40), channel_id=1, source_target_pairs={{2,0},{4,2},{6,4},{8,6},{10,8},{12,10},{14,12},{16,14},{18,16},{20... | collective-permute-start | bytes 786440 | tf_op jit(solution)/shard_map/ppermute | solution.py:20
  766.6 92.9 %copy-start.3 = (f32[512,256]{1,0:T(8,128)S(1)}, f32[512,256]{1,0:T(8,128)}, u32[]{:S(2)}) copy-start(f32[512,256]{1,0:T(8,128)} %shard_map.73) | copy-start | bytes 1572868
  766.6 92.9 %copy-start.4 = (f32[512,256]{1,0:T(8,128)S(1)}, f32[512,256]{1,0:T(8,128)}, u32[]{:S(2)}) copy-start(f32[512,256]{1,0:T(8,128)} %get-tuple-element.41) | copy-start | bytes 1572868
  766.6 92.9 %copy-start.7 = (f32[512,512]{1,0:T(8,128)S(1)}, f32[512,512]{1,0:T(8,128)}, u32[]{:S(2)}) copy-start(f32[512,512]{1,0:T(8,128)} %all-gather.9.cloned.1.call-done) | copy-start | bytes 3145732
  987.5 86.6 %copy-start.1 = (f32[512,512]{1,0:T(8,128)S(1)}, f32[512,512]{1,0:T(8,128)}, u32[]{:S(2)}) copy-start(f32[512,512]{1,0:T(8,128)} %all-gather.11.cloned.1.call-done) | copy-start | bytes 3145732
Sparse Core Ops, SparseCore 0:
  31.4 13.4 all-gather.4
  349.5 13.8 all-gather.6
  584.1 13.4 all-gather.8
  861.7 13.9 all-gather.10

commit v7 on v5

--- a/solution.py
+++ b/solution.py
@@ -133,7 +133,7 @@
     return out.reshape(rows, cols)
 
 
-def tile_products(rows_ref, cols_ref, used_ref, tile_ref, x_ref, out_ref):
+def tile_products(part, base, rows_ref, cols_ref, used_ref, tile_ref, x_ref, out_ref):
     slot = pl.program_id(0)
 
     @pl.when(slot == 0)
@@ -146,17 +146,19 @@
         col = cols_ref[slot]
         tile = tile_ref[0]
         weight = jnp.where(row == col, jnp.float32(0.5), jnp.float32(1.0))
-        direct = jnp.dot(tile, x_ref[col], preferred_element_type=jnp.float32)
-        out_ref[row] += direct * weight
-        mirror = lax.dot_general(
-            tile, x_ref[row], (((0,), (0,)), ((), ())), preferred_element_type=jnp.float32
-        )
-        out_ref[col] += mirror * weight
-
-
-def hessian_window(window_x, blocks, rows_local, cols_local, used):
+        if part == "direct":
+            direct = jnp.dot(tile, x_ref[col], preferred_element_type=jnp.float32)
+            out_ref[row] += direct * weight
+        else:
+            mirror = lax.dot_general(
+                tile, x_ref[row - base], (((0,), (0,)), ((), ())), preferred_element_type=jnp.float32
+            )
+            out_ref[col] += mirror * weight
+
+
+def hessian_window(window_x, blocks, rows_local, cols_local, used, part, window_tiles):
     slots, tile_size, _ = blocks.shape
-    window_tiles, _, col_width = window_x.shape
+    held_tiles, _, col_width = window_x.shape
 
     def tile_at(slot, rows, cols, used_ref):
         return (jnp.maximum(jnp.minimum(slot, used_ref[0] - 1), 0), 0, 0)
@@ -169,13 +171,13 @@
         grid=(slots,),
         in_specs=[
             pl.BlockSpec((1, tile_size, tile_size), tile_at),
-            pl.BlockSpec((window_tiles, tile_size, col_width), whole),
+            pl.BlockSpec((held_tiles, tile_size, col_width), whole),
         ],
         out_specs=pl.BlockSpec((window_tiles, tile_size, col_width), whole),
     )
-    flops = 4 * slots * tile_size * tile_size * col_width
+    flops = 2 * slots * tile_size * tile_size * col_width
     return pl.pallas_call(
-        tile_products,
+        functools.partial(tile_products, part, window_tiles - held_tiles),
         grid_spec=grid_spec,
         out_shape=jax.ShapeDtypeStruct((window_tiles, tile_size, col_width), jnp.float32),
         compiler_params=pltpu.CompilerParams(dimension_semantics=("arbitrary",)),
@@ -235,15 +237,23 @@
         lower_side = jnp.concatenate([pieces[6 - segment] for segment in range(8)], axis=0)
         upper_side = jnp.concatenate([pieces[7 - segment] for segment in range(8)], axis=0)
         window_x = jnp.where(parity == 0, lower_side, upper_side).reshape(16, tile_size, col_width)
-        totals = hessian_window(
-            window_x, blocks, block_row - window_start, block_col - window_start, block_count
-        )
-        segments = totals.reshape(8, dev_rows, col_width)
+        near_x = jnp.where(
+            parity == 0,
+            jnp.concatenate([pieces[0], pieces[-1]], axis=0),
+            jnp.concatenate([pieces[1], pieces[0]], axis=0),
+        ).reshape(4, tile_size, col_width)
+        rows_local = block_row - window_start
+        cols_local = block_col - window_start
+        mirrored = hessian_window(near_x, blocks, rows_local, cols_local, block_count, "mirror", 16)
+        directed = hessian_window(window_x, blocks, rows_local, cols_local, block_count, "direct", 16)
+        far = mirrored.reshape(8, dev_rows, col_width)
+        segments = (mirrored + directed).reshape(8, dev_rows, col_width)
         zero_rows = jnp.zeros((dev_rows, col_width), jnp.float32)
         applied = jnp.where(parity == 0, segments[6], segments[7])
         for offset in (1, -1, -2, -3, -4, -5, -6, -7):
-            lower_seg = segments[offset + 6] if 0 <= offset + 6 <= 7 else zero_rows
-            upper_seg = segments[offset + 7] if 0 <= offset + 7 <= 7 else zero_rows
+            source = segments if offset >= -1 else far
+            lower_seg = source[offset + 6] if 0 <= offset + 6 <= 7 else zero_rows
+            upper_seg = source[offset + 7] if 0 <= offset + 7 <= 7 else zero_rows
             outgoing = jnp.where(parity == 0, lower_seg, upper_seg)
             applied = applied + shifted(outgoing, "patch", offset)
         current_all = lax.all_gather(current, "vec", axis=1, tiled=True)

time: 1010 us -> 1100 us (1.089)
  waiting for transfers between devices: 193 us -> 282 us
  starting transfers between devices: 112 us -> 146 us
  Pallas kernels: 312 us -> 295 us
  matrix products: 38.6 us -> 26 us
    ppermute x32, waiting for transfers between devices: 171 us -> 258 us  [shifted(): return lax.ppermute(block, axis, route)]
    ppermute x32, starting transfers between devices: 112 us -> 145 us  [shifted(): return lax.ppermute(block, axis, route)]
    pallas_call x4, Pallas kernels: 285 us -> 269 us  [summed_over_patch(): pl.pallas_call(functools.partial(exchange_sum, size), out_shape=jax.Shape...]
    pallas_call x2 -> x4, Pallas kernels: 27.4 us -> 26.4 us  [hessian_window(): pl.pallas_call(functools.partial(tile_products, part, window_tiles - held...]
  transfers between devices with their start and end apart: 36 -> 36, of which waited for: 20 -> 21; matrix products, arithmetic and copies ran while one was open for 3% -> 2% of each run, Pallas kernels for 0% -> 0%
where the time goes in v7:
time: 1100 us; the launch traced here: 1090 us
  Pallas kernels  295 us (27%)
  waiting for transfers between devices  282 us (26%)
  other arithmetic  260 us (24%)
  starting transfers between devices  146 us (13%)
  local copies, waits for them, and re-layouts  60.1 us (5%)
  matrix products  26 us (2%)
  between operations  20.8 us (2%)
    pallas_call x4, Pallas kernels, summed_over_patch(): pl.pallas_call(functools.partial(exchange_sum, size), out_shape=jax.Shape...  269 us
    ppermute x32, waiting for transfers between devices, shifted(): return lax.ppermute(block, axis, route)  258 us
    another operation x30, other arithmetic, shards(): factor = jnp.linalg.cholesky(gram_matrix)  159 us
    ppermute x32, starting transfers between devices, shifted(): return lax.ppermute(block, axis, route)  145 us
    another operation x6, other arithmetic, shards(): lax.linalg.triangular_solve(factor, update_all, left_side=False, lower=Tr...  79.2 us
    pallas_call x4, Pallas kernels, hessian_window(): pl.pallas_call(functools.partial(tile_products, part, window_tiles - held...  26.4 us
    all_gather x2, waiting for transfers between devices, shards(): update_all = lax.all_gather(update, 'vec', axis=1, tiled=True)  23.9 us
  transfers between devices with their start and end apart: 36, of which 21 were waited for; matrix products, arithmetic and copies ran while one was open for 2% of the time, Pallas kernels for 0%

profile of v7, /device:TPU:4, one launch (start us, length us, event | category | flops | bytes accessed | tf_op | source)
XLA Modules:
  0.0 1090.5 jit_solution(14617747624294562052)
XLA Ops:
  85.4 34.2 %collective-permute-start.8 = (f32[512,256]{0,1:T(8,128)}, f32[512,256]{0,1:T(8,128)}, u32[]{:S(2)}, u32[]{:S(2)}) collective-permute-start(f32[512,256]{0,1:T(8,128)} %copy.40), channel_id=1, source_target_pairs={{0,2},{2,4},{4,6},{6,8},{8,10},{10,12},{12,14},{14,16},{16,18},{18... | collective-permute-start | bytes 1572872 | tf_op jit(solution)/shard_map/ppermute | solution.py:20
  136.5 21.9 %collective-permute-done.9 = f32[512,256]{0,1:T(8,128)} collective-permute-done((f32[512,256]{0,1:T(8,128)}, f32[512,256]{0,1:T(8,128)}, u32[]{:S(2)}, u32[]{:S(2)}) %collective-permute-start.9) | collective-permute-done | bytes 524320 | tf_op jit(solution)/shard_map/ppermute | solution.py:20
  159.7 23.9 %collective-permute-done.10 = f32[512,256]{0,1:T(8,128)} collective-permute-done((f32[512,256]{0,1:T(8,128)}, f32[512,256]{0,1:T(8,128)}, u32[]{:S(2)}, u32[]{:S(2)}) %collective-permute-start.10) | collective-permute-done | bytes 524320 | tf_op jit(solution)/shard_map/ppermute | solution.py:20
  189.3 70.8 %collective-permute-done.14 = f32[512,256]{0,1:T(8,128)S(1)} collective-permute-done((f32[512,256]{0,1:T(8,128)}, f32[512,256]{0,1:T(8,128)S(1)}, u32[]{:S(2)}, u32[]{:S(2)}) %collective-permute-start.14) | collective-permute-done | bytes 524320 | tf_op jit(solution)/shard_map/ppermute | solution.py:20
  266.6 74.7 %shard_map.70 = f32[128,8,128]{2,1,0:T(8,128)} custom-call(f32[128,8,128]{2,1,0:T(8,128)} %reshape.163.x_ref), custom_call_target="tpu_custom_call" | custom-call | tf_op jit(solution)/shard_map/pallas_call | solution.py:119
  345.5 11.8 %all-gather.7.cloned.1.call-done = f32[512,512]{0,1:T(8,128)} async-done(((f32[512,256]{0,1:T(8,128)}), f32[512,512]{0,1:T(8,128)}) %all-gather.7.cloned.1.call-update) | async-done | bytes 1048592 | tf_op jit(solution)/shard_map/all_gather | solution.py:271
  361.8 60.7 %shard_map.71 = f32[128,16,128]{2,1,0:T(8,128)} custom-call(f32[128,16,128]{2,1,0:T(8,128)} %reshape.165.x_ref), custom_call_target="tpu_custom_call" | custom-call | tf_op jit(solution)/shard_map/pallas_call | solution.py:119
  424.6 11.7 %cholesky.286 = f32[128,128]{1,0:T(8,128)S(1)} custom-call(f32[128,128]{1,0:T(8,128)S(1)} %cholesky.426), custom_call_target="Cholesky" | custom-call | tf_op jit(solution)/shard_map/jit(cholesky)/cholesky | solution.py:279
  436.4 9.8 custom-call.27
  446.9 12.1 %cholesky.305 = f32[128,128]{1,0:T(8,128)S(1)} custom-call(f32[128,128]{1,0:T(8,128)S(1)} %cholesky.430), custom_call_target="Cholesky" | custom-call | tf_op jit(solution)/shard_map/jit(cholesky)/cholesky | solution.py:279
  460.3 9.8 custom-call.28
  470.8 11.7 %cholesky.326 = f32[128,128]{1,0:T(8,128)S(1)} custom-call(f32[128,128]{1,0:T(8,128)S(1)} %cholesky.435), custom_call_target="Cholesky" | custom-call | tf_op jit(solution)/shard_map/jit(cholesky)/cholesky | solution.py:279
  483.2 9.8 custom-call.29
  493.6 11.9 %cholesky.343 = f32[128,128]{1,0:T(8,128)S(1)} custom-call(f32[128,128]{1,0:T(8,128)S(1)} %convolution_subtract_fusion.9), custom_call_target="Cholesky" | custom-call | tf_op jit(solution)/shard_map/jit(cholesky)/cholesky | solution.py:279
  508.8 7.6 while.4
  516.5 39.3 %custom-call.30 = f32[4,128,128]{1,2,0:T(8,128)S(1)} custom-call(f32[4,128,128]{2,1,0:T(8,128)S(1)} %get-tuple-element.18), custom_call_target="InvertDiagBlocksLowerTriangular" | custom-call | tf_op jit(solution)/shard_map/triangular_solve/custom-call.3 | solution.py:280
  629.7 33.2 %collective-permute-start.24 = (f32[512,256]{0,1:T(8,128)}, f32[512,256]{0,1:T(8,128)}, u32[]{:S(2)}, u32[]{:S(2)}) collective-permute-start(f32[512,256]{0,1:T(8,128)} %copy.54), channel_id=1, source_target_pairs={{0,2},{2,4},{4,6},{6,8},{8,10},{10,12},{12,14},{14,16},{16,18},{18... | collective-permute-start | bytes 1572872 | tf_op jit(solution)/shard_map/ppermute | solution.py:20
  678.8 23.0 %collective-permute-done.25 = f32[512,256]{0,1:T(8,128)} collective-permute-done((f32[512,256]{0,1:T(8,128)}, f32[512,256]{0,1:T(8,128)}, u32[]{:S(2)}, u32[]{:S(2)}) %collective-permute-start.25) | collective-permute-done | bytes 524320 | tf_op jit(solution)/shard_map/ppermute | solution.py:20
  703.1 17.3 %collective-permute-done.26 = f32[512,256]{0,1:T(8,128)S(1)} collective-permute-done((f32[512,256]{0,1:T(8,128)}, f32[512,256]{0,1:T(8,128)S(1)}, u32[]{:S(2)}, u32[]{:S(2)}) %collective-permute-start.26) | collective-permute-done | bytes 524320 | tf_op jit(solution)/shard_map/ppermute | solution.py:20
  725.9 59.9 %collective-permute-done.30 = f32[512,256]{0,1:T(8,128)S(1)} collective-permute-done((f32[512,256]{0,1:T(8,128)}, f32[512,256]{0,1:T(8,128)S(1)}, u32[]{:S(2)}, u32[]{:S(2)}) %collective-permute-start.30) | collective-permute-done | bytes 524320 | tf_op jit(solution)/shard_map/ppermute | solution.py:20
  792.0 72.4 %shard_map.74 = f32[128,8,128]{2,1,0:T(8,128)} custom-call(f32[128,8,128]{2,1,0:T(8,128)} %reshape.167.x_ref), custom_call_target="tpu_custom_call" | custom-call | tf_op jit(solution)/shard_map/pallas_call | solution.py:119
  868.6 12.1 %all-gather.11.cloned.1.call-done = f32[512,512]{0,1:T(8,128)} async-done(((f32[512,256]{0,1:T(8,128)}), f32[512,512]{0,1:T(8,128)}) %all-gather.11.cloned.1.call-update) | async-done | bytes 1048592 | tf_op jit(solution)/shard_map/all_gather | solution.py:271
  885.1 60.7 %shard_map.75 = f32[128,16,128]{2,1,0:T(8,128)} custom-call(f32[128,16,128]{2,1,0:T(8,128)} %reshape.169.x_ref), custom_call_target="tpu_custom_call" | custom-call | tf_op jit(solution)/shard_map/pallas_call | solution.py:119
  947.9 11.7 %cholesky.358 = f32[128,128]{1,0:T(8,128)S(1)} custom-call(f32[128,128]{1,0:T(8,128)S(1)} %cholesky.439), custom_call_target="Cholesky" | custom-call | tf_op jit(solution)/shard_map/jit(cholesky)/cholesky | solution.py:279
  959.7 9.9 custom-call.31
  970.3 11.7 %cholesky.377 = f32[128,128]{1,0:T(8,128)S(1)} custom-call(f32[128,128]{1,0:T(8,128)S(1)} %cholesky.443), custom_call_target="Cholesky" | custom-call | tf_op jit(solution)/shard_map/jit(cholesky)/cholesky | solution.py:279
  983.3 9.8 custom-call.32
  993.8 11.9 %cholesky.398 = f32[128,128]{1,0:T(8,128)S(1)} custom-call(f32[128,128]{1,0:T(8,128)S(1)} %cholesky.448), custom_call_target="Cholesky" | custom-call | tf_op jit(solution)/shard_map/jit(cholesky)/cholesky | solution.py:279
  1006.4 9.8 custom-call.33
  1016.9 11.7 %cholesky.415 = f32[128,128]{1,0:T(8,128)S(1)} custom-call(f32[128,128]{1,0:T(8,128)S(1)} %convolution_subtract_fusion.8), custom_call_target="Cholesky" | custom-call | tf_op jit(solution)/shard_map/jit(cholesky)/cholesky | solution.py:279
  1031.9 7.9 while.5
  1039.8 39.3 %custom-call.34 = f32[4,128,128]{1,2,0:T(8,128)S(1)} custom-call(f32[4,128,128]{2,1,0:T(8,128)S(1)} %get-tuple-element.19), custom_call_target="InvertDiagBlocksLowerTriangular" | custom-call | tf_op jit(solution)/shard_map/triangular_solve/custom-call.3 | solution.py:280
  (250 shorter events, 260.5 us)
Async XLA Ops:
  7.2 256.1 %all-gather.5.cloned.1.call-start = ((), (), s32[]{:S(2)}) async-start(), calls=%async_computation | async-start | bytes 1572864 | tf_op jit(solution)/shard_map/all_gather | solution.py:259
  8.5 24.9 %collective-permute-start.7 = (bf16[512,256]{0,1:T(8,128)(2,1)S(1)}, bf16[512,256]{0,1:T(8,128)(2,1)S(1)}, u32[]{:S(2)}, u32[]{:S(2)}) collective-permute-start(bf16[512,256]{0,1:T(8,128)(2,1)S(1)} %convert_element_type.6), channel_id=1, source_target_pairs={{0,14},{2,16},{4,18},{6,20},{8,22},{10,24},{12,26},{14,28},{16,30}... | collective-permute-start | bytes 786440 | tf_op jit(solution)/shard_map/ppermute | solution.py:20
  13.7 24.1 %collective-permute-start.2 = (bf16[512,256]{0,1:T(8,128)(2,1)S(1)}, bf16[512,256]{0,1:T(8,128)(2,1)S(1)}, u32[]{:S(2)}, u32[]{:S(2)}) collective-permute-start(bf16[512,256]{0,1:T(8,128)(2,1)S(1)} %convert_element_type.6), channel_id=1, source_target_pairs={{0,12},{2,14},{4,16},{6,18},{8,20},{10,22},{12,24},{14,26},{16,28}... | collective-permute-start | bytes 786440 | tf_op jit(solution)/shard_map/ppermute | solution.py:20
  19.7 23.0 %collective-permute-start.3 = (bf16[512,256]{0,1:T(8,128)(2,1)S(1)}, bf16[512,256]{0,1:T(8,128)(2,1)S(1)}, u32[]{:S(2)}, u32[]{:S(2)}) collective-permute-start(bf16[512,256]{0,1:T(8,128)(2,1)S(1)} %convert_element_type.6), channel_id=1, source_target_pairs={{0,10},{2,12},{4,14},{6,16},{8,18},{10,20},{12,22},{14,24},{16,26}... | collective-permute-start | bytes 786440 | tf_op jit(solution)/shard_map/ppermute | solution.py:20
  24.5 23.8 %collective-permute-start.4 = (bf16[512,256]{0,1:T(8,128)(2,1)S(1)}, bf16[512,256]{0,1:T(8,128)(2,1)S(1)}, u32[]{:S(2)}, u32[]{:S(2)}) collective-permute-start(bf16[512,256]{0,1:T(8,128)(2,1)S(1)} %convert_element_type.6), channel_id=1, source_target_pairs={{0,8},{2,10},{4,12},{6,14},{8,16},{10,18},{12,20},{14,22},{16,24},... | collective-permute-start | bytes 786440 | tf_op jit(solution)/shard_map/ppermute | solution.py:20
  27.4 26.6 %collective-permute-start.5 = (bf16[512,256]{0,1:T(8,128)(2,1)S(1)}, bf16[512,256]{0,1:T(8,128)(2,1)S(1)}, u32[]{:S(2)}, u32[]{:S(2)}) collective-permute-start(bf16[512,256]{0,1:T(8,128)(2,1)S(1)} %convert_element_type.6), channel_id=1, source_target_pairs={{0,6},{2,8},{4,10},{6,12},{8,14},{10,16},{12,18},{14,20},{16,22},{... | collective-permute-start | bytes 786440 | tf_op jit(solution)/shard_map/ppermute | solution.py:20
  33.4 25.2 %collective-permute-start.6 = (bf16[512,256]{0,1:T(8,128)(2,1)S(1)}, bf16[512,256]{0,1:T(8,128)(2,1)S(1)}, u32[]{:S(2)}, u32[]{:S(2)}) collective-permute-start(bf16[512,256]{0,1:T(8,128)(2,1)S(1)} %convert_element_type.6), channel_id=1, source_target_pairs={{0,4},{2,6},{4,8},{6,10},{8,12},{10,14},{12,16},{14,18},{16,20},{1... | collective-permute-start | bytes 786440 | tf_op jit(solution)/shard_map/ppermute | solution.py:20
  37.8 20.9 %collective-permute-start.1 = (bf16[512,256]{0,1:T(8,128)(2,1)S(1)}, bf16[512,256]{0,1:T(8,128)(2,1)S(1)}, u32[]{:S(2)}, u32[]{:S(2)}) collective-permute-start(bf16[512,256]{0,1:T(8,128)(2,1)S(1)} %convert_element_type.6), channel_id=1, source_target_pairs={{0,2},{2,4},{4,6},{6,8},{8,10},{10,12},{12,14},{14,16},{16,18},{18... | collective-permute-start | bytes 786440 | tf_op jit(solution)/shard_map/ppermute | solution.py:20
  85.4 49.8 %collective-permute-start.8 = (f32[512,256]{0,1:T(8,128)}, f32[512,256]{0,1:T(8,128)}, u32[]{:S(2)}, u32[]{:S(2)}) collective-permute-start(f32[512,256]{0,1:T(8,128)} %copy.40), channel_id=1, source_target_pairs={{0,2},{2,4},{4,6},{6,8},{8,10},{10,12},{12,14},{14,16},{16,18},{18... | collective-permute-start | bytes 1572872 | tf_op jit(solution)/shard_map/ppermute | solution.py:20
  121.6 36.8 %collective-permute-start.9 = (f32[512,256]{0,1:T(8,128)}, f32[512,256]{0,1:T(8,128)}, u32[]{:S(2)}, u32[]{:S(2)}) collective-permute-start(f32[512,256]{0,1:T(8,128)} %copy.42), channel_id=1, source_target_pairs={{2,0},{4,2},{6,4},{8,6},{10,8},{12,10},{14,12},{16,14},{18,16},{20... | collective-permute-start | bytes 1572872 | tf_op jit(solution)/shard_map/ppermute | solution.py:20
  125.5 58.1 %collective-permute-start.10 = (f32[512,256]{0,1:T(8,128)}, f32[512,256]{0,1:T(8,128)}, u32[]{:S(2)}, u32[]{:S(2)}) collective-permute-start(f32[512,256]{0,1:T(8,128)} %copy.43), channel_id=1, source_target_pairs={{4,0},{6,2},{8,4},{10,6},{12,8},{14,10},{16,12},{18,14},{20,16},{2... | collective-permute-start | bytes 1572872 | tf_op jit(solution)/shard_map/ppermute | solution.py:20
  127.5 229.8 %all-gather.7.cloned.1.call-start = ((), (), s32[]{:S(2)}) async-start(), calls=%async_computation.1 | async-start | bytes 1572864 | tf_op jit(solution)/shard_map/all_gather | solution.py:271
  128.6 60.7 %collective-permute-start.11 = (f32[512,256]{0,1:T(8,128)}, f32[512,256]{0,1:T(8,128)}, u32[]{:S(2)}, u32[]{:S(2)}) collective-permute-start(f32[512,256]{0,1:T(8,128)} %copy.44), channel_id=1, source_target_pairs={{6,0},{8,2},{10,4},{12,6},{14,8},{16,10},{18,12},{20,14},{22,16},{... | collective-permute-start | bytes 1572872 | tf_op jit(solution)/shard_map/ppermute | solution.py:20
  130.9 58.4 %collective-permute-start.12 = (f32[512,256]{0,1:T(8,128)}, f32[512,256]{0,1:T(8,128)S(1)}, u32[]{:S(2)}, u32[]{:S(2)}) collective-permute-start(f32[512,256]{0,1:T(8,128)} %copy.45), channel_id=1, source_target_pairs={{8,0},{10,2},{12,4},{14,6},{16,8},{18,10},{20,12},{22,14},{24,16},... | collective-permute-start | bytes 1572872 | tf_op jit(solution)/shard_map/ppermute | solution.py:20
  135.2 54.1 %collective-permute-start.13 = (f32[512,256]{0,1:T(8,128)}, f32[512,256]{0,1:T(8,128)S(1)}, u32[]{:S(2)}, u32[]{:S(2)}) collective-permute-start(f32[512,256]{0,1:T(8,128)} %copy.46), channel_id=1, source_target_pairs={{10,0},{12,2},{14,4},{16,6},{18,8},{20,10},{22,12},{24,14},{26,16}... | collective-permute-start | bytes 1572872 | tf_op jit(solution)/shard_map/ppermute | solution.py:20
  158.4 101.7 %collective-permute-start.14 = (f32[512,256]{0,1:T(8,128)}, f32[512,256]{0,1:T(8,128)S(1)}, u32[]{:S(2)}, u32[]{:S(2)}) collective-permute-start(f32[512,256]{0,1:T(8,128)} %copy.47), channel_id=1, source_target_pairs={{12,0},{14,2},{16,4},{18,6},{20,8},{22,10},{24,12},{26,14},{28,16}... | collective-permute-start | bytes 1572872 | tf_op jit(solution)/shard_map/ppermute | solution.py:20
  183.6 77.3 %collective-permute-start.15 = (f32[512,256]{0,1:T(8,128)}, f32[512,256]{0,1:T(8,128)}, u32[]{:S(2)}, u32[]{:S(2)}) collective-permute-start(f32[512,256]{0,1:T(8,128)} %copy.48), channel_id=1, source_target_pairs={{14,0},{16,2},{18,4},{20,6},{22,8},{24,10},{26,12},{28,14},{30,16}... | collective-permute-start | bytes 1572872 | tf_op jit(solution)/shard_map/ppermute | solution.py:20
  345.2 443.7 %all-gather.9.cloned.1.call-start = ((), (), s32[]{:S(2)}) async-start(), calls=%async_computation.2 | async-start | bytes 1572864 | tf_op jit(solution)/shard_map/all_gather | solution.py:259
  562.9 20.8 %collective-permute-start.18 = (bf16[512,256]{0,1:T(8,128)(2,1)S(1)}, bf16[512,256]{0,1:T(8,128)(2,1)S(1)}, u32[]{:S(2)}, u32[]{:S(2)}) collective-permute-start(bf16[512,256]{0,1:T(8,128)(2,1)S(1)} %get-tuple-element.40), channel_id=1, source_target_pairs={{0,12},{2,14},{4,16},{6,18},{8,20},{10,22},{12,24},{14,26},{16,28}... | collective-permute-start | bytes 786440 | tf_op jit(solution)/shard_map/ppermute | solution.py:20
  568.0 21.2 %collective-permute-start.19 = (bf16[512,256]{0,1:T(8,128)(2,1)S(1)}, bf16[512,256]{0,1:T(8,128)(2,1)S(1)}, u32[]{:S(2)}, u32[]{:S(2)}) collective-permute-start(bf16[512,256]{0,1:T(8,128)(2,1)S(1)} %get-tuple-element.40), channel_id=1, source_target_pairs={{0,10},{2,12},{4,14},{6,16},{8,18},{10,20},{12,22},{14,24},{16,26}... | collective-permute-start | bytes 786440 | tf_op jit(solution)/shard_map/ppermute | solution.py:20
  571.6 23.2 %collective-permute-start.20 = (bf16[512,256]{0,1:T(8,128)(2,1)S(1)}, bf16[512,256]{0,1:T(8,128)(2,1)S(1)}, u32[]{:S(2)}, u32[]{:S(2)}) collective-permute-start(bf16[512,256]{0,1:T(8,128)(2,1)S(1)} %get-tuple-element.40), channel_id=1, source_target_pairs={{0,8},{2,10},{4,12},{6,14},{8,16},{10,18},{12,20},{14,22},{16,24},... | collective-permute-start | bytes 786440 | tf_op jit(solution)/shard_map/ppermute | solution.py:20
  574.3 24.9 %collective-permute-start.21 = (bf16[512,256]{0,1:T(8,128)(2,1)S(1)}, bf16[512,256]{0,1:T(8,128)(2,1)S(1)}, u32[]{:S(2)}, u32[]{:S(2)}) collective-permute-start(bf16[512,256]{0,1:T(8,128)(2,1)S(1)} %get-tuple-element.40), channel_id=1, source_target_pairs={{0,6},{2,8},{4,10},{6,12},{8,14},{10,16},{12,18},{14,20},{16,22},{... | collective-permute-start | bytes 786440 | tf_op jit(solution)/shard_map/ppermute | solution.py:20
  577.7 24.3 %collective-permute-start.22 = (bf16[512,256]{0,1:T(8,128)(2,1)S(1)}, bf16[512,256]{0,1:T(8,128)(2,1)S(1)}, u32[]{:S(2)}, u32[]{:S(2)}) collective-permute-start(bf16[512,256]{0,1:T(8,128)(2,1)S(1)} %get-tuple-element.40), channel_id=1, source_target_pairs={{0,4},{2,6},{4,8},{6,10},{8,12},{10,14},{12,16},{14,18},{16,20},{1... | collective-permute-start | bytes 786440 | tf_op jit(solution)/shard_map/ppermute | solution.py:20
  629.7 47.9 %collective-permute-start.24 = (f32[512,256]{0,1:T(8,128)}, f32[512,256]{0,1:T(8,128)}, u32[]{:S(2)}, u32[]{:S(2)}) collective-permute-start(f32[512,256]{0,1:T(8,128)} %copy.54), channel_id=1, source_target_pairs={{0,2},{2,4},{4,6},{6,8},{8,10},{10,12},{12,14},{14,16},{16,18},{18... | collective-permute-start | bytes 1572872 | tf_op jit(solution)/shard_map/ppermute | solution.py:20
  665.0 36.8 %collective-permute-start.25 = (f32[512,256]{0,1:T(8,128)}, f32[512,256]{0,1:T(8,128)}, u32[]{:S(2)}, u32[]{:S(2)}) collective-permute-start(f32[512,256]{0,1:T(8,128)} %copy.56), channel_id=1, source_target_pairs={{2,0},{4,2},{6,4},{8,6},{10,8},{12,10},{14,12},{16,14},{18,16},{20... | collective-permute-start | bytes 1572872 | tf_op jit(solution)/shard_map/ppermute | solution.py:20
  667.9 52.5 %collective-permute-start.26 = (f32[512,256]{0,1:T(8,128)}, f32[512,256]{0,1:T(8,128)S(1)}, u32[]{:S(2)}, u32[]{:S(2)}) collective-permute-start(f32[512,256]{0,1:T(8,128)} %copy.57), channel_id=1, source_target_pairs={{4,0},{6,2},{8,4},{10,6},{12,8},{14,10},{16,12},{18,14},{20,16},{2... | collective-permute-start | bytes 1572872 | tf_op jit(solution)/shard_map/ppermute | solution.py:20
  669.8 210.8 %all-gather.11.cloned.1.call-start = ((), (), s32[]{:S(2)}) async-start(), calls=%async_computation.3 | async-start | bytes 1572864 | tf_op jit(solution)/shard_map/all_gather | solution.py:271
  670.9 53.7 %collective-permute-start.27 = (f32[512,256]{0,1:T(8,128)}, f32[512,256]{0,1:T(8,128)}, u32[]{:S(2)}, u32[]{:S(2)}) collective-permute-start(f32[512,256]{0,1:T(8,128)} %copy.58), channel_id=1, source_target_pairs={{6,0},{8,2},{10,4},{12,6},{14,8},{16,10},{18,12},{20,14},{22,16},{... | collective-permute-start | bytes 1572872 | tf_op jit(solution)/shard_map/ppermute | solution.py:20
  673.2 51.4 %collective-permute-start.28 = (f32[512,256]{0,1:T(8,128)}, f32[512,256]{0,1:T(8,128)S(1)}, u32[]{:S(2)}, u32[]{:S(2)}) collective-permute-start(f32[512,256]{0,1:T(8,128)} %copy.59), channel_id=1, source_target_pairs={{8,0},{10,2},{12,4},{14,6},{16,8},{18,10},{20,12},{22,14},{24,16},... | collective-permute-start | bytes 1572872 | tf_op jit(solution)/shard_map/ppermute | solution.py:20
  677.5 48.4 %collective-permute-start.29 = (f32[512,256]{0,1:T(8,128)}, f32[512,256]{0,1:T(8,128)S(1)}, u32[]{:S(2)}, u32[]{:S(2)}) collective-permute-start(f32[512,256]{0,1:T(8,128)} %copy.60), channel_id=1, source_target_pairs={{10,0},{12,2},{14,4},{16,6},{18,8},{20,10},{22,12},{24,14},{26,16}... | collective-permute-start | bytes 1572872 | tf_op jit(solution)/shard_map/ppermute | solution.py:20
  701.8 84.0 %collective-permute-start.30 = (f32[512,256]{0,1:T(8,128)}, f32[512,256]{0,1:T(8,128)S(1)}, u32[]{:S(2)}, u32[]{:S(2)}) collective-permute-start(f32[512,256]{0,1:T(8,128)} %copy.61), channel_id=1, source_target_pairs={{12,0},{14,2},{16,4},{18,6},{20,8},{22,10},{24,12},{26,14},{28,16}... | collective-permute-start | bytes 1572872 | tf_op jit(solution)/shard_map/ppermute | solution.py:20
  720.4 66.2 %collective-permute-start.31 = (f32[512,256]{0,1:T(8,128)}, f32[512,256]{0,1:T(8,128)}, u32[]{:S(2)}, u32[]{:S(2)}) collective-permute-start(f32[512,256]{0,1:T(8,128)} %copy.62), channel_id=1, source_target_pairs={{14,0},{16,2},{18,4},{20,6},{22,8},{24,10},{26,12},{28,14},{30,16}... | collective-permute-start | bytes 1572872 | tf_op jit(solution)/shard_map/ppermute | solution.py:20
  (15 other events, 575.0 us)
Sparse Core Ops, SparseCore 0:
  127.6 54.1 all-gather.4
  345.4 11.9 all-gather.6
  670.0 50.4 all-gather.8
  867.7 12.8 all-gather.10

commit v8 on v5

--- a/solution.py
+++ b/solution.py
@@ -20,12 +20,12 @@
     return lax.ppermute(block, axis, route)
 
 
-GROUPS = ((0, 2), (2, 2), (5, 2), (4, 1))
-
-
-def digit_groups(size):
+GROUP_ORDERS = (((0, 2), (5, 2), (2, 2), (4, 1)), ((5, 2), (0, 2), (2, 2), (4, 1)))
+
+
+def digit_groups(size, order=0):
     nbits = size.bit_length() - 1
-    return [(low, min(width, nbits - low)) for low, width in GROUPS if low < nbits]
+    return [(low, min(width, nbits - low)) for low, width in GROUP_ORDERS[order] if low < nbits]
 
 
 def flipped(digit, e, width):
@@ -57,6 +57,29 @@
             greeted += 1
     pl.semaphore_wait(barrier, greeted)
     work_ref[...] = x_ref[...]
+    reduce_and_spread = functools.partial(
+        exchange_body, me, work_ref, recv_ref, final_ref, send_sems, recv_sems
+    )
+    core = lax.axis_index("vec")
+    for order in range(len(GROUP_ORDERS)):
+
+        @pl.when(core % len(GROUP_ORDERS) == order)
+        def _():
+            reduce_and_spread(digit_groups(size, order))
+
+    out_ref[...] = final_ref[...]
+
+
+def exchange_body(me, work_ref, recv_ref, final_ref, send_sems, recv_sems, groups):
+    mesh_ids = pl.DeviceIdType.MESH
+
+    def digit_of(low, width):
+        return (me // (1 << low)) % (1 << width)
+
+    def partner_of(low, width, e):
+        digit = digit_of(low, width)
+        return me + (flipped(digit, e, width) - digit) * (1 << low)
+
     lo = 0
     span = work_ref.shape[0]
     recv_at = 0
@@ -108,7 +131,6 @@
             copy.wait()
         lo = lo - digit * span
         span = span * ways
-    out_ref[...] = final_ref[...]
 
 
 def summed_over_patch(block, collective):

time: 1010 us -> 1010 us (level)
  waiting for transfers between devices: 193 us -> 175 us
  Pallas kernels: 312 us -> 323 us
    ppermute x32, waiting for transfers between devices: 171 us -> 148 us  [shifted(): return lax.ppermute(block, axis, route)]
  transfers between devices with their start and end apart: 36 -> 36, of which waited for: 20 -> 18; matrix products, arithmetic and copies ran while one was open for 3% -> 3% of each run, Pallas kernels for 0% -> 0%
where the time goes in v8:
time: 1010 us; the launch traced here: 998 us
  Pallas kernels  323 us (32%)
  other arithmetic  264 us (26%)
  waiting for transfers between devices  175 us (17%)
  starting transfers between devices  108 us (11%)
  local copies, waits for them, and re-layouts  68.5 us (7%)
  matrix products  38.6 us (4%)
  between operations  21.2 us (2%)
    pallas_call x4, Pallas kernels, summed_over_patch(): pl.pallas_call(functools.partial(exchange_sum, size), out_shape=jax.Shape...  289 us
    another operation x30, other arithmetic, shards(): factor = jnp.linalg.cholesky(gram_matrix)  168 us
    ppermute x32, waiting for transfers between devices, shifted(): return lax.ppermute(block, axis, route)  148 us
    ppermute x32, starting transfers between devices, shifted(): return lax.ppermute(block, axis, route)  107 us
    another operation x6, other arithmetic, shards(): lax.linalg.triangular_solve(factor, update_all, left_side=False, lower=Tr...  81.1 us
    pallas_call x2, Pallas kernels, hessian_window(): pl.pallas_call(tile_products, grid_spec=grid_spec, out_shape=jax.ShapeDty...  34.7 us
    all_gather x2, waiting for transfers between devices, shards(): update_all = lax.all_gather(update, 'vec', axis=1, tiled=True)  26.1 us
    another operation x27, local copies, waits for them, and re-layouts, shards(): lax.linalg.triangular_solve(factor, update_all, left_side=False, lower=Tr...  24 us
  transfers between devices with their start and end apart: 36, of which 18 were waited for; matrix products, arithmetic and copies ran while one was open for 3% of the time, Pallas kernels for 0%

profile of v8, /device:TPU:4, one launch (start us, length us, event | category | flops | bytes accessed | tf_op | source)
XLA Modules:
  0.0 997.6 jit_solution(5282964855889098700)
XLA Ops:
  61.5 17.4 %shard_map.68 = f32[16,256,256]{2,1,0:T(8,128)} custom-call(s32[64]{0:T(128)} %get-tuple-element.119.rows_ref, s32[64]{0:T(128)} %get-tuple-element.118.cols_ref, s32[1]{0:T(128)S(6)} %copy.121.used_ref, bf16[64,256,256]{2,1,0:T(8,128)(2,1)} %tile_ref.3, bf16[16,256,256]{2,1,0:T(8,128)(2,1)} %bitcast.162), custom_call_target="tpu_custom_call" | custom-call | flops 4294967296 | bytes 14680064 | tf_op jit(solution)/shard_map/pallas_call | solution.py:199
  101.3 25.2 %collective-permute-done.15 = f32[512,256]{0,1:T(8,128)} collective-permute-done((f32[512,256]{0,1:T(8,128)}, f32[512,256]{0,1:T(8,128)}, u32[]{:S(2)}, u32[]{:S(2)}) %collective-permute-start.15) | collective-permute-done | bytes 524320 | tf_op jit(solution)/shard_map/ppermute | solution.py:20
  128.4 26.4 %collective-permute-done.14 = f32[512,256]{0,1:T(8,128)} collective-permute-done((f32[512,256]{0,1:T(8,128)}, f32[512,256]{0,1:T(8,128)}, u32[]{:S(2)}, u32[]{:S(2)}) %collective-permute-start.14) | collective-permute-done | bytes 524320 | tf_op jit(solution)/shard_map/ppermute | solution.py:20
  156.7 13.9 %collective-permute-start.8 = (f32[512,256]{0,1:T(8,128)}, f32[512,256]{0,1:T(8,128)}, u32[]{:S(2)}, u32[]{:S(2)}) collective-permute-start(f32[512,256]{0,1:T(8,128)} %copy.37), channel_id=1, source_target_pairs={{0,2},{2,4},{4,6},{6,8},{8,10},{10,12},{12,14},{14,16},{16,18},{18... | collective-permute-start | bytes 1572872 | tf_op jit(solution)/shard_map/ppermute | solution.py:20
  189.0 85.6 %shard_map.69 = f32[128,8,128]{2,1,0:T(8,128)} custom-call(f32[128,8,128]{2,1,0:T(8,128)} %reshape.147.x_ref), custom_call_target="tpu_custom_call" | custom-call | tf_op jit(solution)/shard_map/pallas_call | solution.py:141
  278.9 13.4 %all-gather.7.cloned.1.call-done = f32[512,512]{0,1:T(8,128)} async-done(((f32[512,256]{0,1:T(8,128)}), f32[512,512]{0,1:T(8,128)}) %all-gather.7.cloned.1.call-update) | async-done | bytes 1048592 | tf_op jit(solution)/shard_map/all_gather | solution.py:283
  296.8 57.0 %shard_map.70 = f32[128,16,128]{2,1,0:T(8,128)} custom-call(f32[128,16,128]{2,1,0:T(8,128)} %reshape.149.x_ref), custom_call_target="tpu_custom_call" | custom-call | tf_op jit(solution)/shard_map/pallas_call | solution.py:141
  356.7 11.7 %cholesky.286 = f32[128,128]{1,0:T(8,128)S(1)} custom-call(f32[128,128]{1,0:T(8,128)S(1)} %cholesky.426), custom_call_target="Cholesky" | custom-call | tf_op jit(solution)/shard_map/jit(cholesky)/cholesky | solution.py:291
  368.6 9.8 custom-call.27
  381.0 11.7 %cholesky.305 = f32[128,128]{1,0:T(8,128)S(1)} custom-call(f32[128,128]{1,0:T(8,128)S(1)} %cholesky.430), custom_call_target="Cholesky" | custom-call | tf_op jit(solution)/shard_map/jit(cholesky)/cholesky | solution.py:291
  392.7 18.5 %custom-call.28 = f32[1,128,128]{1,2,0:T(8,128)S(1)} custom-call(f32[1,128,128]{2,1,0:T(8,128)S(1)} %get-tuple-element.108), custom_call_target="InvertDiagBlocksLowerTriangular" | custom-call | tf_op jit(solution)/shard_map/jit(cholesky)/cholesky | solution.py:291
  412.8 11.7 %cholesky.326 = f32[128,128]{1,0:T(8,128)S(1)} custom-call(f32[128,128]{1,0:T(8,128)S(1)} %cholesky.435), custom_call_target="Cholesky" | custom-call | tf_op jit(solution)/shard_map/jit(cholesky)/cholesky | solution.py:291
  424.6 9.8 custom-call.29
  435.8 12.1 %cholesky.343 = f32[128,128]{1,0:T(8,128)S(1)} custom-call(f32[128,128]{1,0:T(8,128)S(1)} %convolution_subtract_fusion.9), custom_call_target="Cholesky" | custom-call | tf_op jit(solution)/shard_map/jit(cholesky)/cholesky | solution.py:291
  454.3 12.0 %while.4 = (s32[]{:T(128)}, f32[512,512]{1,0:T(8,128)}, s32[4,2]{0,1:T(2,128)S(1)}, f32[4,128,128]{2,1,0:T(8,128)S(1)}, s32[]{:T(128)}) while((s32[]{:T(128)}, f32[512,512]{1,0:T(8,128)}, s32[4,2]{0,1:T(2,128)S(1)}, f32[4,128,128]{2,1,0:T(8,128)S(1)}, s32[]{:T(128)}) %tuple.89), condition=%wide.while_cond, body=%wide.while_body.sunk | while | flops 2 | bytes 131189 | solution.py:292
  466.4 39.3 %custom-call.30 = f32[4,128,128]{1,2,0:T(8,128)S(1)} custom-call(f32[4,128,128]{2,1,0:T(8,128)S(1)} %get-tuple-element.18), custom_call_target="InvertDiagBlocksLowerTriangular" | custom-call | tf_op jit(solution)/shard_map/triangular_solve/custom-call.3 | solution.py:292
  555.0 17.4 %shard_map.71 = f32[16,256,256]{2,1,0:T(8,128)} custom-call(s32[64]{0:T(128)} %get-tuple-element.119.rows_ref, s32[64]{0:T(128)} %get-tuple-element.118.cols_ref, s32[1]{0:T(128)S(6)} %copy.121.used_ref, bf16[64,256,256]{2,1,0:T(8,128)(2,1)} %tile_ref.3, bf16[16,256,256]{2,1,0:T(8,128)(2,1)} %bitcast.161), custom_call_target="tpu_custom_call" | custom-call | flops 4294967296 | bytes 14680064 | tf_op jit(solution)/shard_map/pallas_call | solution.py:199
  593.5 35.7 %collective-permute-done.31 = f32[512,256]{0,1:T(8,128)} collective-permute-done((f32[512,256]{0,1:T(8,128)}, f32[512,256]{0,1:T(8,128)}, u32[]{:S(2)}, u32[]{:S(2)}) %collective-permute-start.31) | collective-permute-done | bytes 524320 | tf_op jit(solution)/shard_map/ppermute | solution.py:20
  631.0 12.8 %collective-permute-done.30 = f32[512,256]{0,1:T(8,128)} collective-permute-done((f32[512,256]{0,1:T(8,128)}, f32[512,256]{0,1:T(8,128)}, u32[]{:S(2)}, u32[]{:S(2)}) %collective-permute-start.30) | collective-permute-done | bytes 524320 | tf_op jit(solution)/shard_map/ppermute | solution.py:20
  645.8 14.2 %collective-permute-start.24 = (f32[512,256]{0,1:T(8,128)}, f32[512,256]{0,1:T(8,128)}, u32[]{:S(2)}, u32[]{:S(2)}) collective-permute-start(f32[512,256]{0,1:T(8,128)} %copy.50), channel_id=1, source_target_pairs={{0,2},{2,4},{4,6},{6,8},{8,10},{10,12},{12,14},{14,16},{16,18},{18... | collective-permute-start | bytes 1572872 | tf_op jit(solution)/shard_map/ppermute | solution.py:20
  672.8 88.8 %shard_map.72 = f32[128,8,128]{2,1,0:T(8,128)} custom-call(f32[128,8,128]{2,1,0:T(8,128)} %reshape.151.x_ref), custom_call_target="tpu_custom_call" | custom-call | tf_op jit(solution)/shard_map/pallas_call | solution.py:141
  765.8 12.7 %all-gather.11.cloned.1.call-done = f32[512,512]{0,1:T(8,128)} async-done(((f32[512,256]{0,1:T(8,128)}), f32[512,512]{0,1:T(8,128)}) %all-gather.11.cloned.1.call-update) | async-done | bytes 1048592 | tf_op jit(solution)/shard_map/all_gather | solution.py:283
  783.0 57.1 %shard_map.73 = f32[128,16,128]{2,1,0:T(8,128)} custom-call(f32[128,16,128]{2,1,0:T(8,128)} %reshape.153.x_ref), custom_call_target="tpu_custom_call" | custom-call | tf_op jit(solution)/shard_map/pallas_call | solution.py:141
  843.1 11.7 %cholesky.358 = f32[128,128]{1,0:T(8,128)S(1)} custom-call(f32[128,128]{1,0:T(8,128)S(1)} %cholesky.439), custom_call_target="Cholesky" | custom-call | tf_op jit(solution)/shard_map/jit(cholesky)/cholesky | solution.py:291
  855.0 9.8 custom-call.31
  867.3 11.7 %cholesky.377 = f32[128,128]{1,0:T(8,128)S(1)} custom-call(f32[128,128]{1,0:T(8,128)S(1)} %cholesky.443), custom_call_target="Cholesky" | custom-call | tf_op jit(solution)/shard_map/jit(cholesky)/cholesky | solution.py:291
  879.1 10.0 %custom-call.32 = f32[1,128,128]{1,2,0:T(8,128)S(1)} custom-call(f32[1,128,128]{2,1,0:T(8,128)S(1)} %get-tuple-element.98), custom_call_target="InvertDiagBlocksLowerTriangular" | custom-call | tf_op jit(solution)/shard_map/jit(cholesky)/cholesky | solution.py:291
  890.7 11.7 %cholesky.398 = f32[128,128]{1,0:T(8,128)S(1)} custom-call(f32[128,128]{1,0:T(8,128)S(1)} %cholesky.448), custom_call_target="Cholesky" | custom-call | tf_op jit(solution)/shard_map/jit(cholesky)/cholesky | solution.py:291
  902.4 9.8 custom-call.33
  913.7 11.9 %cholesky.415 = f32[128,128]{1,0:T(8,128)S(1)} custom-call(f32[128,128]{1,0:T(8,128)S(1)} %convolution_subtract_fusion.8), custom_call_target="Cholesky" | custom-call | tf_op jit(solution)/shard_map/jit(cholesky)/cholesky | solution.py:291
  932.0 12.0 %while.5 = (s32[]{:T(128)}, f32[512,512]{1,0:T(8,128)}, s32[4,2]{0,1:T(2,128)S(1)}, f32[4,128,128]{2,1,0:T(8,128)S(1)}, s32[]{:T(128)}) while((s32[]{:T(128)}, f32[512,512]{1,0:T(8,128)}, s32[4,2]{0,1:T(2,128)S(1)}, f32[4,128,128]{2,1,0:T(8,128)S(1)}, s32[]{:T(128)}) %tuple.103), condition=%wide.while_cond.clone, body=%wide.while_body.clone.sunk | while | flops 2 | bytes 131189 | solution.py:292
  944.1 39.3 %custom-call.34 = f32[4,128,128]{1,2,0:T(8,128)S(1)} custom-call(f32[4,128,128]{2,1,0:T(8,128)S(1)} %get-tuple-element.19), custom_call_target="InvertDiagBlocksLowerTriangular" | custom-call | tf_op jit(solution)/shard_map/triangular_solve/custom-call.3 | solution.py:292
  (232 shorter events, 257.9 us)
Async XLA Ops:
  7.2 178.5 %all-gather.5.cloned.1.call-start = ((), (), s32[]{:S(2)}) async-start(), calls=%async_computation | async-start | bytes 1572864 | tf_op jit(solution)/shard_map/all_gather | solution.py:271
  8.5 24.9 %collective-permute-start.7 = (bf16[512,256]{0,1:T(8,128)(2,1)S(1)}, bf16[512,256]{0,1:T(8,128)(2,1)S(1)}, u32[]{:S(2)}, u32[]{:S(2)}) collective-permute-start(bf16[512,256]{0,1:T(8,128)(2,1)S(1)} %convert_element_type.6), channel_id=1, source_target_pairs={{0,14},{2,16},{4,18},{6,20},{8,22},{10,24},{12,26},{14,28},{16,30}... | collective-permute-start | bytes 786440 | tf_op jit(solution)/shard_map/ppermute | solution.py:20
  13.7 24.1 %collective-permute-start = (bf16[512,256]{0,1:T(8,128)(2,1)S(1)}, bf16[512,256]{0,1:T(8,128)(2,1)S(1)}, u32[]{:S(2)}, u32[]{:S(2)}) collective-permute-start(bf16[512,256]{0,1:T(8,128)(2,1)S(1)} %convert_element_type.6), channel_id=1, source_target_pairs={{0,12},{2,14},{4,16},{6,18},{8,20},{10,22},{12,24},{14,26},{16,28}... | collective-permute-start | bytes 786440 | tf_op jit(solution)/shard_map/ppermute | solution.py:20
  19.7 23.0 %collective-permute-start.1 = (bf16[512,256]{0,1:T(8,128)(2,1)S(1)}, bf16[512,256]{0,1:T(8,128)(2,1)S(1)}, u32[]{:S(2)}, u32[]{:S(2)}) collective-permute-start(bf16[512,256]{0,1:T(8,128)(2,1)S(1)} %convert_element_type.6), channel_id=1, source_target_pairs={{0,10},{2,12},{4,14},{6,16},{8,18},{10,20},{12,22},{14,24},{16,26}... | collective-permute-start | bytes 786440 | tf_op jit(solution)/shard_map/ppermute | solution.py:20
  24.5 23.8 %collective-permute-start.2 = (bf16[512,256]{0,1:T(8,128)(2,1)S(1)}, bf16[512,256]{0,1:T(8,128)(2,1)S(1)}, u32[]{:S(2)}, u32[]{:S(2)}) collective-permute-start(bf16[512,256]{0,1:T(8,128)(2,1)S(1)} %convert_element_type.6), channel_id=1, source_target_pairs={{0,8},{2,10},{4,12},{6,14},{8,16},{10,18},{12,20},{14,22},{16,24},... | collective-permute-start | bytes 786440 | tf_op jit(solution)/shard_map/ppermute | solution.py:20
  27.4 26.6 %collective-permute-start.3 = (bf16[512,256]{0,1:T(8,128)(2,1)S(1)}, bf16[512,256]{0,1:T(8,128)(2,1)S(1)}, u32[]{:S(2)}, u32[]{:S(2)}) collective-permute-start(bf16[512,256]{0,1:T(8,128)(2,1)S(1)} %convert_element_type.6), channel_id=1, source_target_pairs={{0,6},{2,8},{4,10},{6,12},{8,14},{10,16},{12,18},{14,20},{16,22},{... | collective-permute-start | bytes 786440 | tf_op jit(solution)/shard_map/ppermute | solution.py:20
  33.4 25.2 %collective-permute-start.4 = (bf16[512,256]{0,1:T(8,128)(2,1)S(1)}, bf16[512,256]{0,1:T(8,128)(2,1)S(1)}, u32[]{:S(2)}, u32[]{:S(2)}) collective-permute-start(bf16[512,256]{0,1:T(8,128)(2,1)S(1)} %convert_element_type.6), channel_id=1, source_target_pairs={{0,4},{2,6},{4,8},{6,10},{8,12},{10,14},{12,16},{14,18},{16,20},{1... | collective-permute-start | bytes 786440 | tf_op jit(solution)/shard_map/ppermute | solution.py:20
  37.8 20.9 %collective-permute-start.5 = (bf16[512,256]{0,1:T(8,128)(2,1)S(1)}, bf16[512,256]{0,1:T(8,128)(2,1)S(1)}, u32[]{:S(2)}, u32[]{:S(2)}) collective-permute-start(bf16[512,256]{0,1:T(8,128)(2,1)S(1)} %convert_element_type.6), channel_id=1, source_target_pairs={{0,2},{2,4},{4,6},{6,8},{8,10},{10,12},{12,14},{14,16},{16,18},{18... | collective-permute-start | bytes 786440 | tf_op jit(solution)/shard_map/ppermute | solution.py:20
  84.6 41.9 %collective-permute-start.15 = (f32[512,256]{0,1:T(8,128)}, f32[512,256]{0,1:T(8,128)}, u32[]{:S(2)}, u32[]{:S(2)}) collective-permute-start(f32[512,256]{0,1:T(8,128)} %copy.45), channel_id=1, source_target_pairs={{14,0},{16,2},{18,4},{20,6},{22,8},{24,10},{26,12},{28,14},{30,16}... | collective-permute-start | bytes 1572872 | tf_op jit(solution)/shard_map/ppermute | solution.py:20
  87.9 66.9 %collective-permute-start.14 = (f32[512,256]{0,1:T(8,128)}, f32[512,256]{0,1:T(8,128)}, u32[]{:S(2)}, u32[]{:S(2)}) collective-permute-start(f32[512,256]{0,1:T(8,128)} %copy.44), channel_id=1, source_target_pairs={{12,0},{14,2},{16,4},{18,6},{20,8},{22,10},{24,12},{26,14},{28,16}... | collective-permute-start | bytes 1572872 | tf_op jit(solution)/shard_map/ppermute | solution.py:20
  91.2 65.5 %collective-permute-start.13 = (f32[512,256]{0,1:T(8,128)}, f32[512,256]{0,1:T(8,128)}, u32[]{:S(2)}, u32[]{:S(2)}) collective-permute-start(f32[512,256]{0,1:T(8,128)} %copy.43), channel_id=1, source_target_pairs={{10,0},{12,2},{14,4},{16,6},{18,8},{20,10},{22,12},{24,14},{26,16}... | collective-permute-start | bytes 1572872 | tf_op jit(solution)/shard_map/ppermute | solution.py:20
  92.5 199.7 %all-gather.7.cloned.1.call-start = ((), (), s32[]{:S(2)}) async-start(), calls=%async_computation.1 | async-start | bytes 1572864 | tf_op jit(solution)/shard_map/all_gather | solution.py:283
  94.6 76.3 %collective-permute-start.12 = (f32[512,256]{0,1:T(8,128)}, f32[512,256]{0,1:T(8,128)}, u32[]{:S(2)}, u32[]{:S(2)}) collective-permute-start(f32[512,256]{0,1:T(8,128)} %copy.42), channel_id=1, source_target_pairs={{8,0},{10,2},{12,4},{14,6},{16,8},{18,10},{20,12},{22,14},{24,16},... | collective-permute-start | bytes 1572872 | tf_op jit(solution)/shard_map/ppermute | solution.py:20
  97.0 74.0 %collective-permute-start.11 = (f32[512,256]{0,1:T(8,128)}, f32[512,256]{0,1:T(8,128)S(1)}, u32[]{:S(2)}, u32[]{:S(2)}) collective-permute-start(f32[512,256]{0,1:T(8,128)} %copy.41), channel_id=1, source_target_pairs={{6,0},{8,2},{10,4},{12,6},{14,8},{16,10},{18,12},{20,14},{22,16},{... | collective-permute-start | bytes 1572872 | tf_op jit(solution)/shard_map/ppermute | solution.py:20
  126.5 50.6 %collective-permute-start.10 = (f32[512,256]{0,1:T(8,128)}, f32[512,256]{0,1:T(8,128)S(1)}, u32[]{:S(2)}, u32[]{:S(2)}) collective-permute-start(f32[512,256]{0,1:T(8,128)} %copy.40), channel_id=1, source_target_pairs={{4,0},{6,2},{8,4},{10,6},{12,8},{14,10},{16,12},{18,14},{20,16},{2... | collective-permute-start | bytes 1572872 | tf_op jit(solution)/shard_map/ppermute | solution.py:20
  154.8 22.3 %collective-permute-start.9 = (f32[512,256]{0,1:T(8,128)}, f32[512,256]{0,1:T(8,128)S(1)}, u32[]{:S(2)}, u32[]{:S(2)}) collective-permute-start(f32[512,256]{0,1:T(8,128)} %copy.39), channel_id=1, source_target_pairs={{2,0},{4,2},{6,4},{8,6},{10,8},{12,10},{14,12},{16,14},{18,16},{20... | collective-permute-start | bytes 1572872 | tf_op jit(solution)/shard_map/ppermute | solution.py:20
  156.7 26.7 %collective-permute-start.8 = (f32[512,256]{0,1:T(8,128)}, f32[512,256]{0,1:T(8,128)}, u32[]{:S(2)}, u32[]{:S(2)}) collective-permute-start(f32[512,256]{0,1:T(8,128)} %copy.37), channel_id=1, source_target_pairs={{0,2},{2,4},{4,6},{6,8},{8,10},{10,12},{12,14},{14,16},{16,18},{18... | collective-permute-start | bytes 1572872 | tf_op jit(solution)/shard_map/ppermute | solution.py:20
  278.6 391.1 %all-gather.9.cloned.1.call-start = ((), (), s32[]{:S(2)}) async-start(), calls=%async_computation.2 | async-start | bytes 1572864 | tf_op jit(solution)/shard_map/all_gather | solution.py:271
  514.0 19.1 %collective-permute-start.16 = (bf16[512,256]{0,1:T(8,128)(2,1)S(1)}, bf16[512,256]{0,1:T(8,128)(2,1)S(1)}, u32[]{:S(2)}, u32[]{:S(2)}) collective-permute-start(bf16[512,256]{0,1:T(8,128)(2,1)S(1)} %get-tuple-element.40), channel_id=1, source_target_pairs={{0,12},{2,14},{4,16},{6,18},{8,20},{10,22},{12,24},{14,26},{16,28}... | collective-permute-start | bytes 786440 | tf_op jit(solution)/shard_map/ppermute | solution.py:20
  519.8 19.7 %collective-permute-start.17 = (bf16[512,256]{0,1:T(8,128)(2,1)S(1)}, bf16[512,256]{0,1:T(8,128)(2,1)S(1)}, u32[]{:S(2)}, u32[]{:S(2)}) collective-permute-start(bf16[512,256]{0,1:T(8,128)(2,1)S(1)} %get-tuple-element.40), channel_id=1, source_target_pairs={{0,10},{2,12},{4,14},{6,16},{8,18},{10,20},{12,22},{14,24},{16,26}... | collective-permute-start | bytes 786440 | tf_op jit(solution)/shard_map/ppermute | solution.py:20
  522.1 23.0 %collective-permute-start.18 = (bf16[512,256]{0,1:T(8,128)(2,1)S(1)}, bf16[512,256]{0,1:T(8,128)(2,1)S(1)}, u32[]{:S(2)}, u32[]{:S(2)}) collective-permute-start(bf16[512,256]{0,1:T(8,128)(2,1)S(1)} %get-tuple-element.40), channel_id=1, source_target_pairs={{0,8},{2,10},{4,12},{6,14},{8,16},{10,18},{12,20},{14,22},{16,24},... | collective-permute-start | bytes 786440 | tf_op jit(solution)/shard_map/ppermute | solution.py:20
  524.8 24.4 %collective-permute-start.19 = (bf16[512,256]{0,1:T(8,128)(2,1)S(1)}, bf16[512,256]{0,1:T(8,128)(2,1)S(1)}, u32[]{:S(2)}, u32[]{:S(2)}) collective-permute-start(bf16[512,256]{0,1:T(8,128)(2,1)S(1)} %get-tuple-element.40), channel_id=1, source_target_pairs={{0,6},{2,8},{4,10},{6,12},{8,14},{10,16},{12,18},{14,20},{16,22},{... | collective-permute-start | bytes 786440 | tf_op jit(solution)/shard_map/ppermute | solution.py:20
  529.8 22.2 %collective-permute-start.20 = (bf16[512,256]{0,1:T(8,128)(2,1)S(1)}, bf16[512,256]{0,1:T(8,128)(2,1)S(1)}, u32[]{:S(2)}, u32[]{:S(2)}) collective-permute-start(bf16[512,256]{0,1:T(8,128)(2,1)S(1)} %get-tuple-element.40), channel_id=1, source_target_pairs={{0,4},{2,6},{4,8},{6,10},{8,12},{10,14},{12,16},{14,18},{16,20},{1... | collective-permute-start | bytes 786440 | tf_op jit(solution)/shard_map/ppermute | solution.py:20
  533.1 19.0 %collective-permute-start.21 = (bf16[512,256]{0,1:T(8,128)(2,1)S(1)}, bf16[512,256]{0,1:T(8,128)(2,1)S(1)}, u32[]{:S(2)}, u32[]{:S(2)}) collective-permute-start(bf16[512,256]{0,1:T(8,128)(2,1)S(1)} %get-tuple-element.40), channel_id=1, source_target_pairs={{0,2},{2,4},{4,6},{6,8},{8,10},{10,12},{12,14},{14,16},{16,18},{18... | collective-permute-start | bytes 786440 | tf_op jit(solution)/shard_map/ppermute | solution.py:20
  577.8 51.3 %collective-permute-start.31 = (f32[512,256]{0,1:T(8,128)}, f32[512,256]{0,1:T(8,128)}, u32[]{:S(2)}, u32[]{:S(2)}) collective-permute-start(f32[512,256]{0,1:T(8,128)} %copy.58), channel_id=1, source_target_pairs={{14,0},{16,2},{18,4},{20,6},{22,8},{24,10},{26,12},{28,14},{30,16}... | collective-permute-start | bytes 1572872 | tf_op jit(solution)/shard_map/ppermute | solution.py:20
  581.1 62.7 %collective-permute-start.30 = (f32[512,256]{0,1:T(8,128)}, f32[512,256]{0,1:T(8,128)}, u32[]{:S(2)}, u32[]{:S(2)}) collective-permute-start(f32[512,256]{0,1:T(8,128)} %copy.57), channel_id=1, source_target_pairs={{12,0},{14,2},{16,4},{18,6},{20,8},{22,10},{24,12},{26,14},{28,16}... | collective-permute-start | bytes 1572872 | tf_op jit(solution)/shard_map/ppermute | solution.py:20
  584.5 61.3 %collective-permute-start.29 = (f32[512,256]{0,1:T(8,128)}, f32[512,256]{0,1:T(8,128)}, u32[]{:S(2)}, u32[]{:S(2)}) collective-permute-start(f32[512,256]{0,1:T(8,128)} %copy.56), channel_id=1, source_target_pairs={{10,0},{12,2},{14,4},{16,6},{18,8},{20,10},{22,12},{24,14},{26,16}... | collective-permute-start | bytes 1572872 | tf_op jit(solution)/shard_map/ppermute | solution.py:20
  585.8 192.7 %all-gather.11.cloned.1.call-start = ((), (), s32[]{:S(2)}) async-start(), calls=%async_computation.3 | async-start | bytes 1572864 | tf_op jit(solution)/shard_map/all_gather | solution.py:283
  586.8 73.4 %collective-permute-start.28 = (f32[512,256]{0,1:T(8,128)}, f32[512,256]{0,1:T(8,128)S(1)}, u32[]{:S(2)}, u32[]{:S(2)}) collective-permute-start(f32[512,256]{0,1:T(8,128)} %copy.55), channel_id=1, source_target_pairs={{8,0},{10,2},{12,4},{14,6},{16,8},{18,10},{20,12},{22,14},{24,16},... | collective-permute-start | bytes 1572872 | tf_op jit(solution)/shard_map/ppermute | solution.py:20
  589.1 71.1 %collective-permute-start.27 = (f32[512,256]{0,1:T(8,128)}, f32[512,256]{0,1:T(8,128)S(1)}, u32[]{:S(2)}, u32[]{:S(2)}) collective-permute-start(f32[512,256]{0,1:T(8,128)} %copy.54), channel_id=1, source_target_pairs={{6,0},{8,2},{10,4},{12,6},{14,8},{16,10},{18,12},{20,14},{22,16},{... | collective-permute-start | bytes 1572872 | tf_op jit(solution)/shard_map/ppermute | solution.py:20
  629.1 33.0 %collective-permute-start.26 = (f32[512,256]{0,1:T(8,128)}, f32[512,256]{0,1:T(8,128)S(1)}, u32[]{:S(2)}, u32[]{:S(2)}) collective-permute-start(f32[512,256]{0,1:T(8,128)} %copy.53), channel_id=1, source_target_pairs={{4,0},{6,2},{8,4},{10,6},{12,8},{14,10},{16,12},{18,14},{20,16},{2... | collective-permute-start | bytes 1572872 | tf_op jit(solution)/shard_map/ppermute | solution.py:20
  645.8 21.8 %collective-permute-start.24 = (f32[512,256]{0,1:T(8,128)}, f32[512,256]{0,1:T(8,128)}, u32[]{:S(2)}, u32[]{:S(2)}) collective-permute-start(f32[512,256]{0,1:T(8,128)} %copy.50), channel_id=1, source_target_pairs={{0,2},{2,4},{4,6},{6,8},{8,10},{10,12},{12,14},{14,16},{16,18},{18... | collective-permute-start | bytes 1572872 | tf_op jit(solution)/shard_map/ppermute | solution.py:20
  (11 other events, 521.5 us)
Sparse Core Ops, SparseCore 0:
  92.7 57.9 all-gather.4
  278.7 13.5 all-gather.6
  585.9 53.3 all-gather.8
  764.9 13.5 all-gather.10

commit v9 on v8

--- a/solution.py
+++ b/solution.py
@@ -155,6 +155,43 @@
     return out.reshape(rows, cols)
 
 
+def swap_halves(x_ref, out_ref, recv_ref, send_sem, recv_sem):
+    core = lax.axis_index("vec")
+    sibling = 1 - core
+    mesh_ids = pl.DeviceIdType.MESH
+    barrier = pltpu.get_barrier_semaphore()
+    pl.semaphore_signal(barrier, 1, device_id={"vec": sibling}, device_id_type=mesh_ids)
+    pl.semaphore_wait(barrier, 1)
+    copy = pltpu.make_async_remote_copy(
+        src_ref=x_ref,
+        dst_ref=recv_ref,
+        send_sem=send_sem,
+        recv_sem=recv_sem,
+        device_id={"vec": sibling},
+        device_id_type=mesh_ids,
+    )
+    copy.start()
+    out_ref[core] = x_ref[...]
+    copy.wait()
+    out_ref[sibling] = recv_ref[...]
+
+
+def gathered_over_vec(block):
+    halves = pl.pallas_call(
+        swap_halves,
+        out_shape=jax.ShapeDtypeStruct((2, *block.shape), block.dtype),
+        in_specs=[pl.BlockSpec(memory_space=pltpu.VMEM)],
+        out_specs=pl.BlockSpec(memory_space=pltpu.VMEM),
+        scratch_shapes=[
+            pltpu.VMEM(block.shape, block.dtype),
+            pltpu.SemaphoreType.DMA(()),
+            pltpu.SemaphoreType.DMA(()),
+        ],
+        compiler_params=pltpu.CompilerParams(collective_id=2, has_side_effects=True),
+    )(block)
+    return jnp.concatenate([halves[0], halves[1]], axis=1)
+
+
 def tile_products(rows_ref, cols_ref, used_ref, tile_ref, x_ref, out_ref):
     slot = pl.program_id(0)
 
@@ -280,7 +317,7 @@
             current_all, rayleigh, precision=exact_mode, preferred_element_type=jnp.float32
         )
         update = current - step_rate * residual
-        update_all = lax.all_gather(update, "vec", axis=1, tiled=True)
+        update_all = gathered_over_vec(update)
         gram_matrix = summed_over_patch(
             jnp.dot(
                 update_all.T, update_all, precision=exact_mode, preferred_element_type=jnp.float32

time: 1010 us -> 954 us (0.945)
  local copies, waits for them, and re-layouts: 68.5 us -> 31.5 us
  Pallas kernels: 323 us -> 302 us
  starting transfers between devices: 108 us -> 121 us
    ppermute x32, waiting for transfers between devices: 148 us -> 179 us  [shifted(): return lax.ppermute(block, axis, route)]
    select_n x20 -> x0, local copies, waits for them, and re-layouts: 28.7 us -> none  [the longest x16 23.4 us: shards(): outgoing = jnp.where(parity == 0, lower_seg, upper_seg)]
    pallas_call x4, Pallas kernels: 289 us -> 262 us  [summed_over_patch(): pl.pallas_call(functools.partial(exchange_sum, size), out_shape=jax.Shape...]
    all_gather x2 -> x0, waiting for transfers between devices: 26.1 us -> none  [shards(): update_all = lax.all_gather(update, 'vec', axis=1, tiled=True)]
    ppermute x32, starting transfers between devices: 107 us -> 121 us  [shifted(): return lax.ppermute(block, axis, route)]
    another operation x27 -> x28, local copies, waits for them, and re-layouts: 24 us -> 15.4 us  [shards(): lax.linalg.triangular_solve(factor, update_all, left_side=False, lower=Tr...]
  transfers between devices with their start and end apart: 36 -> 34, of which waited for: 18 -> 17; matrix products, arithmetic and copies ran while one was open for 3% -> 1% of each run, Pallas kernels for 0% -> 0%
where the time goes in v9:
time: 954 us; the launch traced here: 943 us
  Pallas kernels  302 us (32%)
  other arithmetic  256 us (27%)
  waiting for transfers between devices  179 us (19%)
  starting transfers between devices  121 us (13%)
  matrix products  31.9 us (3%)
  local copies, waits for them, and re-layouts  31.5 us (3%)
  between operations  21 us (2%)
    pallas_call x4, Pallas kernels, summed_over_patch(): pl.pallas_call(functools.partial(exchange_sum, size), out_shape=jax.Shape...  262 us
    ppermute x32, waiting for transfers between devices, shifted(): return lax.ppermute(block, axis, route)  179 us
    another operation x30, other arithmetic, shards(): factor = jnp.linalg.cholesky(gram_matrix)  159 us
    ppermute x32, starting transfers between devices, shifted(): return lax.ppermute(block, axis, route)  121 us
    another operation x6, other arithmetic, shards(): lax.linalg.triangular_solve(factor, update_all, left_side=False, lower=Tr...  79.2 us
    pallas_call x2, Pallas kernels, hessian_window(): pl.pallas_call(tile_products, grid_spec=grid_spec, out_shape=jax.ShapeDty...  31.9 us
  transfers between devices with their start and end apart: 34, of which 17 were waited for; matrix products, arithmetic and copies ran while one was open for 1% of the time, Pallas kernels for 0%

profile of v9, /device:TPU:4, one launch (start us, length us, event | category | flops | bytes accessed | tf_op | source)
XLA Modules:
  0.0 943.1 jit_solution(6688317628386459160)
XLA Ops:
  60.2 15.9 %shard_map.68 = f32[16,256,256]{2,1,0:T(8,128)} custom-call(s32[64]{0:T(128)} %get-tuple-element.123.rows_ref, s32[64]{0:T(128)} %get-tuple-element.122.cols_ref, s32[1]{0:T(128)S(6)} %copy.92.used_ref, bf16[64,256,256]{2,1,0:T(8,128)(2,1)} %tile_ref.3, bf16[16,256,256]{2,1,0:T(8,128)(2,1)} %bitcast.181), custom_call_target="tpu_custom_call" | custom-call | flops 4294967296 | bytes 14680064 | tf_op jit(solution)/shard_map/pallas_call | solution.py:236
  86.5 27.8 %collective-permute-done.15 = f32[512,256]{1,0:T(8,128)S(1)} collective-permute-done((f32[512,256]{1,0:T(8,128)}, f32[512,256]{1,0:T(8,128)S(1)}, u32[]{:S(2)}, u32[]{:S(2)}) %collective-permute-start.15) | collective-permute-done | bytes 524320 | tf_op jit(solution)/shard_map/ppermute | solution.py:20
  121.2 39.9 %collective-permute-done.14 = f32[512,256]{1,0:T(8,128)S(1)} collective-permute-done((f32[512,256]{1,0:T(8,128)}, f32[512,256]{1,0:T(8,128)S(1)}, u32[]{:S(2)}, u32[]{:S(2)}) %collective-permute-start.14) | collective-permute-done | bytes 524320 | tf_op jit(solution)/shard_map/ppermute | solution.py:20
  163.0 13.4 %collective-permute-start.8 = (f32[512,256]{1,0:T(8,128)S(1)}, f32[512,256]{1,0:T(8,128)}, u32[]{:S(2)}, u32[]{:S(2)}) collective-permute-start(f32[512,256]{1,0:T(8,128)S(1)} %bitcast.182), channel_id=1, source_target_pairs={{0,2},{2,4},{4,6},{6,8},{8,10},{10,12},{12,14},{14,16},{16,18},{18... | collective-permute-start | bytes 1572872 | tf_op jit(solution)/shard_map/ppermute | solution.py:20
  192.1 78.9 %shard_map.69 = f32[128,8,128]{2,1,0:T(8,128)} custom-call(f32[128,8,128]{2,1,0:T(8,128)} %reshape.147.x_ref), custom_call_target="tpu_custom_call" | custom-call | tf_op jit(solution)/shard_map/pallas_call | solution.py:141
  282.2 52.9 %shard_map.71 = f32[128,16,128]{2,1,0:T(8,128)} custom-call(f32[128,16,128]{2,1,0:T(8,128)} %reshape.149.x_ref), custom_call_target="tpu_custom_call" | custom-call | tf_op jit(solution)/shard_map/pallas_call | solution.py:141
  338.0 11.7 %cholesky.286 = f32[128,128]{1,0:T(8,128)S(1)} custom-call(f32[128,128]{1,0:T(8,128)S(1)} %cholesky.426), custom_call_target="Cholesky" | custom-call | tf_op jit(solution)/shard_map/jit(cholesky)/cholesky | solution.py:328
  349.9 9.8 %custom-call.27 = f32[1,128,128]{1,2,0:T(8,128)S(1)} custom-call(f32[1,128,128]{2,1,0:T(8,128)S(1)} %get-tuple-element.115), custom_call_target="InvertDiagBlocksLowerTriangular" | custom-call | tf_op jit(solution)/shard_map/jit(cholesky)/cholesky | solution.py:328
  362.2 11.7 %cholesky.305 = f32[128,128]{1,0:T(8,128)S(1)} custom-call(f32[128,128]{1,0:T(8,128)S(1)} %cholesky.430), custom_call_target="Cholesky" | custom-call | tf_op jit(solution)/shard_map/jit(cholesky)/cholesky | solution.py:328
  374.0 10.2 %custom-call.28 = f32[1,128,128]{1,2,0:T(8,128)S(1)} custom-call(f32[1,128,128]{2,1,0:T(8,128)S(1)} %get-tuple-element.112), custom_call_target="InvertDiagBlocksLowerTriangular" | custom-call | tf_op jit(solution)/shard_map/jit(cholesky)/cholesky | solution.py:328
  385.8 11.7 %cholesky.326 = f32[128,128]{1,0:T(8,128)S(1)} custom-call(f32[128,128]{1,0:T(8,128)S(1)} %cholesky.435), custom_call_target="Cholesky" | custom-call | tf_op jit(solution)/shard_map/jit(cholesky)/cholesky | solution.py:328
  397.5 9.8 %custom-call.29 = f32[1,128,128]{1,2,0:T(8,128)S(1)} custom-call(f32[1,128,128]{2,1,0:T(8,128)S(1)} %get-tuple-element.109), custom_call_target="InvertDiagBlocksLowerTriangular" | custom-call | tf_op jit(solution)/shard_map/jit(cholesky)/cholesky | solution.py:328
  408.8 11.9 %cholesky.343 = f32[128,128]{1,0:T(8,128)S(1)} custom-call(f32[128,128]{1,0:T(8,128)S(1)} %convolution_subtract_fusion.12), custom_call_target="Cholesky" | custom-call | tf_op jit(solution)/shard_map/jit(cholesky)/cholesky | solution.py:328
  425.9 7.7 while.4
  433.6 39.3 %custom-call.30 = f32[4,128,128]{1,2,0:T(8,128)S(1)} custom-call(f32[4,128,128]{2,1,0:T(8,128)S(1)} %get-tuple-element.18), custom_call_target="InvertDiagBlocksLowerTriangular" | custom-call | tf_op jit(solution)/shard_map/triangular_solve/custom-call.3 | solution.py:329
  479.4 7.5 collective-permute-start.16
  521.7 15.9 %shard_map.72 = f32[16,256,256]{2,1,0:T(8,128)} custom-call(s32[64]{0:T(128)} %get-tuple-element.123.rows_ref, s32[64]{0:T(128)} %get-tuple-element.122.cols_ref, s32[1]{0:T(128)S(6)} %copy.92.used_ref, bf16[64,256,256]{2,1,0:T(8,128)(2,1)} %tile_ref.3, bf16[16,256,256]{2,1,0:T(8,128)(2,1)} %bitcast.180), custom_call_target="tpu_custom_call" | custom-call | flops 4294967296 | bytes 14680064 | tf_op jit(solution)/shard_map/pallas_call | solution.py:236
  547.9 25.4 %collective-permute-done.31 = f32[512,256]{1,0:T(8,128)S(1)} collective-permute-done((f32[512,256]{1,0:T(8,128)}, f32[512,256]{1,0:T(8,128)S(1)}, u32[]{:S(2)}, u32[]{:S(2)}) %collective-permute-start.31) | collective-permute-done | bytes 524320 | tf_op jit(solution)/shard_map/ppermute | solution.py:20
  573.4 10.1 %collective-permute-start.26 = (f32[512,256]{1,0:T(8,128)S(1)}, f32[512,256]{1,0:T(8,128)S(1)}, u32[]{:S(2)}, u32[]{:S(2)}) collective-permute-start(f32[512,256]{1,0:T(8,128)S(1)} %bitcast.189), channel_id=1, source_target_pairs={{4,0},{6,2},{8,4},{10,6},{12,8},{14,10},{16,12},{18,14},{20,16},{2... | collective-permute-start | bytes 1572872 | tf_op jit(solution)/shard_map/ppermute | solution.py:20
  583.5 39.6 %collective-permute-done.30 = f32[512,256]{1,0:T(8,128)S(1)} collective-permute-done((f32[512,256]{1,0:T(8,128)}, f32[512,256]{1,0:T(8,128)S(1)}, u32[]{:S(2)}, u32[]{:S(2)}) %collective-permute-start.30) | collective-permute-done | bytes 524320 | tf_op jit(solution)/shard_map/ppermute | solution.py:20
  625.1 13.3 %collective-permute-start.24 = (f32[512,256]{1,0:T(8,128)S(1)}, f32[512,256]{1,0:T(8,128)S(1)}, u32[]{:S(2)}, u32[]{:S(2)}) collective-permute-start(f32[512,256]{1,0:T(8,128)S(1)} %bitcast.187), channel_id=1, source_target_pairs={{0,2},{2,4},{4,6},{6,8},{8,10},{10,12},{12,14},{14,16},{16,18},{18... | collective-permute-start | bytes 1572872 | tf_op jit(solution)/shard_map/ppermute | solution.py:20
  650.4 78.2 %shard_map.73 = f32[128,8,128]{2,1,0:T(8,128)} custom-call(f32[128,8,128]{2,1,0:T(8,128)} %reshape.151.x_ref), custom_call_target="tpu_custom_call" | custom-call | tf_op jit(solution)/shard_map/pallas_call | solution.py:141
  740.0 52.3 %shard_map.75 = f32[128,16,128]{2,1,0:T(8,128)} custom-call(f32[128,16,128]{2,1,0:T(8,128)} %reshape.153.x_ref), custom_call_target="tpu_custom_call" | custom-call | tf_op jit(solution)/shard_map/pallas_call | solution.py:141
  795.2 11.7 %cholesky.358 = f32[128,128]{1,0:T(8,128)S(1)} custom-call(f32[128,128]{1,0:T(8,128)S(1)} %cholesky.439), custom_call_target="Cholesky" | custom-call | tf_op jit(solution)/shard_map/jit(cholesky)/cholesky | solution.py:328
  807.1 9.8 %custom-call.31 = f32[1,128,128]{1,2,0:T(8,128)S(1)} custom-call(f32[1,128,128]{2,1,0:T(8,128)S(1)} %get-tuple-element.105), custom_call_target="InvertDiagBlocksLowerTriangular" | custom-call | tf_op jit(solution)/shard_map/jit(cholesky)/cholesky | solution.py:328
  819.4 11.7 %cholesky.377 = f32[128,128]{1,0:T(8,128)S(1)} custom-call(f32[128,128]{1,0:T(8,128)S(1)} %cholesky.443), custom_call_target="Cholesky" | custom-call | tf_op jit(solution)/shard_map/jit(cholesky)/cholesky | solution.py:328
  831.2 10.0 %custom-call.32 = f32[1,128,128]{1,2,0:T(8,128)S(1)} custom-call(f32[1,128,128]{2,1,0:T(8,128)S(1)} %get-tuple-element.102), custom_call_target="InvertDiagBlocksLowerTriangular" | custom-call | tf_op jit(solution)/shard_map/jit(cholesky)/cholesky | solution.py:328
  842.7 11.7 %cholesky.398 = f32[128,128]{1,0:T(8,128)S(1)} custom-call(f32[128,128]{1,0:T(8,128)S(1)} %cholesky.448), custom_call_target="Cholesky" | custom-call | tf_op jit(solution)/shard_map/jit(cholesky)/cholesky | solution.py:328
  854.5 9.8 %custom-call.33 = f32[1,128,128]{1,2,0:T(8,128)S(1)} custom-call(f32[1,128,128]{2,1,0:T(8,128)S(1)} %get-tuple-element.99), custom_call_target="InvertDiagBlocksLowerTriangular" | custom-call | tf_op jit(solution)/shard_map/jit(cholesky)/cholesky | solution.py:328
  865.7 11.9 %cholesky.415 = f32[128,128]{1,0:T(8,128)S(1)} custom-call(f32[128,128]{1,0:T(8,128)S(1)} %convolution_subtract_fusion.11), custom_call_target="Cholesky" | custom-call | tf_op jit(solution)/shard_map/jit(cholesky)/cholesky | solution.py:328
  882.9 7.7 while.5
  890.6 39.3 %custom-call.34 = f32[4,128,128]{1,2,0:T(8,128)S(1)} custom-call(f32[4,128,128]{2,1,0:T(8,128)S(1)} %get-tuple-element.19), custom_call_target="InvertDiagBlocksLowerTriangular" | custom-call | tf_op jit(solution)/shard_map/triangular_solve/custom-call.3 | solution.py:329
  (209 shorter events, 218.7 us)
Async XLA Ops:
  7.2 181.6 %all-gather.3.cloned.1.call-start = ((), (), s32[]{:S(2)}) async-start(), calls=%async_computation | async-start | bytes 1572864 | tf_op jit(solution)/shard_map/all_gather | solution.py:308
  8.3 24.9 %collective-permute-start.7 = (bf16[512,256]{1,0:T(8,128)(2,1)S(1)}, bf16[512,256]{1,0:T(8,128)(2,1)S(1)}, u32[]{:S(2)}, u32[]{:S(2)}) collective-permute-start(bf16[512,256]{1,0:T(8,128)(2,1)S(1)} %convert_element_type.6), channel_id=1, source_target_pairs={{0,14},{2,16},{4,18},{6,20},{8,22},{10,24},{12,26},{14,28},{16,30}... | collective-permute-start | bytes 786440 | tf_op jit(solution)/shard_map/ppermute | solution.py:20
  13.5 24.1 %collective-permute-start = (bf16[512,256]{1,0:T(8,128)(2,1)S(1)}, bf16[512,256]{1,0:T(8,128)(2,1)S(1)}, u32[]{:S(2)}, u32[]{:S(2)}) collective-permute-start(bf16[512,256]{1,0:T(8,128)(2,1)S(1)} %convert_element_type.6), channel_id=1, source_target_pairs={{0,12},{2,14},{4,16},{6,18},{8,20},{10,22},{12,24},{14,26},{16,28}... | collective-permute-start | bytes 786440 | tf_op jit(solution)/shard_map/ppermute | solution.py:20
  19.5 23.0 %collective-permute-start.1 = (bf16[512,256]{1,0:T(8,128)(2,1)S(1)}, bf16[512,256]{1,0:T(8,128)(2,1)S(1)}, u32[]{:S(2)}, u32[]{:S(2)}) collective-permute-start(bf16[512,256]{1,0:T(8,128)(2,1)S(1)} %convert_element_type.6), channel_id=1, source_target_pairs={{0,10},{2,12},{4,14},{6,16},{8,18},{10,20},{12,22},{14,24},{16,26}... | collective-permute-start | bytes 786440 | tf_op jit(solution)/shard_map/ppermute | solution.py:20
  24.3 23.8 %collective-permute-start.2 = (bf16[512,256]{1,0:T(8,128)(2,1)S(1)}, bf16[512,256]{1,0:T(8,128)(2,1)S(1)}, u32[]{:S(2)}, u32[]{:S(2)}) collective-permute-start(bf16[512,256]{1,0:T(8,128)(2,1)S(1)} %convert_element_type.6), channel_id=1, source_target_pairs={{0,8},{2,10},{4,12},{6,14},{8,16},{10,18},{12,20},{14,22},{16,24},... | collective-permute-start | bytes 786440 | tf_op jit(solution)/shard_map/ppermute | solution.py:20
  27.2 26.6 %collective-permute-start.3 = (bf16[512,256]{1,0:T(8,128)(2,1)S(1)}, bf16[512,256]{1,0:T(8,128)(2,1)S(1)}, u32[]{:S(2)}, u32[]{:S(2)}) collective-permute-start(bf16[512,256]{1,0:T(8,128)(2,1)S(1)} %convert_element_type.6), channel_id=1, source_target_pairs={{0,6},{2,8},{4,10},{6,12},{8,14},{10,16},{12,18},{14,20},{16,22},{... | collective-permute-start | bytes 786440 | tf_op jit(solution)/shard_map/ppermute | solution.py:20
  33.2 25.2 %collective-permute-start.4 = (bf16[512,256]{1,0:T(8,128)(2,1)S(1)}, bf16[512,256]{1,0:T(8,128)(2,1)S(1)}, u32[]{:S(2)}, u32[]{:S(2)}) collective-permute-start(bf16[512,256]{1,0:T(8,128)(2,1)S(1)} %convert_element_type.6), channel_id=1, source_target_pairs={{0,4},{2,6},{4,8},{6,10},{8,12},{10,14},{12,16},{14,18},{16,20},{1... | collective-permute-start | bytes 786440 | tf_op jit(solution)/shard_map/ppermute | solution.py:20
  37.6 20.9 %collective-permute-start.5 = (bf16[512,256]{1,0:T(8,128)(2,1)S(1)}, bf16[512,256]{1,0:T(8,128)(2,1)S(1)}, u32[]{:S(2)}, u32[]{:S(2)}) collective-permute-start(bf16[512,256]{1,0:T(8,128)(2,1)S(1)} %convert_element_type.6), channel_id=1, source_target_pairs={{0,2},{2,4},{4,6},{6,8},{8,10},{10,12},{12,14},{14,16},{16,18},{18... | collective-permute-start | bytes 786440 | tf_op jit(solution)/shard_map/ppermute | solution.py:20
  42.5 16.1 %collective-permute-start.6 = (bf16[512,256]{1,0:T(8,128)(2,1)S(1)}, bf16[512,256]{1,0:T(8,128)(2,1)S(1)}, u32[]{:S(2)}, u32[]{:S(2)}) collective-permute-start(bf16[512,256]{1,0:T(8,128)(2,1)S(1)} %convert_element_type.6), channel_id=1, source_target_pairs={{2,0},{4,2},{6,4},{8,6},{10,8},{12,10},{14,12},{16,14},{18,16},{20... | collective-permute-start | bytes 786440 | tf_op jit(solution)/shard_map/ppermute | solution.py:20
  80.0 34.3 %collective-permute-start.15 = (f32[512,256]{1,0:T(8,128)}, f32[512,256]{1,0:T(8,128)S(1)}, u32[]{:S(2)}, u32[]{:S(2)}) collective-permute-start(f32[512,256]{1,0:T(8,128)} %bitcast.9), channel_id=1, source_target_pairs={{14,0},{16,2},{18,4},{20,6},{22,8},{24,10},{26,12},{28,14},{30,16}... | collective-permute-start | bytes 1572872 | tf_op jit(solution)/shard_map/ppermute | solution.py:20
  81.3 79.9 %collective-permute-start.14 = (f32[512,256]{1,0:T(8,128)}, f32[512,256]{1,0:T(8,128)S(1)}, u32[]{:S(2)}, u32[]{:S(2)}) collective-permute-start(f32[512,256]{1,0:T(8,128)} %bitcast.8), channel_id=1, source_target_pairs={{12,0},{14,2},{16,4},{18,6},{20,8},{22,10},{24,12},{26,14},{28,16}... | collective-permute-start | bytes 1572872 | tf_op jit(solution)/shard_map/ppermute | solution.py:20
  82.6 80.5 %collective-permute-start.13 = (f32[512,256]{1,0:T(8,128)}, f32[512,256]{1,0:T(8,128)}, u32[]{:S(2)}, u32[]{:S(2)}) collective-permute-start(f32[512,256]{1,0:T(8,128)} %bitcast.7), channel_id=1, source_target_pairs={{10,0},{12,2},{14,4},{16,6},{18,8},{20,10},{22,12},{24,14},{26,16}... | collective-permute-start | bytes 1572872 | tf_op jit(solution)/shard_map/ppermute | solution.py:20
  83.9 562.7 %all-gather.5.cloned.1.call-start = ((), (), s32[]{:S(2)}) async-start(), calls=%async_computation.1 | async-start | bytes 1572864 | tf_op jit(solution)/shard_map/all_gather | solution.py:308
  83.9 92.5 %collective-permute-start.12 = (f32[512,256]{1,0:T(8,128)}, f32[512,256]{1,0:T(8,128)}, u32[]{:S(2)}, u32[]{:S(2)}) collective-permute-start(f32[512,256]{1,0:T(8,128)} %bitcast.186), channel_id=1, source_target_pairs={{8,0},{10,2},{12,4},{14,6},{16,8},{18,10},{20,12},{22,14},{24,16},... | collective-permute-start | bytes 1572872 | tf_op jit(solution)/shard_map/ppermute | solution.py:20
  85.2 91.2 %collective-permute-start.11 = (f32[512,256]{1,0:T(8,128)}, f32[512,256]{1,0:T(8,128)}, u32[]{:S(2)}, u32[]{:S(2)}) collective-permute-start(f32[512,256]{1,0:T(8,128)} %bitcast.185), channel_id=1, source_target_pairs={{6,0},{8,2},{10,4},{12,6},{14,8},{16,10},{18,12},{20,14},{22,16},{... | collective-permute-start | bytes 1572872 | tf_op jit(solution)/shard_map/ppermute | solution.py:20
  114.3 64.9 %collective-permute-start.10 = (f32[512,256]{1,0:T(8,128)S(1)}, f32[512,256]{1,0:T(8,128)}, u32[]{:S(2)}, u32[]{:S(2)}) collective-permute-start(f32[512,256]{1,0:T(8,128)S(1)} %bitcast.184), channel_id=1, source_target_pairs={{4,0},{6,2},{8,4},{10,6},{12,8},{14,10},{16,12},{18,14},{20,16},{2... | collective-permute-start | bytes 1572872 | tf_op jit(solution)/shard_map/ppermute | solution.py:20
  161.1 18.1 %collective-permute-start.9 = (f32[512,256]{1,0:T(8,128)S(1)}, f32[512,256]{1,0:T(8,128)}, u32[]{:S(2)}, u32[]{:S(2)}) collective-permute-start(f32[512,256]{1,0:T(8,128)S(1)} %bitcast.183), channel_id=1, source_target_pairs={{2,0},{4,2},{6,4},{8,6},{10,8},{12,10},{14,12},{16,14},{18,16},{20... | collective-permute-start | bytes 1572872 | tf_op jit(solution)/shard_map/ppermute | solution.py:20
  163.0 23.6 %collective-permute-start.8 = (f32[512,256]{1,0:T(8,128)S(1)}, f32[512,256]{1,0:T(8,128)}, u32[]{:S(2)}, u32[]{:S(2)}) collective-permute-start(f32[512,256]{1,0:T(8,128)S(1)} %bitcast.182), channel_id=1, source_target_pairs={{0,2},{2,4},{4,6},{6,8},{8,10},{10,12},{12,14},{14,16},{16,18},{18... | collective-permute-start | bytes 1572872 | tf_op jit(solution)/shard_map/ppermute | solution.py:20
  477.6 17.9 %collective-permute-start.23 = (bf16[512,256]{1,0:T(8,128)(2,1)S(1)}, bf16[512,256]{1,0:T(8,128)(2,1)S(1)}, u32[]{:S(2)}, u32[]{:S(2)}) collective-permute-start(bf16[512,256]{1,0:T(8,128)(2,1)S(1)} %get-tuple-element.40), channel_id=1, source_target_pairs={{0,14},{2,16},{4,18},{6,20},{8,22},{10,24},{12,26},{14,28},{16,30}... | collective-permute-start | bytes 786440 | tf_op jit(solution)/shard_map/ppermute | solution.py:20
  479.4 21.4 %collective-permute-start.16 = (bf16[512,256]{1,0:T(8,128)(2,1)S(1)}, bf16[512,256]{1,0:T(8,128)(2,1)S(1)}, u32[]{:S(2)}, u32[]{:S(2)}) collective-permute-start(bf16[512,256]{1,0:T(8,128)(2,1)S(1)} %get-tuple-element.40), channel_id=1, source_target_pairs={{0,12},{2,14},{4,16},{6,18},{8,20},{10,22},{12,24},{14,26},{16,28}... | collective-permute-start | bytes 786440 | tf_op jit(solution)/shard_map/ppermute | solution.py:20
  486.9 18.8 %collective-permute-start.17 = (bf16[512,256]{1,0:T(8,128)(2,1)S(1)}, bf16[512,256]{1,0:T(8,128)(2,1)S(1)}, u32[]{:S(2)}, u32[]{:S(2)}) collective-permute-start(bf16[512,256]{1,0:T(8,128)(2,1)S(1)} %get-tuple-element.40), channel_id=1, source_target_pairs={{0,10},{2,12},{4,14},{6,16},{8,18},{10,20},{12,22},{14,24},{16,26}... | collective-permute-start | bytes 786440 | tf_op jit(solution)/shard_map/ppermute | solution.py:20
  488.7 22.6 %collective-permute-start.18 = (bf16[512,256]{1,0:T(8,128)(2,1)S(1)}, bf16[512,256]{1,0:T(8,128)(2,1)S(1)}, u32[]{:S(2)}, u32[]{:S(2)}) collective-permute-start(bf16[512,256]{1,0:T(8,128)(2,1)S(1)} %get-tuple-element.40), channel_id=1, source_target_pairs={{0,8},{2,10},{4,12},{6,14},{8,16},{10,18},{12,20},{14,22},{16,24},... | collective-permute-start | bytes 786440 | tf_op jit(solution)/shard_map/ppermute | solution.py:20
  494.1 22.6 %collective-permute-start.19 = (bf16[512,256]{1,0:T(8,128)(2,1)S(1)}, bf16[512,256]{1,0:T(8,128)(2,1)S(1)}, u32[]{:S(2)}, u32[]{:S(2)}) collective-permute-start(bf16[512,256]{1,0:T(8,128)(2,1)S(1)} %get-tuple-element.40), channel_id=1, source_target_pairs={{0,6},{2,8},{4,10},{6,12},{8,14},{10,16},{12,18},{14,20},{16,22},{... | collective-permute-start | bytes 786440 | tf_op jit(solution)/shard_map/ppermute | solution.py:20
  495.5 24.1 %collective-permute-start.20 = (bf16[512,256]{1,0:T(8,128)(2,1)S(1)}, bf16[512,256]{1,0:T(8,128)(2,1)S(1)}, u32[]{:S(2)}, u32[]{:S(2)}) collective-permute-start(bf16[512,256]{1,0:T(8,128)(2,1)S(1)} %get-tuple-element.40), channel_id=1, source_target_pairs={{0,4},{2,6},{4,8},{6,10},{8,12},{10,14},{12,16},{14,18},{16,20},{1... | collective-permute-start | bytes 786440 | tf_op jit(solution)/shard_map/ppermute | solution.py:20
  500.7 18.9 %collective-permute-start.21 = (bf16[512,256]{1,0:T(8,128)(2,1)S(1)}, bf16[512,256]{1,0:T(8,128)(2,1)S(1)}, u32[]{:S(2)}, u32[]{:S(2)}) collective-permute-start(bf16[512,256]{1,0:T(8,128)(2,1)S(1)} %get-tuple-element.40), channel_id=1, source_target_pairs={{0,2},{2,4},{4,6},{6,8},{8,10},{10,12},{12,14},{14,16},{16,18},{18... | collective-permute-start | bytes 786440 | tf_op jit(solution)/shard_map/ppermute | solution.py:20
  541.4 32.0 %collective-permute-start.31 = (f32[512,256]{1,0:T(8,128)}, f32[512,256]{1,0:T(8,128)S(1)}, u32[]{:S(2)}, u32[]{:S(2)}) collective-permute-start(f32[512,256]{1,0:T(8,128)} %bitcast.35), channel_id=1, source_target_pairs={{14,0},{16,2},{18,4},{20,6},{22,8},{24,10},{26,12},{28,14},{30,16}... | collective-permute-start | bytes 1572872 | tf_op jit(solution)/shard_map/ppermute | solution.py:20
  542.7 80.4 %collective-permute-start.30 = (f32[512,256]{1,0:T(8,128)}, f32[512,256]{1,0:T(8,128)S(1)}, u32[]{:S(2)}, u32[]{:S(2)}) collective-permute-start(f32[512,256]{1,0:T(8,128)} %bitcast.34), channel_id=1, source_target_pairs={{12,0},{14,2},{16,4},{18,6},{20,8},{22,10},{24,12},{26,14},{28,16}... | collective-permute-start | bytes 1572872 | tf_op jit(solution)/shard_map/ppermute | solution.py:20
  544.0 81.0 %collective-permute-start.29 = (f32[512,256]{1,0:T(8,128)}, f32[512,256]{1,0:T(8,128)}, u32[]{:S(2)}, u32[]{:S(2)}) collective-permute-start(f32[512,256]{1,0:T(8,128)} %bitcast.33), channel_id=1, source_target_pairs={{10,0},{12,2},{14,4},{16,6},{18,8},{20,10},{22,12},{24,14},{26,16}... | collective-permute-start | bytes 1572872 | tf_op jit(solution)/shard_map/ppermute | solution.py:20
  545.3 93.1 %collective-permute-start.28 = (f32[512,256]{1,0:T(8,128)}, f32[512,256]{1,0:T(8,128)S(1)}, u32[]{:S(2)}, u32[]{:S(2)}) collective-permute-start(f32[512,256]{1,0:T(8,128)} %bitcast.191), channel_id=1, source_target_pairs={{8,0},{10,2},{12,4},{14,6},{16,8},{18,10},{20,12},{22,14},{24,16},... | collective-permute-start | bytes 1572872 | tf_op jit(solution)/shard_map/ppermute | solution.py:20
  546.6 91.8 %collective-permute-start.27 = (f32[512,256]{1,0:T(8,128)}, f32[512,256]{1,0:T(8,128)S(1)}, u32[]{:S(2)}, u32[]{:S(2)}) collective-permute-start(f32[512,256]{1,0:T(8,128)} %bitcast.190), channel_id=1, source_target_pairs={{6,0},{8,2},{10,4},{12,6},{14,8},{16,10},{18,12},{20,14},{22,16},{... | collective-permute-start | bytes 1572872 | tf_op jit(solution)/shard_map/ppermute | solution.py:20
  573.4 65.4 %collective-permute-start.26 = (f32[512,256]{1,0:T(8,128)S(1)}, f32[512,256]{1,0:T(8,128)S(1)}, u32[]{:S(2)}, u32[]{:S(2)}) collective-permute-start(f32[512,256]{1,0:T(8,128)S(1)} %bitcast.189), channel_id=1, source_target_pairs={{4,0},{6,2},{8,4},{10,6},{12,8},{14,10},{16,12},{18,14},{20,16},{2... | collective-permute-start | bytes 1572872 | tf_op jit(solution)/shard_map/ppermute | solution.py:20
  625.1 20.0 %collective-permute-start.24 = (f32[512,256]{1,0:T(8,128)S(1)}, f32[512,256]{1,0:T(8,128)S(1)}, u32[]{:S(2)}, u32[]{:S(2)}) collective-permute-start(f32[512,256]{1,0:T(8,128)S(1)} %bitcast.187), channel_id=1, source_target_pairs={{0,2},{2,4},{4,6},{6,8},{8,10},{10,12},{12,14},{14,16},{16,18},{18... | collective-permute-start | bytes 1572872 | tf_op jit(solution)/shard_map/ppermute | solution.py:20
  (9 other events, 373.4 us)
Sparse Core Ops, SparseCore 0:
  84.0 48.3 all-gather.2
  545.4 46.4 all-gather.4

commit v10 on v9

--- a/solution.py
+++ b/solution.py
@@ -305,7 +305,7 @@
             upper_seg = segments[offset + 7] if 0 <= offset + 7 <= 7 else zero_rows
             outgoing = jnp.where(parity == 0, lower_seg, upper_seg)
             applied = applied + shifted(outgoing, "patch", offset)
-        current_all = lax.all_gather(current, "vec", axis=1, tiled=True)
+        current_all = gathered_over_vec(current)
         rayleigh = summed_over_patch(
             jnp.dot(
                 current_all.T, applied, precision=exact_mode, preferred_element_type=jnp.float32

time: 954 us -> 945 us (level)
  between operations: 21 us -> 8 us
  transfers between devices with their start and end apart: 34 -> 32, of which waited for: 17 -> 14; matrix products, arithmetic and copies ran while one was open for 1% -> 0% of each run, Pallas kernels for 0% -> 1%
where the time goes in v10:
time: 945 us; the launch traced here: 929 us
  Pallas kernels  297 us (31%)
  other arithmetic  256 us (27%)
  waiting for transfers between devices  184 us (19%)
  starting transfers between devices  118 us (12%)
  local copies, waits for them, and re-layouts  35.5 us (4%)
  matrix products  30.2 us (3%)
    pallas_call x4, Pallas kernels, summed_over_patch(): pl.pallas_call(functools.partial(exchange_sum, size), out_shape=jax.Shape...  255 us
    ppermute x32, waiting for transfers between devices, shifted(): return lax.ppermute(block, axis, route)  184 us
    another operation x30, other arithmetic, shards(): factor = jnp.linalg.cholesky(gram_matrix)  159 us
    ppermute x32, starting transfers between devices, shifted(): return lax.ppermute(block, axis, route)  118 us
    another operation x6, other arithmetic, shards(): lax.linalg.triangular_solve(factor, update_all, left_side=False, lower=Tr...  79.2 us
    pallas_call x2, Pallas kernels, hessian_window(): pl.pallas_call(tile_products, grid_spec=grid_spec, out_shape=jax.ShapeDty...  25.8 us
  transfers between devices with their start and end apart: 32, of which 14 were waited for; matrix products, arithmetic and copies ran while one was open for 0% of the time, Pallas kernels for 1%

profile of v10, /device:TPU:4, one launch (start us, length us, event | category | flops | bytes accessed | tf_op | source)
XLA Modules:
  0.0 928.7 jit_solution(7022235407487539153)
XLA Ops:
  6.9 6.0 collective-permute-start
  53.6 12.9 %shard_map.68 = f32[16,256,256]{2,1,0:T(8,128)} custom-call(s32[64]{0:T(128)} %get-tuple-element.127.rows_ref, s32[64]{0:T(128)} %get-tuple-element.126.cols_ref, s32[1]{0:T(128)S(6)} %copy.87.used_ref, bf16[64,256,256]{2,1,0:T(8,128)(2,1)} %tile_ref.3, bf16[16,256,256]{2,1,0:T(8,128)(2,1)} %bitcast.175), custom_call_target="tpu_custom_call" | custom-call | flops 4294967296 | bytes 14680064 | tf_op jit(solution)/shard_map/pallas_call | solution.py:236
  76.6 26.3 %collective-permute-done.15 = f32[512,256]{1,0:T(8,128)S(1)} collective-permute-done((f32[512,256]{1,0:T(8,128)S(1)}, f32[512,256]{1,0:T(8,128)S(1)}, u32[]{:S(2)}, u32[]{:S(2)}) %collective-permute-start.15) | collective-permute-done | bytes 524320 | tf_op jit(solution)/shard_map/ppermute | solution.py:20
  104.9 50.2 %collective-permute-done.14 = f32[512,256]{1,0:T(8,128)S(1)} collective-permute-done((f32[512,256]{1,0:T(8,128)S(1)}, f32[512,256]{1,0:T(8,128)S(1)}, u32[]{:S(2)}, u32[]{:S(2)}) %collective-permute-start.14) | collective-permute-done | bytes 524320 | tf_op jit(solution)/shard_map/ppermute | solution.py:20
  157.8 20.9 %collective-permute-start.8 = (f32[512,256]{1,0:T(8,128)S(1)}, f32[512,256]{1,0:T(8,128)}, u32[]{:S(2)}, u32[]{:S(2)}) collective-permute-start(f32[512,256]{1,0:T(8,128)S(1)} %bitcast.176), channel_id=1, source_target_pairs={{0,2},{2,4},{4,6},{6,8},{8,10},{10,12},{12,14},{14,16},{16,18},{18... | collective-permute-start | bytes 1572872 | tf_op jit(solution)/shard_map/ppermute | solution.py:20
  194.6 69.7 %shard_map.70 = f32[128,8,128]{2,1,0:T(8,128)} custom-call(f32[128,8,128]{2,1,0:T(8,128)} %reshape.147.x_ref), custom_call_target="tpu_custom_call" | custom-call | tf_op jit(solution)/shard_map/pallas_call | solution.py:141
  275.5 53.3 %shard_map.72 = f32[128,16,128]{2,1,0:T(8,128)} custom-call(f32[128,16,128]{2,1,0:T(8,128)} %reshape.149.x_ref), custom_call_target="tpu_custom_call" | custom-call | tf_op jit(solution)/shard_map/pallas_call | solution.py:141
  331.7 11.7 %cholesky.286 = f32[128,128]{1,0:T(8,128)S(1)} custom-call(f32[128,128]{1,0:T(8,128)S(1)} %cholesky.426), custom_call_target="Cholesky" | custom-call | tf_op jit(solution)/shard_map/jit(cholesky)/cholesky | solution.py:328
  343.6 9.8 %custom-call.27 = f32[1,128,128]{1,2,0:T(8,128)S(1)} custom-call(f32[1,128,128]{2,1,0:T(8,128)S(1)} %get-tuple-element.119), custom_call_target="InvertDiagBlocksLowerTriangular" | custom-call | tf_op jit(solution)/shard_map/jit(cholesky)/cholesky | solution.py:328
  356.0 11.7 %cholesky.305 = f32[128,128]{1,0:T(8,128)S(1)} custom-call(f32[128,128]{1,0:T(8,128)S(1)} %cholesky.430), custom_call_target="Cholesky" | custom-call | tf_op jit(solution)/shard_map/jit(cholesky)/cholesky | solution.py:328
  367.7 10.0 %custom-call.28 = f32[1,128,128]{1,2,0:T(8,128)S(1)} custom-call(f32[1,128,128]{2,1,0:T(8,128)S(1)} %get-tuple-element.116), custom_call_target="InvertDiagBlocksLowerTriangular" | custom-call | tf_op jit(solution)/shard_map/jit(cholesky)/cholesky | solution.py:328
  379.3 11.7 %cholesky.326 = f32[128,128]{1,0:T(8,128)S(1)} custom-call(f32[128,128]{1,0:T(8,128)S(1)} %cholesky.435), custom_call_target="Cholesky" | custom-call | tf_op jit(solution)/shard_map/jit(cholesky)/cholesky | solution.py:328
  391.0 9.8 %custom-call.29 = f32[1,128,128]{1,2,0:T(8,128)S(1)} custom-call(f32[1,128,128]{2,1,0:T(8,128)S(1)} %get-tuple-element.113), custom_call_target="InvertDiagBlocksLowerTriangular" | custom-call | tf_op jit(solution)/shard_map/jit(cholesky)/cholesky | solution.py:328
  402.3 11.9 %cholesky.343 = f32[128,128]{1,0:T(8,128)S(1)} custom-call(f32[128,128]{1,0:T(8,128)S(1)} %convolution_subtract_fusion.13), custom_call_target="Cholesky" | custom-call | tf_op jit(solution)/shard_map/jit(cholesky)/cholesky | solution.py:328
  419.6 8.0 while.4
  427.6 39.3 %custom-call.30 = f32[4,128,128]{1,2,0:T(8,128)S(1)} custom-call(f32[4,128,128]{2,1,0:T(8,128)S(1)} %get-tuple-element.18), custom_call_target="InvertDiagBlocksLowerTriangular" | custom-call | tf_op jit(solution)/shard_map/triangular_solve/custom-call.3 | solution.py:329
  472.8 6.8 collective-permute-start.16
  515.5 12.9 %shard_map.73 = f32[16,256,256]{2,1,0:T(8,128)} custom-call(s32[64]{0:T(128)} %get-tuple-element.127.rows_ref, s32[64]{0:T(128)} %get-tuple-element.126.cols_ref, s32[1]{0:T(128)S(6)} %copy.87.used_ref, bf16[64,256,256]{2,1,0:T(8,128)(2,1)} %tile_ref.3, bf16[16,256,256]{2,1,0:T(8,128)(2,1)} %bitcast.174), custom_call_target="tpu_custom_call" | custom-call | flops 4294967296 | bytes 14680064 | tf_op jit(solution)/shard_map/pallas_call | solution.py:236
  538.5 39.7 %collective-permute-done.31 = f32[512,256]{1,0:T(8,128)S(1)} collective-permute-done((f32[512,256]{1,0:T(8,128)S(1)}, f32[512,256]{1,0:T(8,128)S(1)}, u32[]{:S(2)}, u32[]{:S(2)}) %collective-permute-start.31) | collective-permute-done | bytes 524320 | tf_op jit(solution)/shard_map/ppermute | solution.py:20
  580.1 32.5 %collective-permute-done.30 = f32[512,256]{1,0:T(8,128)S(1)} collective-permute-done((f32[512,256]{1,0:T(8,128)S(1)}, f32[512,256]{1,0:T(8,128)S(1)}, u32[]{:S(2)}, u32[]{:S(2)}) %collective-permute-start.30) | collective-permute-done | bytes 524320 | tf_op jit(solution)/shard_map/ppermute | solution.py:20
  614.5 15.5 %collective-permute-start.24 = (f32[512,256]{1,0:T(8,128)S(1)}, f32[512,256]{1,0:T(8,128)}, u32[]{:S(2)}, u32[]{:S(2)}) collective-permute-start(f32[512,256]{1,0:T(8,128)S(1)} %bitcast.178), channel_id=1, source_target_pairs={{0,2},{2,4},{4,6},{6,8},{8,10},{10,12},{12,14},{14,16},{16,18},{18... | collective-permute-start | bytes 1572872 | tf_op jit(solution)/shard_map/ppermute | solution.py:20
  641.1 80.2 %shard_map.75 = f32[128,8,128]{2,1,0:T(8,128)} custom-call(f32[128,8,128]{2,1,0:T(8,128)} %reshape.151.x_ref), custom_call_target="tpu_custom_call" | custom-call | tf_op jit(solution)/shard_map/pallas_call | solution.py:141
  732.7 51.4 %shard_map.77 = f32[128,16,128]{2,1,0:T(8,128)} custom-call(f32[128,16,128]{2,1,0:T(8,128)} %reshape.153.x_ref), custom_call_target="tpu_custom_call" | custom-call | tf_op jit(solution)/shard_map/pallas_call | solution.py:141
  787.1 11.7 %cholesky.358 = f32[128,128]{1,0:T(8,128)S(1)} custom-call(f32[128,128]{1,0:T(8,128)S(1)} %cholesky.439), custom_call_target="Cholesky" | custom-call | tf_op jit(solution)/shard_map/jit(cholesky)/cholesky | solution.py:328
  799.0 9.8 %custom-call.31 = f32[1,128,128]{1,2,0:T(8,128)S(1)} custom-call(f32[1,128,128]{2,1,0:T(8,128)S(1)} %get-tuple-element.109), custom_call_target="InvertDiagBlocksLowerTriangular" | custom-call | tf_op jit(solution)/shard_map/jit(cholesky)/cholesky | solution.py:328
  811.3 11.7 %cholesky.377 = f32[128,128]{1,0:T(8,128)S(1)} custom-call(f32[128,128]{1,0:T(8,128)S(1)} %cholesky.443), custom_call_target="Cholesky" | custom-call | tf_op jit(solution)/shard_map/jit(cholesky)/cholesky | solution.py:328
  823.1 10.0 %custom-call.32 = f32[1,128,128]{1,2,0:T(8,128)S(1)} custom-call(f32[1,128,128]{2,1,0:T(8,128)S(1)} %get-tuple-element.106), custom_call_target="InvertDiagBlocksLowerTriangular" | custom-call | tf_op jit(solution)/shard_map/jit(cholesky)/cholesky | solution.py:328
  834.6 11.7 %cholesky.398 = f32[128,128]{1,0:T(8,128)S(1)} custom-call(f32[128,128]{1,0:T(8,128)S(1)} %cholesky.448), custom_call_target="Cholesky" | custom-call | tf_op jit(solution)/shard_map/jit(cholesky)/cholesky | solution.py:328
  846.4 9.8 %custom-call.33 = f32[1,128,128]{1,2,0:T(8,128)S(1)} custom-call(f32[1,128,128]{2,1,0:T(8,128)S(1)} %get-tuple-element.103), custom_call_target="InvertDiagBlocksLowerTriangular" | custom-call | tf_op jit(solution)/shard_map/jit(cholesky)/cholesky | solution.py:328
  857.6 11.9 %cholesky.415 = f32[128,128]{1,0:T(8,128)S(1)} custom-call(f32[128,128]{1,0:T(8,128)S(1)} %convolution_subtract_fusion.12), custom_call_target="Cholesky" | custom-call | tf_op jit(solution)/shard_map/jit(cholesky)/cholesky | solution.py:328
  874.9 8.0 while.5
  882.9 39.3 %custom-call.34 = f32[4,128,128]{1,2,0:T(8,128)S(1)} custom-call(f32[4,128,128]{2,1,0:T(8,128)S(1)} %get-tuple-element.19), custom_call_target="InvertDiagBlocksLowerTriangular" | custom-call | tf_op jit(solution)/shard_map/triangular_solve/custom-call.3 | solution.py:329
  (218 shorter events, 210.3 us)
Async XLA Ops:
  1.7 24.9 %collective-permute-start.7 = (bf16[512,256]{1,0:T(8,128)(2,1)S(1)}, bf16[512,256]{1,0:T(8,128)(2,1)S(1)}, u32[]{:S(2)}, u32[]{:S(2)}) collective-permute-start(bf16[512,256]{1,0:T(8,128)(2,1)S(1)} %convert_element_type.6), channel_id=1, source_target_pairs={{0,14},{2,16},{4,18},{6,20},{8,22},{10,24},{12,26},{14,28},{16,30}... | collective-permute-start | bytes 786440 | tf_op jit(solution)/shard_map/ppermute | solution.py:20
  6.9 24.1 %collective-permute-start = (bf16[512,256]{1,0:T(8,128)(2,1)S(1)}, bf16[512,256]{1,0:T(8,128)(2,1)S(1)}, u32[]{:S(2)}, u32[]{:S(2)}) collective-permute-start(bf16[512,256]{1,0:T(8,128)(2,1)S(1)} %convert_element_type.6), channel_id=1, source_target_pairs={{0,12},{2,14},{4,16},{6,18},{8,20},{10,22},{12,24},{14,26},{16,28}... | collective-permute-start | bytes 786440 | tf_op jit(solution)/shard_map/ppermute | solution.py:20
  12.9 23.0 %collective-permute-start.1 = (bf16[512,256]{1,0:T(8,128)(2,1)S(1)}, bf16[512,256]{1,0:T(8,128)(2,1)S(1)}, u32[]{:S(2)}, u32[]{:S(2)}) collective-permute-start(bf16[512,256]{1,0:T(8,128)(2,1)S(1)} %convert_element_type.6), channel_id=1, source_target_pairs={{0,10},{2,12},{4,14},{6,16},{8,18},{10,20},{12,22},{14,24},{16,26}... | collective-permute-start | bytes 786440 | tf_op jit(solution)/shard_map/ppermute | solution.py:20
  17.7 23.8 %collective-permute-start.2 = (bf16[512,256]{1,0:T(8,128)(2,1)S(1)}, bf16[512,256]{1,0:T(8,128)(2,1)S(1)}, u32[]{:S(2)}, u32[]{:S(2)}) collective-permute-start(bf16[512,256]{1,0:T(8,128)(2,1)S(1)} %convert_element_type.6), channel_id=1, source_target_pairs={{0,8},{2,10},{4,12},{6,14},{8,16},{10,18},{12,20},{14,22},{16,24},... | collective-permute-start | bytes 786440 | tf_op jit(solution)/shard_map/ppermute | solution.py:20
  20.6 26.6 %collective-permute-start.3 = (bf16[512,256]{1,0:T(8,128)(2,1)S(1)}, bf16[512,256]{1,0:T(8,128)(2,1)S(1)}, u32[]{:S(2)}, u32[]{:S(2)}) collective-permute-start(bf16[512,256]{1,0:T(8,128)(2,1)S(1)} %convert_element_type.6), channel_id=1, source_target_pairs={{0,6},{2,8},{4,10},{6,12},{8,14},{10,16},{12,18},{14,20},{16,22},{... | collective-permute-start | bytes 786440 | tf_op jit(solution)/shard_map/ppermute | solution.py:20
  26.6 25.3 %collective-permute-start.4 = (bf16[512,256]{1,0:T(8,128)(2,1)S(1)}, bf16[512,256]{1,0:T(8,128)(2,1)S(1)}, u32[]{:S(2)}, u32[]{:S(2)}) collective-permute-start(bf16[512,256]{1,0:T(8,128)(2,1)S(1)} %convert_element_type.6), channel_id=1, source_target_pairs={{0,4},{2,6},{4,8},{6,10},{8,12},{10,14},{12,16},{14,18},{16,20},{1... | collective-permute-start | bytes 786440 | tf_op jit(solution)/shard_map/ppermute | solution.py:20
  31.0 20.9 %collective-permute-start.5 = (bf16[512,256]{1,0:T(8,128)(2,1)S(1)}, bf16[512,256]{1,0:T(8,128)(2,1)S(1)}, u32[]{:S(2)}, u32[]{:S(2)}) collective-permute-start(bf16[512,256]{1,0:T(8,128)(2,1)S(1)} %convert_element_type.6), channel_id=1, source_target_pairs={{0,2},{2,4},{4,6},{6,8},{8,10},{10,12},{12,14},{14,16},{16,18},{18... | collective-permute-start | bytes 786440 | tf_op jit(solution)/shard_map/ppermute | solution.py:20
  35.9 16.1 %collective-permute-start.6 = (bf16[512,256]{1,0:T(8,128)(2,1)S(1)}, bf16[512,256]{1,0:T(8,128)(2,1)S(1)}, u32[]{:S(2)}, u32[]{:S(2)}) collective-permute-start(bf16[512,256]{1,0:T(8,128)(2,1)S(1)} %convert_element_type.6), channel_id=1, source_target_pairs={{2,0},{4,2},{6,4},{8,6},{10,8},{12,10},{14,12},{16,14},{18,16},{20... | collective-permute-start | bytes 786440 | tf_op jit(solution)/shard_map/ppermute | solution.py:20
  70.1 32.8 %collective-permute-start.15 = (f32[512,256]{1,0:T(8,128)S(1)}, f32[512,256]{1,0:T(8,128)S(1)}, u32[]{:S(2)}, u32[]{:S(2)}) collective-permute-start(f32[512,256]{1,0:T(8,128)S(1)} %bitcast.185), channel_id=1, source_target_pairs={{14,0},{16,2},{18,4},{20,6},{22,8},{24,10},{26,12},{28,14},{30,16}... | collective-permute-start | bytes 1572872 | tf_op jit(solution)/shard_map/ppermute | solution.py:20
  71.4 83.6 %collective-permute-start.14 = (f32[512,256]{1,0:T(8,128)S(1)}, f32[512,256]{1,0:T(8,128)S(1)}, u32[]{:S(2)}, u32[]{:S(2)}) collective-permute-start(f32[512,256]{1,0:T(8,128)S(1)} %bitcast.183), channel_id=1, source_target_pairs={{12,0},{14,2},{16,4},{18,6},{20,8},{22,10},{24,12},{26,14},{28,16}... | collective-permute-start | bytes 1572872 | tf_op jit(solution)/shard_map/ppermute | solution.py:20
  72.7 84.2 %collective-permute-start.13 = (f32[512,256]{1,0:T(8,128)S(1)}, f32[512,256]{1,0:T(8,128)S(1)}, u32[]{:S(2)}, u32[]{:S(2)}) collective-permute-start(f32[512,256]{1,0:T(8,128)S(1)} %bitcast.181), channel_id=1, source_target_pairs={{10,0},{12,2},{14,4},{16,6},{18,8},{20,10},{22,12},{24,14},{26,16}... | collective-permute-start | bytes 1572872 | tf_op jit(solution)/shard_map/ppermute | solution.py:20
  74.0 110.2 %collective-permute-start.12 = (f32[512,256]{1,0:T(8,128)}, f32[512,256]{1,0:T(8,128)}, u32[]{:S(2)}, u32[]{:S(2)}) collective-permute-start(f32[512,256]{1,0:T(8,128)} %bitcast.6), channel_id=1, source_target_pairs={{8,0},{10,2},{12,4},{14,6},{16,8},{18,10},{20,12},{22,14},{24,16},... | collective-permute-start | bytes 1572872 | tf_op jit(solution)/shard_map/ppermute | solution.py:20
  75.3 108.9 %collective-permute-start.11 = (f32[512,256]{1,0:T(8,128)}, f32[512,256]{1,0:T(8,128)}, u32[]{:S(2)}, u32[]{:S(2)}) collective-permute-start(f32[512,256]{1,0:T(8,128)} %bitcast.5), channel_id=1, source_target_pairs={{6,0},{8,2},{10,4},{12,6},{14,8},{16,10},{18,12},{20,14},{22,16},{... | collective-permute-start | bytes 1572872 | tf_op jit(solution)/shard_map/ppermute | solution.py:20
  102.9 81.3 %collective-permute-start.10 = (f32[512,256]{1,0:T(8,128)}, f32[512,256]{1,0:T(8,128)}, u32[]{:S(2)}, u32[]{:S(2)}) collective-permute-start(f32[512,256]{1,0:T(8,128)} %bitcast.4), channel_id=1, source_target_pairs={{4,0},{6,2},{8,4},{10,6},{12,8},{14,10},{16,12},{18,14},{20,16},{2... | collective-permute-start | bytes 1572872 | tf_op jit(solution)/shard_map/ppermute | solution.py:20
  155.0 29.2 %collective-permute-start.9 = (f32[512,256]{1,0:T(8,128)S(1)}, f32[512,256]{1,0:T(8,128)}, u32[]{:S(2)}, u32[]{:S(2)}) collective-permute-start(f32[512,256]{1,0:T(8,128)S(1)} %bitcast.177), channel_id=1, source_target_pairs={{2,0},{4,2},{6,4},{8,6},{10,8},{12,10},{14,12},{16,14},{18,16},{20... | collective-permute-start | bytes 1572872 | tf_op jit(solution)/shard_map/ppermute | solution.py:20
  157.8 32.1 %collective-permute-start.8 = (f32[512,256]{1,0:T(8,128)S(1)}, f32[512,256]{1,0:T(8,128)}, u32[]{:S(2)}, u32[]{:S(2)}) collective-permute-start(f32[512,256]{1,0:T(8,128)S(1)} %bitcast.176), channel_id=1, source_target_pairs={{0,2},{2,4},{4,6},{6,8},{8,10},{10,12},{12,14},{14,16},{16,18},{18... | collective-permute-start | bytes 1572872 | tf_op jit(solution)/shard_map/ppermute | solution.py:20
  471.5 17.5 %collective-permute-start.23 = (bf16[512,256]{1,0:T(8,128)(2,1)S(1)}, bf16[512,256]{1,0:T(8,128)(2,1)S(1)}, u32[]{:S(2)}, u32[]{:S(2)}) collective-permute-start(bf16[512,256]{1,0:T(8,128)(2,1)S(1)} %get-tuple-element.40), channel_id=1, source_target_pairs={{0,14},{2,16},{4,18},{6,20},{8,22},{10,24},{12,26},{14,28},{16,30}... | collective-permute-start | bytes 786440 | tf_op jit(solution)/shard_map/ppermute | solution.py:20
  472.8 20.9 %collective-permute-start.16 = (bf16[512,256]{1,0:T(8,128)(2,1)S(1)}, bf16[512,256]{1,0:T(8,128)(2,1)S(1)}, u32[]{:S(2)}, u32[]{:S(2)}) collective-permute-start(bf16[512,256]{1,0:T(8,128)(2,1)S(1)} %get-tuple-element.40), channel_id=1, source_target_pairs={{0,12},{2,14},{4,16},{6,18},{8,20},{10,22},{12,24},{14,26},{16,28}... | collective-permute-start | bytes 786440 | tf_op jit(solution)/shard_map/ppermute | solution.py:20
  479.6 19.9 %collective-permute-start.17 = (bf16[512,256]{1,0:T(8,128)(2,1)S(1)}, bf16[512,256]{1,0:T(8,128)(2,1)S(1)}, u32[]{:S(2)}, u32[]{:S(2)}) collective-permute-start(bf16[512,256]{1,0:T(8,128)(2,1)S(1)} %get-tuple-element.40), channel_id=1, source_target_pairs={{0,10},{2,12},{4,14},{6,16},{8,18},{10,20},{12,22},{14,24},{16,26}... | collective-permute-start | bytes 786440 | tf_op jit(solution)/shard_map/ppermute | solution.py:20
  482.6 22.5 %collective-permute-start.18 = (bf16[512,256]{1,0:T(8,128)(2,1)S(1)}, bf16[512,256]{1,0:T(8,128)(2,1)S(1)}, u32[]{:S(2)}, u32[]{:S(2)}) collective-permute-start(bf16[512,256]{1,0:T(8,128)(2,1)S(1)} %get-tuple-element.40), channel_id=1, source_target_pairs={{0,8},{2,10},{4,12},{6,14},{8,16},{10,18},{12,20},{14,22},{16,24},... | collective-permute-start | bytes 786440 | tf_op jit(solution)/shard_map/ppermute | solution.py:20
  485.3 24.4 %collective-permute-start.19 = (bf16[512,256]{1,0:T(8,128)(2,1)S(1)}, bf16[512,256]{1,0:T(8,128)(2,1)S(1)}, u32[]{:S(2)}, u32[]{:S(2)}) collective-permute-start(bf16[512,256]{1,0:T(8,128)(2,1)S(1)} %get-tuple-element.40), channel_id=1, source_target_pairs={{0,6},{2,8},{4,10},{6,12},{8,14},{10,16},{12,18},{14,20},{16,22},{... | collective-permute-start | bytes 786440 | tf_op jit(solution)/shard_map/ppermute | solution.py:20
  489.0 23.5 %collective-permute-start.20 = (bf16[512,256]{1,0:T(8,128)(2,1)S(1)}, bf16[512,256]{1,0:T(8,128)(2,1)S(1)}, u32[]{:S(2)}, u32[]{:S(2)}) collective-permute-start(bf16[512,256]{1,0:T(8,128)(2,1)S(1)} %get-tuple-element.40), channel_id=1, source_target_pairs={{0,4},{2,6},{4,8},{6,10},{8,12},{10,14},{12,16},{14,18},{16,20},{1... | collective-permute-start | bytes 786440 | tf_op jit(solution)/shard_map/ppermute | solution.py:20
  493.8 18.8 %collective-permute-start.21 = (bf16[512,256]{1,0:T(8,128)(2,1)S(1)}, bf16[512,256]{1,0:T(8,128)(2,1)S(1)}, u32[]{:S(2)}, u32[]{:S(2)}) collective-permute-start(bf16[512,256]{1,0:T(8,128)(2,1)S(1)} %get-tuple-element.40), channel_id=1, source_target_pairs={{0,2},{2,4},{4,6},{6,8},{8,10},{10,12},{12,14},{14,16},{16,18},{18... | collective-permute-start | bytes 786440 | tf_op jit(solution)/shard_map/ppermute | solution.py:20
  499.5 14.3 %collective-permute-start.22 = (bf16[512,256]{1,0:T(8,128)(2,1)S(1)}, bf16[512,256]{1,0:T(8,128)(2,1)S(1)}, u32[]{:S(2)}, u32[]{:S(2)}) collective-permute-start(bf16[512,256]{1,0:T(8,128)(2,1)S(1)} %get-tuple-element.40), channel_id=1, source_target_pairs={{2,0},{4,2},{6,4},{8,6},{10,8},{12,10},{14,12},{16,14},{18,16},{20... | collective-permute-start | bytes 786440 | tf_op jit(solution)/shard_map/ppermute | solution.py:20
  532.0 46.2 %collective-permute-start.31 = (f32[512,256]{1,0:T(8,128)S(1)}, f32[512,256]{1,0:T(8,128)S(1)}, u32[]{:S(2)}, u32[]{:S(2)}) collective-permute-start(f32[512,256]{1,0:T(8,128)S(1)} %bitcast.184), channel_id=1, source_target_pairs={{14,0},{16,2},{18,4},{20,6},{22,8},{24,10},{26,12},{28,14},{30,16}... | collective-permute-start | bytes 1572872 | tf_op jit(solution)/shard_map/ppermute | solution.py:20
  533.3 79.3 %collective-permute-start.30 = (f32[512,256]{1,0:T(8,128)S(1)}, f32[512,256]{1,0:T(8,128)S(1)}, u32[]{:S(2)}, u32[]{:S(2)}) collective-permute-start(f32[512,256]{1,0:T(8,128)S(1)} %bitcast.182), channel_id=1, source_target_pairs={{12,0},{14,2},{16,4},{18,6},{20,8},{22,10},{24,12},{26,14},{28,16}... | collective-permute-start | bytes 1572872 | tf_op jit(solution)/shard_map/ppermute | solution.py:20
  534.6 79.9 %collective-permute-start.29 = (f32[512,256]{1,0:T(8,128)S(1)}, f32[512,256]{1,0:T(8,128)S(1)}, u32[]{:S(2)}, u32[]{:S(2)}) collective-permute-start(f32[512,256]{1,0:T(8,128)S(1)} %bitcast.180), channel_id=1, source_target_pairs={{10,0},{12,2},{14,4},{16,6},{18,8},{20,10},{22,12},{24,14},{26,16}... | collective-permute-start | bytes 1572872 | tf_op jit(solution)/shard_map/ppermute | solution.py:20
  535.9 99.7 %collective-permute-start.28 = (f32[512,256]{1,0:T(8,128)}, f32[512,256]{1,0:T(8,128)}, u32[]{:S(2)}, u32[]{:S(2)}) collective-permute-start(f32[512,256]{1,0:T(8,128)} %bitcast.32), channel_id=1, source_target_pairs={{8,0},{10,2},{12,4},{14,6},{16,8},{18,10},{20,12},{22,14},{24,16},... | collective-permute-start | bytes 1572872 | tf_op jit(solution)/shard_map/ppermute | solution.py:20
  537.2 98.5 %collective-permute-start.27 = (f32[512,256]{1,0:T(8,128)}, f32[512,256]{1,0:T(8,128)}, u32[]{:S(2)}, u32[]{:S(2)}) collective-permute-start(f32[512,256]{1,0:T(8,128)} %bitcast.31), channel_id=1, source_target_pairs={{6,0},{8,2},{10,4},{12,6},{14,8},{16,10},{18,12},{20,14},{22,16},{... | collective-permute-start | bytes 1572872 | tf_op jit(solution)/shard_map/ppermute | solution.py:20
  578.2 57.4 %collective-permute-start.26 = (f32[512,256]{1,0:T(8,128)}, f32[512,256]{1,0:T(8,128)}, u32[]{:S(2)}, u32[]{:S(2)}) collective-permute-start(f32[512,256]{1,0:T(8,128)} %bitcast.30), channel_id=1, source_target_pairs={{4,0},{6,2},{8,4},{10,6},{12,8},{14,10},{16,12},{18,14},{20,16},{2... | collective-permute-start | bytes 1572872 | tf_op jit(solution)/shard_map/ppermute | solution.py:20
  612.6 23.1 %collective-permute-start.25 = (f32[512,256]{1,0:T(8,128)S(1)}, f32[512,256]{1,0:T(8,128)}, u32[]{:S(2)}, u32[]{:S(2)}) collective-permute-start(f32[512,256]{1,0:T(8,128)S(1)} %bitcast.179), channel_id=1, source_target_pairs={{2,0},{4,2},{6,4},{8,6},{10,8},{12,10},{14,12},{16,14},{18,16},{20... | collective-permute-start | bytes 1572872 | tf_op jit(solution)/shard_map/ppermute | solution.py:20
  614.5 21.8 %collective-permute-start.24 = (f32[512,256]{1,0:T(8,128)S(1)}, f32[512,256]{1,0:T(8,128)}, u32[]{:S(2)}, u32[]{:S(2)}) collective-permute-start(f32[512,256]{1,0:T(8,128)S(1)} %bitcast.178), channel_id=1, source_target_pairs={{0,2},{2,4},{4,6},{6,8},{8,10},{10,12},{12,14},{14,16},{16,18},{18... | collective-permute-start | bytes 1572872 | tf_op jit(solution)/shard_map/ppermute | solution.py:20
  (13 other events, 228.9 us)
